TPU v7x, 512 devices: a whole 4x4x16 slice. The times are simulated.
512 devices in a mesh: gy: 64 (over z, y_hi, core), ch: 8 (over y_lo, x).
Axes of the slice: x: 4, y: 4 (y_hi: 2, y_lo: 2; y = y_hi * 2 + y_lo), z: 16, core: 2. Of those that a mesh axis runs over, the one named last changes fastest.
Arguments:
- volume: bfloat16 [256, 512, 4, 128], P('ch', 'gy'), may hold values from -6 to 6
- first_weight: bfloat16 [3, 3, 3, 256, 256], P(None, None, None, 'ch'), may hold values from -0.078125 to 0.078125
- first_bias: float32 [256], P('ch'), may hold values from -3 to 3
- second_weight: bfloat16 [3, 3, 3, 256, 256], P(None, None, None, 'ch'), may hold values from -0.078125 to 0.078125
- second_bias: float32 [256], P('ch'), may hold values from -3 to 3
Outputs:
- block_out: bfloat16 [256, 512, 4, 128], P('ch', 'gy')
All inputs are finite; a program needn't handle non-finite values.
Results may differ from a plain program's by a relative error of at most 0.003.
Values may be sent and summed in bfloat16 or wider, within the bound.
No kernel may reach another device: no remote copies, remote signals or barrier semaphores. Data moves between devices by JAX's collectives and lax.ppermute only.
A program may use at most 64 MiB of HBM per device.

v0:
```python
import jax
import jax.numpy as jnp
from jax import lax
from jax.sharding import PartitionSpec as P


def with_halo(shard, sides, width):
    for axis, dim in sides:
        size, length = (lax.axis_size(axis), shard.shape[dim])
        up = [(i, (i + 1) % size) for i in range(size - 1)]
        down = [(j, i) for i, j in up]
        last = lax.slice_in_dim(shard, length - width, length, axis=dim)
        initial = lax.slice_in_dim(shard, 0, width, axis=dim)
        before = lax.ppermute(last, axis, up)
        after = lax.ppermute(initial, axis, down)
        shard = jnp.concatenate([before, shard, after], axis=dim)
    return shard


def apply_kernel(section, kernel):
    result = lax.conv_general_dilated(
        section[None],
        kernel,
        (1, 1, 1),
        ((0, 0), (1, 1), (1, 1)),
        dimension_numbers=("NCDHW", "OIDHW", "NCDHW"),
        preferred_element_type=jnp.float32,
    )
    return result[0]


def convolve(active, filters):
    kernel = jnp.transpose(filters, (3, 4, 0, 1, 2))
    gathered = lax.all_gather(active, "ch", axis=0, tiled=True)
    framed = with_halo(gathered, (("gy", 1),), 1)
    return apply_kernel(framed, kernel)


def per_device(volume, first_weight, first_bias, second_weight, second_bias):
    before = convolve(volume, first_weight) + first_bias[:, None, None, None]
    hidden = jax.nn.gelu(before, approximate=False).astype(jnp.bfloat16)
    after = convolve(hidden, second_weight) + second_bias[:, None, None, None]
    return (volume.astype(jnp.float32) + after).astype(jnp.bfloat16)


def solution(mesh):
    in_specs = (
        P("ch", "gy", None, None),
        P(None, None, None, "ch", None),
        P("ch"),
        P(None, None, None, "ch", None),
        P("ch"),
    )
    out_specs = P("ch", "gy", None, None)
    return jax.shard_map(
        per_device, mesh=mesh, in_specs=in_specs, out_specs=out_specs, check_vma=False
    )
```

profile of v0, /device:TPU:129, one launch (start us, length us, event | category | flops | bytes accessed | tf_op | source)
XLA Modules:
  0.0 230.0 jit_solution(3810804304901273524)
XLA Ops:
  6.5 1.7 copy.28
  8.4 48.1 %all-gather.3.cloned.1.call-done = bf16[256,8,4,128]{3,1,2,0:T(8,128)(2,1)} async-done(((bf16[32,8,4,128]{3,1,2,0:T(8,128)(2,1)}), bf16[256,8,4,128]{3,1,2,0:T(8,128)(2,1)}) %all-gather.3.cloned.1.call-update) | async-done | bytes 2097168 | tf_op jit(solution)/shard_map/all_gather | solution.py:34
  56.4 3.2 %fusion.43 = (bf16[256,1,4,128]{3,1,2,0:T(2,128)(2,1)S(1)}, bf16[256,1,4,128]{3,1,2,0:T(2,128)(2,1)S(1)}) fusion(bf16[256,8,4,128]{3,1,2,0:T(8,128)(2,1)} %all-gather.3.cloned.1.call-done), kind=kLoop, calls=%fused_computation.51 | loop fusion | bytes 1048576 | tf_op jit(solution)/shard_map/slice | solution.py:12
  59.6 10.0 %collective-permute-start = (bf16[256,1,4,128]{3,1,2,0:T(2,128)(2,1)S(1)}, bf16[256,1,4,128]{3,1,2,0:T(2,128)(2,1)S(1)}, u32[]{:S(2)}, u32[]{:S(2)}) collective-permute-start(bf16[256,1,4,128]{3,1,2,0:T(2,128)(2,1)S(1)} %get-tuple-element.7), channel_id=1, source_target_pairs={{0,8},{8,16},{16,24},{24,32},{32,40},{40,48},{48,56},{56,64},{64,7... | collective-permute-start | bytes 786440 | tf_op jit(solution)/shard_map/ppermute | solution.py:14
  69.6 1.9 collective-permute-start.1
  71.5 9.8 %collective-permute-done = bf16[256,1,4,128]{3,1,2,0:T(2,128)(2,1)S(1)} collective-permute-done((bf16[256,1,4,128]{3,1,2,0:T(2,128)(2,1)S(1)}, bf16[256,1,4,128]{3,1,2,0:T(2,128)(2,1)S(1)}, u32[]{:S(2)}, u32[]{:S(2)}) %collective-permute-start) | collective-permute-done | bytes 262176 | tf_op jit(solution)/shard_map/ppermute | solution.py:14
  81.3 3.1 %collective-permute-done.1 = bf16[256,1,4,128]{3,1,2,0:T(2,128)(2,1)S(1)} collective-permute-done((bf16[256,1,4,128]{3,1,2,0:T(2,128)(2,1)S(1)}, bf16[256,1,4,128]{3,1,2,0:T(2,128)(2,1)S(1)}, u32[]{:S(2)}, u32[]{:S(2)}) %collective-permute-start.1) | collective-permute-done | bytes 262176 | tf_op jit(solution)/shard_map/ppermute | solution.py:15
  84.4 4.2 %maximum_bitcast_fusion = bf16[256,10,4,1,128]{4,1,2,0,3:T(8,128)(2,1)} fusion(bf16[256,1,4,128]{3,1,2,0:T(2,128)(2,1)S(1)} %collective-permute-done.1, bf16[256,8,4,128]{3,1,2,0:T(8,128)(2,1)S(1)} %copy-done.1, bf16[256,1,4,128]{3,1,2,0:T(2,128)(2,1)S(1)} %collective-permute-done), kind=kLoop, calls=%fused_computation.3 | loop fusion | flops 7864320 | bytes 5242880 | tf_op jit(solution)/shard_map/broadcast_in_dim | solution.py:22
  88.5 8.0 %copy.43 = bf16[256,10,4,1,128]{0,2,4,1,3:T(4,128)(2,1)S(1)} copy(bf16[256,10,4,1,128]{4,1,2,0,3:T(8,128)(2,1)} %maximum_bitcast_fusion) | data formatting | bytes 5242880
  96.5 1.2 pad.clone
  97.7 0.4 copy.32
  98.2 0.2 copy-done.7
  98.4 16.7 %fusion.21 = f32[8,4,8,17,32]{4,2,3,1,0:T(8,128)S(1)} fusion(bf16[3,3,3,32,256]{4,3,2,1,0:T(8,128)(2,1)S(1)} %copy-done, bf16[256,10,4,1,7,2]{0,4,5,2,1,3:T(8,128)(2,1)S(1)} %slice.22, bf16[256,10,4,1,8,17]{0,4,5,2,1,3:T(8,128)(2,1)S(1)} %copy.32, pred[8,17]{0,1:T(8,128)(4,1)S(1)} %copy-done.7), kind=kOutput, calls=%fused_computation.20 | convolution fusion | flops 1613799424 | bytes 4071560 | tf_op jit(solution)/shard_map/conv_general_dilated | solution.py:21
  115.0 1.3 copy.33
  116.3 0.1 slice.23
  116.5 0.8 copy.41
  117.4 1.9 fusion.26
  119.3 41.6 %all-gather.5.cloned.1.call-done = bf16[256,8,4,128]{3,1,2,0:T(8,128)(2,1)} async-done(((bf16[32,8,4,128]{3,1,2,0:T(8,128)(2,1)}), bf16[256,8,4,128]{3,1,2,0:T(8,128)(2,1)}) %all-gather.5.cloned.1.call-update) | async-done | bytes 2097168 | tf_op jit(solution)/shard_map/all_gather | solution.py:34
  160.9 3.2 %fusion.42 = (bf16[256,1,4,128]{3,1,2,0:T(2,128)(2,1)S(1)}, bf16[256,1,4,128]{3,1,2,0:T(2,128)(2,1)S(1)}) fusion(bf16[256,8,4,128]{3,1,2,0:T(8,128)(2,1)} %all-gather.5.cloned.1.call-done), kind=kLoop, calls=%fused_computation.50 | loop fusion | bytes 1048576 | tf_op jit(solution)/shard_map/slice | solution.py:12
  164.1 10.0 %collective-permute-start.2 = (bf16[256,1,4,128]{3,1,2,0:T(2,128)(2,1)S(1)}, bf16[256,1,4,128]{3,1,2,0:T(2,128)(2,1)S(1)}, u32[]{:S(2)}, u32[]{:S(2)}) collective-permute-start(bf16[256,1,4,128]{3,1,2,0:T(2,128)(2,1)S(1)} %get-tuple-element.5), channel_id=1, source_target_pairs={{0,8},{8,16},{16,24},{24,32},{32,40},{40,48},{48,56},{56,64},{64,7... | collective-permute-start | bytes 786440 | tf_op jit(solution)/shard_map/ppermute | solution.py:14
  174.0 1.9 collective-permute-start.3
  176.0 9.8 %collective-permute-done.2 = bf16[256,1,4,128]{3,1,2,0:T(2,128)(2,1)S(1)} collective-permute-done((bf16[256,1,4,128]{3,1,2,0:T(2,128)(2,1)S(1)}, bf16[256,1,4,128]{3,1,2,0:T(2,128)(2,1)S(1)}, u32[]{:S(2)}, u32[]{:S(2)}) %collective-permute-start.2) | collective-permute-done | bytes 262176 | tf_op jit(solution)/shard_map/ppermute | solution.py:14
  185.8 3.1 %collective-permute-done.3 = bf16[256,1,4,128]{3,1,2,0:T(2,128)(2,1)S(1)} collective-permute-done((bf16[256,1,4,128]{3,1,2,0:T(2,128)(2,1)S(1)}, bf16[256,1,4,128]{3,1,2,0:T(2,128)(2,1)S(1)}, u32[]{:S(2)}, u32[]{:S(2)}) %collective-permute-start.3) | collective-permute-done | bytes 262176 | tf_op jit(solution)/shard_map/ppermute | solution.py:15
  188.8 4.2 %maximum_bitcast_fusion.1 = bf16[256,10,4,1,128]{4,1,2,0,3:T(8,128)(2,1)} fusion(bf16[256,1,4,128]{3,1,2,0:T(2,128)(2,1)S(1)} %collective-permute-done.3, bf16[256,8,4,128]{3,1,2,0:T(8,128)(2,1)S(1)} %copy-done.2, bf16[256,1,4,128]{3,1,2,0:T(2,128)(2,1)S(1)} %collective-permute-done.2), kind=kLoop, calls=%fused_computation.4 | loop fusion | flops 7864320 | bytes 5242880 | tf_op jit(solution)/shard_map/broadcast_in_dim | solution.py:22
  193.0 7.9 %copy.44 = bf16[256,10,4,1,128]{0,2,4,1,3:T(4,128)(2,1)S(1)} copy(bf16[256,10,4,1,128]{4,1,2,0,3:T(8,128)(2,1)} %maximum_bitcast_fusion.1) | data formatting | bytes 5242880
  200.9 1.2 pad.2.clone
  202.1 0.4 copy.37
  202.6 0.5 copy-done.6
  203.1 16.5 %fusion.18 = f32[8,4,8,17,32]{4,2,3,1,0:T(8,128)S(1)} fusion(bf16[3,3,3,32,256]{4,3,2,1,0:T(8,128)(2,1)S(1)} %copy-done.6, bf16[256,10,4,1,7,2]{0,4,5,2,1,3:T(8,128)(2,1)S(1)} %slice.26, bf16[256,10,4,1,8,17]{0,4,5,2,1,3:T(8,128)(2,1)S(1)} %copy.37, pred[8,17]{0,1:T(8,128)(4,1)S(1)} %copy-done.7), kind=kOutput, calls=%fused_computation.19 | convolution fusion | flops 1613799424 | bytes 4071560 | tf_op jit(solution)/shard_map/conv_general_dilated | solution.py:21
  219.6 1.3 copy.38
  221.1 0.8 copy.42
  222.1 0.8 copy.40
  (22 shorter events, 0.5 us)
Async XLA Ops:
  6.5 91.7 %copy-start = (bf16[3,3,3,32,256]{4,3,2,1,0:T(8,128)(2,1)S(1)}, bf16[3,3,3,32,256]{4,3,2,1,0:T(8,128)(2,1)}, u32[]{:S(2)}) copy-start(bf16[3,3,3,32,256]{4,3,2,1,0:T(8,128)(2,1)} %param.6) | copy-start | bytes 1327108
  6.5 49.9 %all-gather.3.cloned.1.call-start = ((), (), s32[]{:S(2)}) async-start(), calls=%async_computation | async-start | bytes 2359296 | tf_op jit(solution)/shard_map/all_gather | solution.py:34
  8.3 152.6 %all-gather.5.cloned.1.call-start = ((), (), s32[]{:S(2)}) async-start(), calls=%async_computation.1 | async-start | bytes 2359296 | tf_op jit(solution)/shard_map/all_gather | solution.py:34
  56.4 28.0 %copy-start.1 = (bf16[256,8,4,128]{3,1,2,0:T(8,128)(2,1)S(1)}, bf16[256,8,4,128]{3,1,2,0:T(8,128)(2,1)}, u32[]{:S(2)}) copy-start(bf16[256,8,4,128]{3,1,2,0:T(8,128)(2,1)} %all-gather.3.cloned.1.call-done) | copy-start | bytes 6291460
  59.6 21.7 %collective-permute-start = (bf16[256,1,4,128]{3,1,2,0:T(2,128)(2,1)S(1)}, bf16[256,1,4,128]{3,1,2,0:T(2,128)(2,1)S(1)}, u32[]{:S(2)}, u32[]{:S(2)}) collective-permute-start(bf16[256,1,4,128]{3,1,2,0:T(2,128)(2,1)S(1)} %get-tuple-element.7), channel_id=1, source_target_pairs={{0,8},{8,16},{16,24},{24,32},{32,40},{40,48},{48,56},{56,64},{64,7... | collective-permute-start | bytes 786440 | tf_op jit(solution)/shard_map/ppermute | solution.py:14
  69.6 14.8 %collective-permute-start.1 = (bf16[256,1,4,128]{3,1,2,0:T(2,128)(2,1)S(1)}, bf16[256,1,4,128]{3,1,2,0:T(2,128)(2,1)S(1)}, u32[]{:S(2)}, u32[]{:S(2)}) collective-permute-start(bf16[256,1,4,128]{3,1,2,0:T(2,128)(2,1)S(1)} %get-tuple-element.8), channel_id=1, source_target_pairs={{8,0},{16,8},{24,16},{32,24},{40,32},{48,40},{56,48},{64,56},{72,6... | collective-permute-start | bytes 786440 | tf_op jit(solution)/shard_map/ppermute | solution.py:15
  97.7 0.7 copy-start.7
  116.3 1.0 copy-start.5
  160.9 28.0 %copy-start.2 = (bf16[256,8,4,128]{3,1,2,0:T(8,128)(2,1)S(1)}, bf16[256,8,4,128]{3,1,2,0:T(8,128)(2,1)}, u32[]{:S(2)}) copy-start(bf16[256,8,4,128]{3,1,2,0:T(8,128)(2,1)} %all-gather.5.cloned.1.call-done) | copy-start | bytes 6291460
  164.1 21.7 %collective-permute-start.2 = (bf16[256,1,4,128]{3,1,2,0:T(2,128)(2,1)S(1)}, bf16[256,1,4,128]{3,1,2,0:T(2,128)(2,1)S(1)}, u32[]{:S(2)}, u32[]{:S(2)}) collective-permute-start(bf16[256,1,4,128]{3,1,2,0:T(2,128)(2,1)S(1)} %get-tuple-element.5), channel_id=1, source_target_pairs={{0,8},{8,16},{16,24},{24,32},{32,40},{40,48},{48,56},{56,64},{64,7... | collective-permute-start | bytes 786440 | tf_op jit(solution)/shard_map/ppermute | solution.py:14
  174.0 14.8 %collective-permute-start.3 = (bf16[256,1,4,128]{3,1,2,0:T(2,128)(2,1)S(1)}, bf16[256,1,4,128]{3,1,2,0:T(2,128)(2,1)S(1)}, u32[]{:S(2)}, u32[]{:S(2)}) collective-permute-start(bf16[256,1,4,128]{3,1,2,0:T(2,128)(2,1)S(1)} %get-tuple-element.6), channel_id=1, source_target_pairs={{8,0},{16,8},{24,16},{32,24},{40,32},{48,40},{56,48},{64,56},{72,6... | collective-permute-start | bytes 786440 | tf_op jit(solution)/shard_map/ppermute | solution.py:15
  202.1 1.0 copy-start.6
  220.9 1.0 copy-start.3
  220.9 1.0 copy-start.4
Sparse Core Ops, SparseCore 0:
  9.4 46.9 all-gather.2
  119.4 41.3 all-gather.4
where the time goes:
time: 234 us; the launch traced here: 230 us
  waiting for transfers between devices  115 us (49%)
  local copies, waits for them, and re-layouts  33.3 us (14%)
  matrix products  33.2 us (14%)
  starting transfers between devices  23.8 us (10%)
  between operations  13.9 us (6%)
  other arithmetic  10.4 us (4%)
    all_gather x2, waiting for transfers between devices, convolve(): gathered = lax.all_gather(active, 'ch', axis=0, tiled=True)  89.6 us
    conv_general_dilated x2, matrix products, apply_kernel(): lax.conv_general_dilated(section[None], kernel, (1, 1, 1), ((0, 0), (1, 1...  33.2 us
    unnamed x21, local copies, waits for them, and re-layouts  20 us
    ppermute x2, starting transfers between devices, with_halo(): before = lax.ppermute(last, axis, up)  19.9 us
    ppermute x2, waiting for transfers between devices, with_halo(): before = lax.ppermute(last, axis, up)  19.6 us
    broadcast_in_dim x2, other arithmetic, apply_kernel(): section[None]  8.3 us
    slice x2, local copies, waits for them, and re-layouts, with_halo(): last = lax.slice_in_dim(shard, length - width, length, axis=dim)  6.37 us
    ppermute x2, waiting for transfers between devices, with_halo(): after = lax.ppermute(initial, axis, down)  6.16 us
  transfers between devices with their start and end apart: 6, of which 6 were waited for; matrix products, arithmetic and copies ran while one was open for 0% of the time, Pallas kernels for 0%

commit v1 on v0

v1 whole, which is shorter than its diff:
```python
import jax
import jax.numpy as jnp
import numpy as np
from jax import lax
from jax.experimental import pallas as pl
from jax.experimental.pallas import tpu as pltpu
from jax.sharding import PartitionSpec as P

ROOT_HALF = np.float32(np.sqrt(0.5))
F32, BF16 = jnp.float32, jnp.bfloat16


def column(row_ref, n):
    i = lax.broadcasted_iota(jnp.int32, (n, n), 0)
    j = lax.broadcasted_iota(jnp.int32, (n, n), 1)
    square = jnp.where(i == j, jnp.broadcast_to(row_ref[...], (n, n)), 0.0)
    return jnp.sum(square, axis=1, keepdims=True)


def gelu(v):
    return 0.5 * v * (1.0 + lax.erf(v * ROOT_HALF))


def x_taps(a, co, nx):
    lane = lax.broadcasted_iota(jnp.int32, (co, nx), 1)
    left = jnp.where(lane == 0, 0.0, pltpu.roll(a[:co], 1, 1))
    right = jnp.where(lane == nx - 1, 0.0, pltpu.roll(a[2 * co :], nx - 1, 1))
    return a[co : 2 * co] + left + right


def z_taps(parts, co):
    nz = len(parts)
    sums = [None] * nz
    for zz in range(nz):
        for dz in range(3):
            z = zz - dz + 1
            if 0 <= z < nz:
                e = parts[zz][dz * 3 * co : (dz + 1) * 3 * co]
                sums[z] = e if sums[z] is None else sums[z] + e
    return sums


def rows(w_ref, dy):
    return w_ref[dy].reshape(-1, w_ref.shape[-1])


def cells(planes, p, z):
    n, ny, _, c, nx = planes.shape
    if not 0 <= p < ny:
        return jnp.zeros((n * c, nx), BF16)
    return planes[:, p, z].reshape(n * c, nx)


def edge_kernel(planes, w_ref, below, above):
    _, ny, nz, co, nx = planes.shape
    for out, p, dy in ((below, 0, 2), (above, ny - 1, 0)):
        parts = [
            jnp.dot(rows(w_ref, dy), cells(planes, p, zz), preferred_element_type=F32)
            for zz in range(nz)
        ]
        for z, s in enumerate(z_taps(parts, co)):
            out[z] = x_taps(s, co, nx)


def conv(planes, w_ref, bias, take):
    _, ny, nz, co, nx = planes.shape
    half = ny // 2
    for q in range(half):
        parts = []
        for zz in range(nz):
            part = None
            for dy in range(3):
                p = q + dy - 1
                x = jnp.concatenate([cells(planes, p, zz), cells(planes, p + half, zz)], axis=1)
                d = jnp.dot(rows(w_ref, dy), x, preferred_element_type=F32)
                part = d if part is None else part + d
            parts.append(part)
        sums = z_taps(parts, co)
        for h in range(2):
            take(q + h * half, [x_taps(s[:, h * nx : (h + 1) * nx], co, nx) + bias for s in sums])


def first_kernel(planes, w_ref, b_ref, out, ends, hidden, sems):
    n, ny, nz, co, nx = planes.shape
    bias = jnp.broadcast_to(column(b_ref, co), (co, nx))

    def take(y, values):
        for z, v in enumerate(values):
            if y == 0 or y == ny - 1:
                ends[y // (ny - 1), z] = v
            else:
                hidden[y - 1, z] = gelu(v).astype(BF16)

    conv(planes, w_ref, bias, take)
    copies = [
        pltpu.make_async_copy(hidden, out.at[d, 1 : ny - 1], sems.at[d]) for d in range(n)
    ]
    for c in copies:
        c.start()
    for c in copies:
        c.wait()


def first_ends_kernel(ends, below, above, _, out, hidden, sems):
    n, ny = out.shape[:2]
    copies = []
    for side, other in enumerate((below, above)):
        hidden[side] = gelu(ends[side] + other[...]).astype(BF16)
        for d in range(n):
            c = pltpu.make_async_copy(
                hidden.at[side], out.at[d, side * (ny - 1)], sems.at[side, d]
            )
            c.start()
            copies.append(c)
    for c in copies:
        c.wait()


def channels_first(values):
    return jnp.stack(values, axis=1).astype(BF16)


def second_kernel(planes, w_ref, b_ref, v_ref, out, ends, inner, sem):
    _, ny, nz, co, nx = planes.shape
    bias = jnp.broadcast_to(column(b_ref, co), (co, nx))

    def take(y, values):
        values = [v_ref[y, z].astype(F32) + v for z, v in enumerate(values)]
        if y == 0 or y == ny - 1:
            for z, v in enumerate(values):
                ends[y // (ny - 1), z] = v
        else:
            inner[:, y - 1] = channels_first(values)

    conv(planes, w_ref, bias, take)
    copy = pltpu.make_async_copy(inner, out.at[:, 1 : ny - 1], sem)
    copy.start()
    copy.wait()


def second_ends_kernel(ends, below, above, _, out, outer, sems):
    ny = out.shape[1]
    copies = []
    for side, other in enumerate((below, above)):
        outer[side] = channels_first([ends[side, z] + other[z] for z in range(ends.shape[1])])
        c = pltpu.make_async_copy(outer.at[side], out.at[:, side * (ny - 1)], sems.at[side])
        c.start()
        copies.append(c)
    for c in copies:
        c.wait()


ANY = pl.BlockSpec(memory_space=pl.ANY)
VMEM = pl.BlockSpec(memory_space=pltpu.VMEM)
DMA = pltpu.SemaphoreType.DMA
PARAMS = pltpu.CompilerParams(vmem_limit_bytes=48 << 20)


def per_device(volume, first_weight, first_bias, second_weight, second_bias):
    co, ny, nz, nx = volume.shape
    n, length = lax.axis_size("ch"), lax.axis_size("gy")
    up = [(i, i + 1) for i in range(length - 1)]
    down = [(i + 1, i) for i in range(length - 1)]
    plane = jax.ShapeDtypeStruct((nz, co, nx), F32)
    ends_type = jax.ShapeDtypeStruct((2, nz, co, nx), F32)

    def call(kernel, out_shape, in_specs, out_specs, scratch, **extra):
        return pl.pallas_call(
            kernel,
            out_shape=out_shape,
            in_specs=in_specs,
            out_specs=out_specs,
            scratch_shapes=scratch,
            compiler_params=PARAMS,
            name=kernel.__name__,
            **extra,
        )

    def edges(planes, weight):
        below, above = call(edge_kernel, (plane, plane), [VMEM, VMEM], (VMEM, VMEM), [])(planes, weight)
        return lax.ppermute(above, "gy", up), lax.ppermute(below, "gy", down)

    cells_first = jnp.transpose(volume, (1, 2, 0, 3))
    sent = jnp.broadcast_to(cells_first, (n, ny, nz, co, nx))
    main = lax.all_to_all(sent, "ch", 0, 0, tiled=True)
    lower, upper = edges(main, first_weight)
    all_hidden = jax.ShapeDtypeStruct((n, ny, nz, co, nx), BF16)
    hidden, ends = call(
        first_kernel,
        (all_hidden, ends_type),
        [VMEM, VMEM, VMEM],
        (ANY, VMEM),
        [pltpu.VMEM((ny - 2, nz, co, nx), BF16), DMA((n,))],
    )(main, first_weight, first_bias[None])
    hidden = call(
        first_ends_kernel,
        all_hidden,
        [VMEM, VMEM, VMEM, ANY],
        ANY,
        [pltpu.VMEM((2, nz, co, nx), BF16), DMA((2, n))],
        input_output_aliases={3: 0},
    )(ends, lower, upper, hidden)

    gathered = lax.all_to_all(hidden, "ch", 0, 0, tiled=True)
    lower, upper = edges(gathered, second_weight)
    out_type = jax.ShapeDtypeStruct(volume.shape, BF16)
    out, ends = call(
        second_kernel,
        (out_type, ends_type),
        [VMEM, VMEM, VMEM, VMEM],
        (ANY, VMEM),
        [pltpu.VMEM((co, ny - 2, nz, nx), BF16), DMA],
    )(gathered, second_weight, second_bias[None], cells_first)
    return call(
        second_ends_kernel,
        out_type,
        [VMEM, VMEM, VMEM, ANY],
        ANY,
        [pltpu.VMEM((2, co, nz, nx), BF16), DMA((2,))],
        input_output_aliases={3: 0},
    )(ends, lower, upper, out)


def solution(mesh):
    in_specs = (
        P("ch", "gy", None, None),
        P(None, None, None, "ch", None),
        P("ch"),
        P(None, None, None, "ch", None),
        P("ch"),
    )
    out_specs = P("ch", "gy", None, None)
    return jax.shard_map(
        per_device, mesh=mesh, in_specs=in_specs, out_specs=out_specs, check_vma=False
    )
```

time: 234 us -> 93.1 us (0.40)
  the two profiles are of different devices: /device:TPU:129 before, /device:TPU:241 now
where the time goes in v1:
time: 93.1 us; the launch traced here: 92.8 us
  blocking collectives  58.8 us (63%)
  starting transfers between devices  15.1 us (16%)
  Pallas kernels  9.87 us (11%)
  waiting for transfers between devices  7.36 us (8%)
  local copies, waits for them, and re-layouts  1.57 us (2%)
    all_to_all x1, blocking collectives, per_device(): main = lax.all_to_all(sent, 'ch', 0, 0, tiled=True)  30.8 us
    all_to_all x1, blocking collectives, per_device(): gathered = lax.all_to_all(hidden, 'ch', 0, 0, tiled=True)  28 us
    ppermute x4, starting transfers between devices, edges(): return (lax.ppermute(above, 'gy', up), lax.ppermute(below, 'gy', down))  15.1 us
    ppermute x4, waiting for transfers between devices, edges(): return (lax.ppermute(above, 'gy', up), lax.ppermute(below, 'gy', down))  7.36 us
    pallas_call x1, Pallas kernels, per_device(): call(first_kernel, (all_hidden, ends_type), [VMEM, VMEM, VMEM], (ANY, VME...  4.22 us
    pallas_call x1, Pallas kernels, per_device(): call(second_kernel, (out_type, ends_type), [VMEM, VMEM, VMEM, VMEM], (ANY...  2.91 us
  transfers between devices with their start and end apart: 4, of which 2 were waited for; matrix products, arithmetic and copies ran while one was open for 0% of the time, Pallas kernels for 8%

profile of v1, /device:TPU:241, one launch (start us, length us, event | category | flops | bytes accessed | tf_op | source)
XLA Modules:
  0.0 92.8 jit_solution(1503816470282698429)
XLA Ops:
  0.0 1.1 %copy.10 = bf16[32,8,4,128]{3,0,2,1:T(8,128)(2,1)S(1)} copy(bf16[32,8,4,128]{3,2,1,0:T(4,128)(2,1)} %param.5) | data formatting | bytes 524288 | tf_op args[0]
  1.1 0.5 broadcast_in_dim.9
  1.6 0.0 copy-start
  1.6 30.8 %all_to_all.10.planes = bf16[8,8,4,32,128]{4,3,2,1,0:T(8,128)(2,1)S(1)} all-to-all(bf16[8,8,4,32,128]{4,3,2,1,0:T(8,128)(2,1)S(1)} %broadcast_in_dim.9), channel_id=1, replica_groups=mesh['gy'=64,'ch'=8] {'ch'}, dimensions={0} | all-to-all | bytes 4194304 | tf_op jit(solution)/shard_map/all_to_all | solution.py:185
  32.3 0.0 copy-done
  32.3 0.0 copy-start.3
  32.3 0.6 edge_kernel.2
  32.9 6.5 %collective-permute-start = (f32[4,32,128]{2,1,0:T(8,128)S(1)}, f32[4,32,128]{2,1,0:T(8,128)S(1)}, u32[]{:S(2)}, u32[]{:S(2)}) collective-permute-start(f32[4,32,128]{2,1,0:T(8,128)S(1)} %get-tuple-element.14), channel_id=1, source_target_pairs={{0,8},{8,16},{16,24},{24,32},{32,40},{40,48},{48,56},{56,64},{64,7... | collective-permute-start | bytes 196616 | tf_op jit(solution)/shard_map/ppermute | solution.py:181
  39.4 1.9 %collective-permute-start.1 = (f32[4,32,128]{2,1,0:T(8,128)S(1)}, f32[4,32,128]{2,1,0:T(8,128)S(1)}, u32[]{:S(2)}, u32[]{:S(2)}) collective-permute-start(f32[4,32,128]{2,1,0:T(8,128)S(1)} %get-tuple-element.15), channel_id=1, source_target_pairs={{8,0},{16,8},{24,16},{32,24},{40,32},{48,40},{56,48},{64,56},{72,6... | collective-permute-start | bytes 196616 | tf_op jit(solution)/shard_map/ppermute | solution.py:181
  41.3 0.0 copy-done.3
  41.3 4.2 %first_kernel.1 = (bf16[8,8,4,32,128]{4,3,2,1,0:T(8,128)(2,1)S(1)}, f32[2,4,32,128]{3,2,1,0:T(8,128)S(1)}) custom-call(bf16[8,8,4,32,128]{4,3,2,1,0:T(8,128)(2,1)S(1)} %all_to_all.10.planes, bf16[3,3,3,32,256]{4,3,2,1,0:T(8,128)(2,1)S(1)} %copy-done, f32[1,32]{1,0:T(1,128)S(1)} %bitcast.8), custom_call_target="tpu_custom_call" | custom-call | tf_op jit(solution)/shard_map/first_kernel/pallas_call | solution.py:188
  45.6 0.0 collective-permute-done.below
  45.6 3.0 %collective-permute-done.1.above = f32[4,32,128]{2,1,0:T(8,128)S(1)} collective-permute-done((f32[4,32,128]{2,1,0:T(8,128)S(1)}, f32[4,32,128]{2,1,0:T(8,128)S(1)}, u32[]{:S(2)}, u32[]{:S(2)}) %collective-permute-start.1) | collective-permute-done | bytes 65568 | tf_op jit(solution)/shard_map/ppermute | solution.py:181
  48.6 0.9 first_ends_kernel.1
  49.5 0.0 copy-start.1
  49.5 28.0 %all_to_all.11.planes = bf16[8,8,4,32,128]{4,3,2,1,0:T(8,128)(2,1)S(1)} all-to-all(bf16[8,8,4,32,128]{4,3,2,1,0:T(8,128)(2,1)S(1)} %first_ends_kernel.1), channel_id=1, replica_groups=mesh['gy'=64,'ch'=8] {'ch'}, dimensions={0} | all-to-all | bytes 4194304 | tf_op jit(solution)/shard_map/all_to_all | solution.py:204
  77.5 0.0 copy-done.1
  77.5 0.0 copy-start.2
  77.5 0.5 edge_kernel.3
  78.1 4.8 %collective-permute-start.2 = (f32[4,32,128]{2,1,0:T(8,128)S(1)}, f32[4,32,128]{2,1,0:T(8,128)S(1)}, u32[]{:S(2)}, u32[]{:S(2)}) collective-permute-start(f32[4,32,128]{2,1,0:T(8,128)S(1)} %get-tuple-element.18), channel_id=1, source_target_pairs={{0,8},{8,16},{16,24},{24,32},{32,40},{40,48},{48,56},{56,64},{64,7... | collective-permute-start | bytes 196616 | tf_op jit(solution)/shard_map/ppermute | solution.py:181
  82.9 1.9 %collective-permute-start.3 = (f32[4,32,128]{2,1,0:T(8,128)S(1)}, f32[4,32,128]{2,1,0:T(8,128)S(1)}, u32[]{:S(2)}, u32[]{:S(2)}) collective-permute-start(f32[4,32,128]{2,1,0:T(8,128)S(1)} %get-tuple-element.19), channel_id=1, source_target_pairs={{8,0},{16,8},{24,16},{32,24},{40,32},{48,40},{56,48},{64,56},{72,6... | collective-permute-start | bytes 196616 | tf_op jit(solution)/shard_map/ppermute | solution.py:181
  84.8 0.0 copy-done.2
  84.8 2.9 %second_kernel.1 = (bf16[32,8,4,128]{3,2,1,0:T(4,128)(2,1)}, f32[2,4,32,128]{3,2,1,0:T(8,128)S(1)}) custom-call(bf16[8,8,4,32,128]{4,3,2,1,0:T(8,128)(2,1)S(1)} %all_to_all.11.planes, bf16[3,3,3,32,256]{4,3,2,1,0:T(8,128)(2,1)S(1)} %copy-done.1, f32[1,32]{1,0:T(1,128)S(1)} %bitcast.7, bf16[8,4,32,128]{3,2,1,0:T(8,128)(2,1)S(1)} %bitcast.6), custom_call_target="tpu_custom_call" | custom-call | tf_op jit(solution)/shard_map/second_kernel/pallas_call | solution.py:207
  87.7 0.0 collective-permute-done.2.below
  87.7 4.3 %collective-permute-done.3.above = f32[4,32,128]{2,1,0:T(8,128)S(1)} collective-permute-done((f32[4,32,128]{2,1,0:T(8,128)S(1)}, f32[4,32,128]{2,1,0:T(8,128)S(1)}, u32[]{:S(2)}, u32[]{:S(2)}) %collective-permute-start.3) | collective-permute-done | bytes 65568 | tf_op jit(solution)/shard_map/ppermute | solution.py:181
  92.1 0.8 second_ends_kernel.1
Async XLA Ops:
  1.6 30.8 %copy-start = (bf16[3,3,3,32,256]{4,3,2,1,0:T(8,128)(2,1)S(1)}, bf16[3,3,3,32,256]{4,3,2,1,0:T(8,128)(2,1)}, u32[]{:S(2)}) copy-start(bf16[3,3,3,32,256]{4,3,2,1,0:T(8,128)(2,1)} %w_ref.5) | copy-start | bytes 1327108
  32.3 9.0 %copy-start.3 = (f32[32]{0:T(128)S(1)}, f32[32]{0:T(128)}, u32[]{:S(2)}) copy-start(f32[32]{0:T(128)} %param.7) | copy-start | bytes 388
  32.9 12.7 %collective-permute-start = (f32[4,32,128]{2,1,0:T(8,128)S(1)}, f32[4,32,128]{2,1,0:T(8,128)S(1)}, u32[]{:S(2)}, u32[]{:S(2)}) collective-permute-start(f32[4,32,128]{2,1,0:T(8,128)S(1)} %get-tuple-element.14), channel_id=1, source_target_pairs={{0,8},{8,16},{16,24},{24,32},{32,40},{40,48},{48,56},{56,64},{64,7... | collective-permute-start | bytes 196616 | tf_op jit(solution)/shard_map/ppermute | solution.py:181
  39.4 9.2 %collective-permute-start.1 = (f32[4,32,128]{2,1,0:T(8,128)S(1)}, f32[4,32,128]{2,1,0:T(8,128)S(1)}, u32[]{:S(2)}, u32[]{:S(2)}) collective-permute-start(f32[4,32,128]{2,1,0:T(8,128)S(1)} %get-tuple-element.15), channel_id=1, source_target_pairs={{8,0},{16,8},{24,16},{32,24},{40,32},{48,40},{56,48},{64,56},{72,6... | collective-permute-start | bytes 196616 | tf_op jit(solution)/shard_map/ppermute | solution.py:181
  49.5 28.0 %copy-start.1 = (bf16[3,3,3,32,256]{4,3,2,1,0:T(8,128)(2,1)S(1)}, bf16[3,3,3,32,256]{4,3,2,1,0:T(8,128)(2,1)}, u32[]{:S(2)}) copy-start(bf16[3,3,3,32,256]{4,3,2,1,0:T(8,128)(2,1)} %w_ref.7) | copy-start | bytes 1327108
  77.5 7.2 %copy-start.2 = (f32[32]{0:T(128)S(1)}, f32[32]{0:T(128)}, u32[]{:S(2)}) copy-start(f32[32]{0:T(128)} %param.9) | copy-start | bytes 388
  78.1 9.6 %collective-permute-start.2 = (f32[4,32,128]{2,1,0:T(8,128)S(1)}, f32[4,32,128]{2,1,0:T(8,128)S(1)}, u32[]{:S(2)}, u32[]{:S(2)}) collective-permute-start(f32[4,32,128]{2,1,0:T(8,128)S(1)} %get-tuple-element.18), channel_id=1, source_target_pairs={{0,8},{8,16},{16,24},{24,32},{32,40},{40,48},{48,56},{56,64},{64,7... | collective-permute-start | bytes 196616 | tf_op jit(solution)/shard_map/ppermute | solution.py:181
  82.9 9.2 %collective-permute-start.3 = (f32[4,32,128]{2,1,0:T(8,128)S(1)}, f32[4,32,128]{2,1,0:T(8,128)S(1)}, u32[]{:S(2)}, u32[]{:S(2)}) collective-permute-start(f32[4,32,128]{2,1,0:T(8,128)S(1)} %get-tuple-element.19), channel_id=1, source_target_pairs={{8,0},{16,8},{24,16},{32,24},{40,32},{48,40},{56,48},{64,56},{72,6... | collective-permute-start | bytes 196616 | tf_op jit(solution)/shard_map/ppermute | solution.py:181

commit v2 on v0

v2 whole, which is shorter than its diff:
```python
import jax
import jax.numpy as jnp
import numpy as np
from jax import lax
from jax.experimental import pallas as pl
from jax.experimental.pallas import tpu as pltpu
from jax.sharding import PartitionSpec as P

ROOT_HALF = np.float32(np.sqrt(0.5))
F32, BF16 = jnp.float32, jnp.bfloat16


def column(row_ref, n):
    i = lax.broadcasted_iota(jnp.int32, (n, n), 0)
    j = lax.broadcasted_iota(jnp.int32, (n, n), 1)
    square = jnp.where(i == j, jnp.broadcast_to(row_ref[...], (n, n)), 0.0)
    return jnp.sum(square, axis=1, keepdims=True)


def gelu(v):
    return 0.5 * v * (1.0 + lax.erf(v * ROOT_HALF))


def x_taps(a, co, nx):
    lane = lax.broadcasted_iota(jnp.int32, (co, nx), 1)
    left = jnp.where(lane == 0, 0.0, pltpu.roll(a[:co], 1, 1))
    right = jnp.where(lane == nx - 1, 0.0, pltpu.roll(a[2 * co :], nx - 1, 1))
    return a[co : 2 * co] + left + right


def z_taps(parts, co):
    nz = len(parts)
    sums = [None] * nz
    for zz in range(nz):
        for dz in range(3):
            z = zz - dz + 1
            if 0 <= z < nz:
                e = parts[zz][dz * 3 * co : (dz + 1) * 3 * co]
                sums[z] = e if sums[z] is None else sums[z] + e
    return sums


def rows(w_ref, dy):
    k = w_ref.shape[-1]
    if len(w_ref.shape) == 5:
        return w_ref[dy].reshape(-1, k)
    return w_ref[pl.ds(9 * dy, 9)].reshape(-1, k)


def cells(planes, p, z):
    lead, nx = planes.shape[:-4], planes.shape[-1]
    if len(lead) == 1:
        return planes[:, p, z].reshape(-1, nx)
    return jnp.concatenate([planes[:, a, p, z].reshape(-1, nx) for a in range(lead[1])], axis=0)


def edge(planes, w_ref, p, dy):
    nz, co, nx = planes.shape[-3:]
    parts = [
        jnp.dot(rows(w_ref, dy), cells(planes, p, zz), preferred_element_type=F32)
        for zz in range(nz)
    ]
    return [x_taps(s, co, nx) for s in z_taps(parts, co)]


def conv(planes, weights, take):
    ny, nz, co, nx = planes.shape[-4:]
    half = ny // 2
    none = jnp.zeros((weights[0].shape[-1], nx), BF16)
    for q in range(half):
        parts = [[] for _ in weights]
        for zz in range(nz):
            tiles = []
            for dy in range(3):
                pair = [q + dy - 1, q + dy - 1 + half]
                pair = [cells(planes, p, zz) if 0 <= p < ny else none for p in pair]
                tiles.append(jnp.concatenate(pair, axis=1))
            for j, w_ref in enumerate(weights):
                part = None
                for dy in range(3):
                    d = jnp.dot(rows(w_ref, dy), tiles[dy], preferred_element_type=F32)
                    part = d if part is None else part + d
                parts[j].append(part)
        for j in range(len(weights)):
            sums = z_taps(parts[j], co)
            for h in range(2):
                values = [x_taps(s[:, h * nx : (h + 1) * nx], co, nx) for s in sums]
                take(j, q + h * half, values)


def parcel_bias(slab, at):
    parts = slab[:, at : at + 3].astype(F32)
    return parts[:, 0:1] + parts[:, 1:2] + parts[:, 2:3]


def first_edge_kernel(planes, own, other, below, above):
    ny = planes.shape[-4]
    for out, p, dy in ((below, 0, 2), (above, ny - 1, 0)):
        for j, w_ref in enumerate((own, other)):
            for z, v in enumerate(edge(planes, w_ref, p, dy)):
                out[j, z] = v


def first_kernel(me, planes, own, other, b_ref, out, ends, other_bias, hidden, sems):
    ny, nz, co, nx = planes.shape[-4:]
    n = out.shape[0]
    slab = other[27]
    biases = [column(b_ref, co), parcel_bias(slab, 0)]
    biases = [jnp.broadcast_to(b, (co, nx)) for b in biases]
    other_bias[...] = jnp.broadcast_to(parcel_bias(slab, 3), (co, nx))

    def take(j, y, values):
        for z, v in enumerate(values):
            v = v + biases[j]
            if y == 0 or y == ny - 1:
                ends[y // (ny - 1), j, z] = v
            else:
                hidden[j, y - 1, z] = gelu(v).astype(BF16)

    conv(planes, (own, other), take)
    half = me[0] // n
    copies = []
    for j, slot in enumerate((half, 1 - half)):
        for d in range(n):
            c = pltpu.make_async_copy(hidden.at[j], out.at[d, slot, 1 : ny - 1], sems.at[j, d])
            c.start()
            copies.append(c)
    for c in copies:
        c.wait()


def first_ends_kernel(me, ends, below, above, _, out, hidden, sems):
    n, _, ny = out.shape[:3]
    half = me[0] // n
    copies = []
    for side, other in enumerate((below, above)):
        for j, slot in enumerate((half, 1 - half)):
            hidden[side, j] = gelu(ends[side, j] + other[1 - j]).astype(BF16)
            for d in range(n):
                c = pltpu.make_async_copy(
                    hidden.at[side, j], out.at[d, slot, side * (ny - 1)], sems.at[side, j, d]
                )
                c.start()
                copies.append(c)
    for c in copies:
        c.wait()


def second_edge_kernel(me, planes, own, other, outer_own, outer_other, inner_own, inner_other):
    ny = planes.shape[-4]
    half = me[0] // planes.shape[0]
    outer, inner = ((ny - 1) * half, 2 - 2 * half), ((ny - 1) * (1 - half), 2 * half)
    for at, outs in ((outer, (outer_own, outer_other)), (inner, (inner_own, inner_other))):
        for w_ref, out in zip((own, other), outs):
            for z, v in enumerate(edge(planes, w_ref, *at)):
                out[z] = v


def channels_first(values):
    return jnp.stack(values, axis=1).astype(BF16)


def two_parts(v):
    high = v.astype(BF16)
    return high, (v - high.astype(F32)).astype(BF16)


def second_kernel(me, planes, own, other, b_ref, other_bias, v_ref, inner_other, out, ends, sent, mine, sem):
    ny, nz, co, nx = planes.shape[-4:]
    n = planes.shape[0]
    half = me[0] // n
    own_bias = jnp.broadcast_to(column(b_ref, co), (co, nx))
    partner = me[0] + n - 2 * n * half

    def send(at, z, v):
        high, low = two_parts(v)
        sent[at, z] = high
        sent[at + 1, z] = low

    def take(j, y, values):
        side = y // (ny - 1)
        is_end = y == 0 or y == ny - 1
        role = half if side == 0 else 1 - half
        if j == 0:
            values = [v_ref[me[0], y, z].astype(F32) + (v + own_bias) for z, v in enumerate(values)]
            if not is_end:
                mine[:, y - 1] = channels_first(values)
                return
            for z, v in enumerate(values):
                ends[role, z] = v
            return
        values = [v_ref[partner, y, z].astype(F32) + (v + other_bias[...]) for z, v in enumerate(values)]
        for z, v in enumerate(values):
            if is_end:
                send(2 + 2 * role, z, v)
            else:
                sent[y - 1, z] = v.astype(BF16)

    conv(planes, (own, other), take)
    for z in range(nz):
        send(6, z, inner_other[z])
    copy = pltpu.make_async_copy(mine, out.at[:, pl.ds(half * ny + 1, ny - 2)], sem)
    copy.start()
    copy.wait()


def last_kernel(me, ends, inner_own, straight, across, received, _, out, whole, rest, sems):
    nz = ends.shape[1]
    ny = out.shape[1] // 2
    half = me[0] // 4
    mine, theirs = half * ny, (1 - half) * ny
    outer, inner = (ny - 1) * half, (ny - 1) * (1 - half)

    def got(at, z):
        return received[at, z].astype(F32) + received[at + 1, z].astype(F32)

    ends_at = (
        (mine + outer, lambda z: ends[0, z] + across[z]),
        (mine + inner, lambda z: ends[1, z] + got(6, z)),
        (theirs + inner, lambda z: got(2, z) + straight[z]),
        (theirs + outer, lambda z: got(4, z) + inner_own[z]),
    )
    copies = []
    for i, (at, value) in enumerate(ends_at):
        rest[i] = channels_first([value(z) for z in range(nz)])
        copies.append(pltpu.make_async_copy(rest.at[i], out.at[:, at], sems.at[i]))
        copies[-1].start()
    for y in range(ny - 2):
        whole[:, y] = channels_first([received[y, z].astype(F32) for z in range(nz)])
    copies.append(pltpu.make_async_copy(whole, out.at[:, pl.ds(theirs + 1, ny - 2)], sems.at[4]))
    copies[-1].start()
    for c in copies:
        c.wait()


ANY = pl.BlockSpec(memory_space=pl.ANY)
VMEM = pl.BlockSpec(memory_space=pltpu.VMEM)
SMEM = pl.BlockSpec(memory_space=pltpu.SMEM)
DMA = pltpu.SemaphoreType.DMA
PARAMS = pltpu.CompilerParams(vmem_limit_bytes=48 << 20)


def call(kernel, out_shape, in_specs, out_specs, scratch, **extra):
    return pl.pallas_call(
        kernel,
        out_shape=out_shape,
        in_specs=in_specs,
        out_specs=out_specs,
        scratch_shapes=scratch,
        compiler_params=PARAMS,
        name=kernel.__name__,
        **extra,
    )


def three_parts(v):
    parts = []
    for _ in range(3):
        high = lax.reduce_precision(v, 8, 7)
        parts.append(high.astype(BF16))
        v = v - high
    return parts


def per_device(volume, first_weight, first_bias, second_weight, second_bias):
    co, full, nz, nx = volume.shape
    n, length = lax.axis_size("ch"), lax.axis_size("gy")
    g, ny = n // 2, full // 2
    axes = ("gy", "ch")
    f32 = lambda *lead: jax.ShapeDtypeStruct((*lead, nz, co, nx), F32)
    bf16 = lambda *lead: jax.ShapeDtypeStruct((*lead, nz, co, nx), BF16)

    def device(row, half, x):
        return row * n + half * g + x

    def route(*moves):
        return [
            (device(row, half, x), device(row + on, there, x))
            for half, on, there in moves
            for row in range(length)
            if 0 <= row + on < length
            for x in range(g)
        ]

    to_next = route((0, 0, 1), (1, 1, 0))
    to_previous = route((1, 0, 0), (0, -1, 1))
    to_outer = route((0, -1, 0), (1, 1, 1))
    to_across = route((0, -1, 1), (1, 1, 0))
    to_partner = route((0, 0, 1), (1, 0, 0))
    weights_route = [
        (device(row ^ 2, 1 - half, x), device(row, half, x))
        for row in range(length)
        for half in range(2)
        for x in range(g)
    ]

    me = lax.axis_index("ch").astype(jnp.int32)[None]
    columns = jnp.stack(three_parts(first_bias) + three_parts(second_bias), axis=1)
    slab = jnp.pad(columns, ((0, 0), (0, first_weight.shape[4] - 6)))
    parcel = jnp.concatenate([first_weight.reshape(27, co, -1), slab[None]], axis=0)
    other_first = lax.ppermute(parcel, axes, weights_route)
    other_second = lax.ppermute(second_weight, axes, weights_route)

    cells_first = jnp.transpose(volume, (1, 2, 0, 3))
    sent = jnp.broadcast_to(cells_first.reshape(2, 1, ny, nz, co, nx), (2, g, ny, nz, co, nx))
    main = lax.all_to_all(sent.reshape(n, ny, nz, co, nx), "ch", 0, 0, tiled=True)

    below, above = call(first_edge_kernel, (f32(2), f32(2)), [VMEM] * 3, (VMEM, VMEM), [])(
        main, first_weight, other_first
    )
    lower = lax.ppermute(above, axes, to_next)
    upper = lax.ppermute(below, axes, to_previous)
    hidden, ends, other_bias = call(
        first_kernel,
        (bf16(g, 2, ny), f32(2, 2), jax.ShapeDtypeStruct((co, nx), F32)),
        [SMEM] + [VMEM] * 4,
        (ANY, VMEM, VMEM),
        [pltpu.VMEM((2, ny - 2, nz, co, nx), BF16), DMA((2, g))],
    )(me, main, first_weight, other_first, first_bias[None])
    hidden = call(
        first_ends_kernel,
        bf16(g, 2, ny),
        [SMEM] + [VMEM] * 3 + [ANY],
        ANY,
        [pltpu.VMEM((2, 2, nz, co, nx), BF16), DMA((2, 2, g))],
        input_output_aliases={4: 0},
    )(me, ends, lower, upper, hidden)

    groups = [list(range(g)), list(range(g, n))]
    gathered = lax.all_to_all(hidden, "ch", 0, 0, tiled=True, axis_index_groups=groups)

    outer_own, outer_other, inner_own, inner_other = call(
        second_edge_kernel, (f32(),) * 4, [SMEM] + [VMEM] * 3, (VMEM,) * 4, []
    )(me, gathered, second_weight, other_second)
    straight = lax.ppermute(outer_own, axes, to_outer)
    across = lax.ppermute(outer_other, axes, to_across)
    out_type = jax.ShapeDtypeStruct(volume.shape, BF16)
    out, ends, sent = call(
        second_kernel,
        (out_type, f32(2), bf16(8)),
        [SMEM] + [VMEM] * 7,
        (ANY, VMEM, VMEM),
        [pltpu.VMEM((co, ny - 2, nz, nx), BF16), DMA],
    )(me, gathered, second_weight, other_second, second_bias[None], other_bias, main, inner_other)
    received = lax.ppermute(sent, axes, to_partner)
    return call(
        last_kernel,
        out_type,
        [SMEM] + [VMEM] * 5 + [ANY],
        ANY,
        [pltpu.VMEM((co, ny - 2, nz, nx), BF16), pltpu.VMEM((4, co, nz, nx), BF16), DMA((5,))],
        input_output_aliases={6: 0},
    )(me, ends, inner_own, straight, across, received, out)


def solution(mesh):
    in_specs = (
        P("ch", "gy", None, None),
        P(None, None, None, "ch", None),
        P("ch"),
        P(None, None, None, "ch", None),
        P("ch"),
    )
    out_specs = P("ch", "gy", None, None)
    return jax.shard_map(
        per_device, mesh=mesh, in_specs=in_specs, out_specs=out_specs, check_vma=False
    )
```

time: 234 us -> 79.2 us (0.34)
  the two profiles are of different devices: /device:TPU:129 before, /device:TPU:123 now
where the time goes in v2:
time: 79.2 us; the launch traced here: 78.8 us
  starting transfers between devices  34 us (43%)
  waiting for transfers between devices  32.6 us (41%)
  Pallas kernels  9.51 us (12%)
  local copies, waits for them, and re-layouts  2.44 us (3%)
    ppermute x1, waiting for transfers between devices, per_device(): other_first = lax.ppermute(parcel, axes, weights_route)  11.9 us
    ppermute x1, waiting for transfers between devices, per_device(): other_second = lax.ppermute(second_weight, axes, weights_route)  9.48 us
    ppermute x1, starting transfers between devices, per_device(): straight = lax.ppermute(outer_own, axes, to_outer)  7.68 us
    ppermute x1, starting transfers between devices, per_device(): lower = lax.ppermute(above, axes, to_next)  6.57 us
    ppermute x1, waiting for transfers between devices, per_device(): across = lax.ppermute(outer_other, axes, to_across)  6.51 us
    all_to_all x1, starting transfers between devices, per_device(): lax.all_to_all(sent.reshape(n, ny, nz, co, nx), 'ch', 0, 0, tiled=True)  5.3 us
    ppermute x1, waiting for transfers between devices, per_device(): upper = lax.ppermute(below, axes, to_previous)  4.69 us
    all_to_all x1, starting transfers between devices, per_device(): lax.all_to_all(hidden, 'ch', 0, 0, tiled=True, axis_index_groups=groups)  4.38 us
  transfers between devices with their start and end apart: 9, of which 4 were waited for; matrix products, arithmetic and copies ran while one was open for 0% of the time, Pallas kernels for 4%

profile of v2, /device:TPU:123, one launch (start us, length us, event | category | flops | bytes accessed | tf_op | source)
XLA Modules:
  0.0 78.8 jit_solution(15244482393409165727)
XLA Ops:
  0.0 1.1 %copy.15 = bf16[2,4,4,32,128]{4,3,2,1,0:T(8,128)(2,1)S(1)} copy(bf16[2,4,4,32,128]{4,2,1,0,3:T(4,128)(2,1)} %bitcast.25) | data formatting | bytes 524288 | tf_op jit(solution)/shard_map/broadcast_in_dim | solution.py:305
  1.1 1.2 %broadcast_in_dim.21 = bf16[2,4,4,4,32,128]{5,4,3,2,1,0:T(8,128)(2,1)} broadcast(bf16[2,4,4,32,128]{4,3,2,1,0:T(8,128)(2,1)S(1)} %copy.15), dimensions={0,2,3,4,5} | broadcast | bytes 1310720 | tf_op jit(solution)/shard_map/broadcast_in_dim | solution.py:305
  2.3 5.3 %all-to-all-start = ((bf16[8,4,4,32,128]{4,3,2,1,0:T(8,128)(2,1)}), bf16[8,4,4,32,128]{4,3,2,1,0:T(8,128)(2,1)S(1)}, u32[]{:S(2)}, u32[]{:S(2)}) async-start(bf16[8,4,4,32,128]{4,3,2,1,0:T(8,128)(2,1)} %bitcast.3), calls=%async_computation | async-start | bytes 2097152 | tf_op jit(solution)/shard_map/all_to_all | solution.py:306
  7.6 0.0 copy-done.2
  7.6 0.0 copy-done.3
  7.6 0.1 copy.16
  7.8 0.0 copy-done
  7.8 2.0 %collective-permute-start = (bf16[28,32,256]{2,1,0:T(8,128)(2,1)S(1)}, bf16[28,32,256]{2,1,0:T(8,128)(2,1)S(1)}, u32[]{:S(2)}, u32[]{:S(2)}) collective-permute-start(bf16[28,32,256]{2,1,0:T(8,128)(2,1)S(1)} %pad_maximum_fusion), channel_id=1, source_target_pairs={{20,0},{21,1},{22,2},{23,3},{16,4},{17,5},{18,6},{19,7},{28,8},{29... | collective-permute-start | bytes 1376264 | tf_op jit(solution)/shard_map/ppermute | solution.py:301
  9.8 11.9 %collective-permute-done.other = bf16[28,32,256]{2,1,0:T(8,128)(2,1)S(1)} collective-permute-done((bf16[28,32,256]{2,1,0:T(8,128)(2,1)S(1)}, bf16[28,32,256]{2,1,0:T(8,128)(2,1)S(1)}, u32[]{:S(2)}, u32[]{:S(2)}) %collective-permute-start) | collective-permute-done | bytes 458784 | tf_op jit(solution)/shard_map/ppermute | solution.py:301
  21.7 0.0 all-to-all-done.planes.v_ref
  21.7 0.9 %first_edge_kernel.1 = (f32[2,4,32,128]{3,2,1,0:T(8,128)S(1)}, f32[2,4,32,128]{3,2,1,0:T(8,128)S(1)}) custom-call(bf16[8,4,4,32,128]{4,3,2,1,0:T(8,128)(2,1)S(1)} %all-to-all-done.planes.v_ref, bf16[3,3,3,32,256]{4,3,2,1,0:T(8,128)(2,1)S(1)} %copy-done, bf16[28,32,256]{2,1,0:T(8,128)(2,1)S(1)} %collective-permute-done.other), custom_call_target="tpu_custom_call" | custom-call | tf_op jit(solution)/shard_map/first_edge_kernel/pallas_call | solution.py:308
  22.6 6.6 %collective-permute-start.1 = (f32[2,4,32,128]{3,2,1,0:T(8,128)S(1)}, f32[2,4,32,128]{3,2,1,0:T(8,128)S(1)}, u32[]{:S(2)}, u32[]{:S(2)}) collective-permute-start(f32[2,4,32,128]{3,2,1,0:T(8,128)S(1)} %get-tuple-element.18), channel_id=1, source_target_pairs={{0,4},{1,5},{2,6},{3,7},{8,12},{9,13},{10,14},{11,15},{16,20},{17,... | collective-permute-start | bytes 393224 | tf_op jit(solution)/shard_map/ppermute | solution.py:311
  29.1 1.9 %collective-permute-start.2 = (f32[2,4,32,128]{3,2,1,0:T(8,128)S(1)}, f32[2,4,32,128]{3,2,1,0:T(8,128)S(1)}, u32[]{:S(2)}, u32[]{:S(2)}) collective-permute-start(f32[2,4,32,128]{3,2,1,0:T(8,128)S(1)} %get-tuple-element.19), channel_id=1, source_target_pairs={{4,0},{5,1},{6,2},{7,3},{12,8},{13,9},{14,10},{15,11},{20,16},{21,... | collective-permute-start | bytes 393224 | tf_op jit(solution)/shard_map/ppermute | solution.py:312
  31.1 3.0 %first_kernel.1 = (bf16[4,2,4,4,32,128]{5,4,3,2,1,0:T(8,128)(2,1)}, f32[2,2,4,32,128]{4,3,2,1,0:T(8,128)S(1)}, f32[32,128]{1,0:T(8,128)S(1)}) custom-call(s32[1]{0:T(128)} %bitcast.me, bf16[8,4,4,32,128]{4,3,2,1,0:T(8,128)(2,1)S(1)} %all-to-all-done.planes.v_ref, bf16[3,3,3,32,256]{4,3,2,1,0:T(8,128)(2,1)S(1)} %copy-done, ...), custom_call_target="tpu_custom_call" | custom-call | tf_op jit(solution)/shard_map/first_kernel/pallas_call | solution.py:313
  34.0 0.0 collective-permute-done.1.below
  34.1 4.7 %collective-permute-done.2.above = f32[2,4,32,128]{3,2,1,0:T(8,128)S(1)} collective-permute-done((f32[2,4,32,128]{3,2,1,0:T(8,128)S(1)}, f32[2,4,32,128]{3,2,1,0:T(8,128)S(1)}, u32[]{:S(2)}, u32[]{:S(2)}) %collective-permute-start.2) | collective-permute-done | bytes 131104 | tf_op jit(solution)/shard_map/ppermute | solution.py:312
  38.7 1.0 %first_ends_kernel.1 = bf16[4,2,4,4,32,128]{5,4,3,2,1,0:T(8,128)(2,1)} custom-call(s32[1]{0:T(128)} %bitcast.me, f32[2,2,4,32,128]{4,3,2,1,0:T(8,128)S(1)} %get-tuple-element.17.ends, f32[2,4,32,128]{3,2,1,0:T(8,128)S(1)} %collective-permute-done.1.below, f32[2,4,32,128]{3,2,1,0:T(8,128)S(1)} %collective-permute-done.2.above, ...), custom_call_target="tpu_custom_call", output_to_operand_aliasing={{}: (4, {})} | custom-call | tf_op jit(solution)/shard_map/first_ends_kernel/pallas_call | solution.py:320
  39.7 0.0 copy-start.1
  39.7 4.4 %all-to-all-start.1 = ((bf16[4,2,4,4,32,128]{5,4,3,2,1,0:T(8,128)(2,1)}), bf16[4,2,4,4,32,128]{5,4,3,2,1,0:T(8,128)(2,1)S(1)}, u32[]{:S(2)}, u32[]{:S(2)}) async-start(bf16[4,2,4,4,32,128]{5,4,3,2,1,0:T(8,128)(2,1)} %first_ends_kernel.1), calls=%async_computation.1 | async-start | bytes 2097152 | tf_op jit(solution)/shard_map/all_to_all | solution.py:330
  44.1 0.0 copy-done.1
  44.1 1.9 %collective-permute-start.3 = (bf16[3,3,3,32,256]{4,3,2,1,0:T(8,128)(2,1)S(1)}, bf16[3,3,3,32,256]{4,3,2,1,0:T(8,128)(2,1)S(1)}, u32[]{:S(2)}, u32[]{:S(2)}) collective-permute-start(bf16[3,3,3,32,256]{4,3,2,1,0:T(8,128)(2,1)S(1)} %copy-done.1), channel_id=1, source_target_pairs={{20,0},{21,1},{22,2},{23,3},{16,4},{17,5},{18,6},{19,7},{28,8},{29... | collective-permute-start | bytes 1327112 | tf_op jit(solution)/shard_map/ppermute | solution.py:302
  46.0 9.5 %collective-permute-done.3.other = bf16[3,3,3,32,256]{4,3,2,1,0:T(8,128)(2,1)S(1)} collective-permute-done((bf16[3,3,3,32,256]{4,3,2,1,0:T(8,128)(2,1)S(1)}, bf16[3,3,3,32,256]{4,3,2,1,0:T(8,128)(2,1)S(1)}, u32[]{:S(2)}, u32[]{:S(2)}) %collective-permute-start.3) | collective-permute-done | bytes 442400 | tf_op jit(solution)/shard_map/ppermute | solution.py:302
  55.5 0.0 all-to-all-done.1.planes
  55.5 0.9 %second_edge_kernel.1 = (f32[4,32,128]{2,1,0:T(8,128)S(1)}, f32[4,32,128]{2,1,0:T(8,128)S(1)}, f32[4,32,128]{2,1,0:T(8,128)S(1)}, f32[4,32,128]{2,1,0:T(8,128)S(1)}) custom-call(s32[1]{0:T(128)} %bitcast.me, bf16[4,2,4,4,32,128]{5,4,3,2,1,0:T(8,128)(2,1)S(1)} %all-to-all-done.1.planes, bf16[3,3,3,32,256]{4,3,2,1,0:T(8,128)(2,1)S(1)} %copy-done.1, ...), custom_call_target="tpu_custom_call" | custom-call | tf_op jit(solution)/shard_map/second_edge_kernel/pallas_call | solution.py:332
  56.4 2.8 %second_kernel.1 = (bf16[32,8,4,128]{3,2,1,0:T(4,128)(2,1)}, f32[2,4,32,128]{3,2,1,0:T(8,128)S(1)}, bf16[8,4,32,128]{3,2,1,0:T(8,128)(2,1)S(1)}) custom-call(s32[1]{0:T(128)} %bitcast.me, bf16[4,2,4,4,32,128]{5,4,3,2,1,0:T(8,128)(2,1)S(1)} %all-to-all-done.1.planes, bf16[3,3,3,32,256]{4,3,2,1,0:T(8,128)(2,1)S(1)} %copy-done.1, ...), custom_call_target="tpu_custom_call" | custom-call | tf_op jit(solution)/shard_map/second_kernel/pallas_call | solution.py:338
  59.2 1.9 %collective-permute-start.6 = (bf16[8,4,32,128]{3,2,1,0:T(8,128)(2,1)S(1)}, bf16[8,4,32,128]{3,2,1,0:T(8,128)(2,1)S(1)}, u32[]{:S(2)}, u32[]{:S(2)}) collective-permute-start(bf16[8,4,32,128]{3,2,1,0:T(8,128)(2,1)S(1)} %get-tuple-element.27), channel_id=1, source_target_pairs={{0,4},{1,5},{2,6},{3,7},{8,12},{9,13},{10,14},{11,15},{16,20},{17,... | collective-permute-start | bytes 786440 | tf_op jit(solution)/shard_map/ppermute | solution.py:345
  61.1 7.7 %collective-permute-start.4 = (f32[4,32,128]{2,1,0:T(8,128)S(1)}, f32[4,32,128]{2,1,0:T(8,128)S(1)}, u32[]{:S(2)}, u32[]{:S(2)}) collective-permute-start(f32[4,32,128]{2,1,0:T(8,128)S(1)} %get-tuple-element.25), channel_id=1, source_target_pairs={{8,0},{9,1},{10,2},{11,3},{16,8},{17,9},{18,10},{19,11},{24,16},{2... | collective-permute-start | bytes 196616 | tf_op jit(solution)/shard_map/ppermute | solution.py:335
  68.8 2.4 %collective-permute-start.5 = (f32[4,32,128]{2,1,0:T(8,128)S(1)}, f32[4,32,128]{2,1,0:T(8,128)S(1)}, u32[]{:S(2)}, u32[]{:S(2)}) collective-permute-start(f32[4,32,128]{2,1,0:T(8,128)S(1)} %get-tuple-element.26), channel_id=1, source_target_pairs={{8,4},{9,5},{10,6},{11,7},{16,12},{17,13},{18,14},{19,15},{24,20},... | collective-permute-start | bytes 196616 | tf_op jit(solution)/shard_map/ppermute | solution.py:336
  71.2 0.0 collective-permute-done.4.straight
  71.2 6.5 %collective-permute-done.5.across = f32[4,32,128]{2,1,0:T(8,128)S(1)} collective-permute-done((f32[4,32,128]{2,1,0:T(8,128)S(1)}, f32[4,32,128]{2,1,0:T(8,128)S(1)}, u32[]{:S(2)}, u32[]{:S(2)}) %collective-permute-start.5) | collective-permute-done | bytes 65568 | tf_op jit(solution)/shard_map/ppermute | solution.py:336
  77.7 0.0 collective-permute-done.6.received
  77.7 1.1 %last_kernel.1 = bf16[32,8,4,128]{3,2,1,0:T(4,128)(2,1)} custom-call(s32[1]{0:T(128)} %bitcast.me, f32[2,4,32,128]{3,2,1,0:T(8,128)S(1)} %get-tuple-element.23.ends, f32[4,32,128]{2,1,0:T(8,128)S(1)} %get-tuple-element.24.inner_own, f32[4,32,128]{2,1,0:T(8,128)S(1)} %collective-permute-done.4.straight, ...), custom_call_target="tpu_custom_call", output_to_operand_aliasing={{}: (6, {})} | custom-call | tf_op jit(solution)/shard_map/last_kernel/pallas_call | solution.py:346
  (7 shorter events, 0.1 us)
Async XLA Ops:
  2.3 5.3 %copy-start.2 = (f32[32]{0:T(128)S(1)}, f32[32]{0:T(128)}, u32[]{:S(2)}) copy-start(f32[32]{0:T(128)} %param.7) | copy-start | bytes 388
  2.3 5.3 %copy-start.3 = (f32[32]{0:T(128)S(1)}, f32[32]{0:T(128)}, u32[]{:S(2)}) copy-start(f32[32]{0:T(128)} %param.9) | copy-start | bytes 388
  2.3 5.5 %copy-start = (bf16[3,3,3,32,256]{4,3,2,1,0:T(8,128)(2,1)S(1)}, bf16[3,3,3,32,256]{4,3,2,1,0:T(8,128)(2,1)}, u32[]{:S(2)}) copy-start(bf16[3,3,3,32,256]{4,3,2,1,0:T(8,128)(2,1)} %own.5) | copy-start | bytes 1327108
  2.3 19.4 %all-to-all-start = ((bf16[8,4,4,32,128]{4,3,2,1,0:T(8,128)(2,1)}), bf16[8,4,4,32,128]{4,3,2,1,0:T(8,128)(2,1)S(1)}, u32[]{:S(2)}, u32[]{:S(2)}) async-start(bf16[8,4,4,32,128]{4,3,2,1,0:T(8,128)(2,1)} %bitcast.3), calls=%async_computation | async-start | bytes 2097152 | tf_op jit(solution)/shard_map/all_to_all | solution.py:306
  7.8 13.9 %collective-permute-start = (bf16[28,32,256]{2,1,0:T(8,128)(2,1)S(1)}, bf16[28,32,256]{2,1,0:T(8,128)(2,1)S(1)}, u32[]{:S(2)}, u32[]{:S(2)}) collective-permute-start(bf16[28,32,256]{2,1,0:T(8,128)(2,1)S(1)} %pad_maximum_fusion), channel_id=1, source_target_pairs={{20,0},{21,1},{22,2},{23,3},{16,4},{17,5},{18,6},{19,7},{28,8},{29... | collective-permute-start | bytes 1376264 | tf_op jit(solution)/shard_map/ppermute | solution.py:301
  22.6 11.5 %collective-permute-start.1 = (f32[2,4,32,128]{3,2,1,0:T(8,128)S(1)}, f32[2,4,32,128]{3,2,1,0:T(8,128)S(1)}, u32[]{:S(2)}, u32[]{:S(2)}) collective-permute-start(f32[2,4,32,128]{3,2,1,0:T(8,128)S(1)} %get-tuple-element.18), channel_id=1, source_target_pairs={{0,4},{1,5},{2,6},{3,7},{8,12},{9,13},{10,14},{11,15},{16,20},{17,... | collective-permute-start | bytes 393224 | tf_op jit(solution)/shard_map/ppermute | solution.py:311
  29.1 9.6 %collective-permute-start.2 = (f32[2,4,32,128]{3,2,1,0:T(8,128)S(1)}, f32[2,4,32,128]{3,2,1,0:T(8,128)S(1)}, u32[]{:S(2)}, u32[]{:S(2)}) collective-permute-start(f32[2,4,32,128]{3,2,1,0:T(8,128)S(1)} %get-tuple-element.19), channel_id=1, source_target_pairs={{4,0},{5,1},{6,2},{7,3},{12,8},{13,9},{14,10},{15,11},{20,16},{21,... | collective-permute-start | bytes 393224 | tf_op jit(solution)/shard_map/ppermute | solution.py:312
  39.7 4.4 %copy-start.1 = (bf16[3,3,3,32,256]{4,3,2,1,0:T(8,128)(2,1)S(1)}, bf16[3,3,3,32,256]{4,3,2,1,0:T(8,128)(2,1)}, u32[]{:S(2)}) copy-start(bf16[3,3,3,32,256]{4,3,2,1,0:T(8,128)(2,1)} %own.7) | copy-start | bytes 1327108
  39.7 15.8 %all-to-all-start.1 = ((bf16[4,2,4,4,32,128]{5,4,3,2,1,0:T(8,128)(2,1)}), bf16[4,2,4,4,32,128]{5,4,3,2,1,0:T(8,128)(2,1)S(1)}, u32[]{:S(2)}, u32[]{:S(2)}) async-start(bf16[4,2,4,4,32,128]{5,4,3,2,1,0:T(8,128)(2,1)} %first_ends_kernel.1), calls=%async_computation.1 | async-start | bytes 2097152 | tf_op jit(solution)/shard_map/all_to_all | solution.py:330
  44.1 11.4 %collective-permute-start.3 = (bf16[3,3,3,32,256]{4,3,2,1,0:T(8,128)(2,1)S(1)}, bf16[3,3,3,32,256]{4,3,2,1,0:T(8,128)(2,1)S(1)}, u32[]{:S(2)}, u32[]{:S(2)}) collective-permute-start(bf16[3,3,3,32,256]{4,3,2,1,0:T(8,128)(2,1)S(1)} %copy-done.1), channel_id=1, source_target_pairs={{20,0},{21,1},{22,2},{23,3},{16,4},{17,5},{18,6},{19,7},{28,8},{29... | collective-permute-start | bytes 1327112 | tf_op jit(solution)/shard_map/ppermute | solution.py:302
  59.2 18.5 %collective-permute-start.6 = (bf16[8,4,32,128]{3,2,1,0:T(8,128)(2,1)S(1)}, bf16[8,4,32,128]{3,2,1,0:T(8,128)(2,1)S(1)}, u32[]{:S(2)}, u32[]{:S(2)}) collective-permute-start(bf16[8,4,32,128]{3,2,1,0:T(8,128)(2,1)S(1)} %get-tuple-element.27), channel_id=1, source_target_pairs={{0,4},{1,5},{2,6},{3,7},{8,12},{9,13},{10,14},{11,15},{16,20},{17,... | collective-permute-start | bytes 786440 | tf_op jit(solution)/shard_map/ppermute | solution.py:345
  61.1 10.1 %collective-permute-start.4 = (f32[4,32,128]{2,1,0:T(8,128)S(1)}, f32[4,32,128]{2,1,0:T(8,128)S(1)}, u32[]{:S(2)}, u32[]{:S(2)}) collective-permute-start(f32[4,32,128]{2,1,0:T(8,128)S(1)} %get-tuple-element.25), channel_id=1, source_target_pairs={{8,0},{9,1},{10,2},{11,3},{16,8},{17,9},{18,10},{19,11},{24,16},{2... | collective-permute-start | bytes 196616 | tf_op jit(solution)/shard_map/ppermute | solution.py:335
  68.8 8.9 %collective-permute-start.5 = (f32[4,32,128]{2,1,0:T(8,128)S(1)}, f32[4,32,128]{2,1,0:T(8,128)S(1)}, u32[]{:S(2)}, u32[]{:S(2)}) collective-permute-start(f32[4,32,128]{2,1,0:T(8,128)S(1)} %get-tuple-element.26), channel_id=1, source_target_pairs={{8,4},{9,5},{10,6},{11,7},{16,12},{17,13},{18,14},{19,15},{24,20},... | collective-permute-start | bytes 196616 | tf_op jit(solution)/shard_map/ppermute | solution.py:336

commit v3 on v2

--- a/solution.py
+++ b/solution.py
@@ -93,18 +93,39 @@
     return parts[:, 0:1] + parts[:, 1:2] + parts[:, 2:3]
 
 
-def first_edge_kernel(planes, own, other, below, above):
+def half_index():
+    return lax.axis_index("ch") // (lax.axis_size("ch") // 2)
+
+
+def spread_kernel(planes, out, sems):
+    n, ny = out.shape[:2]
+    copies = [
+        pltpu.make_async_copy(planes.at[pl.ds(d // (n // 2) * ny, ny)], out.at[d], sems.at[d])
+        for d in range(n)
+    ]
+    for c in copies:
+        c.start()
+    for c in copies:
+        c.wait()
+
+
+def first_edge_kernel(planes, own, fetched, swapped, below, above, other):
     ny = planes.shape[-4]
+    part = fetched.shape[0]
+    second = other.shape[0] - part
+    core = lax.axis_index("gy") % 2
+    other[pl.ds(second * core, part)] = fetched[...]
+    other[pl.ds(second * (1 - core), part)] = swapped[...]
     for out, p, dy in ((below, 0, 2), (above, ny - 1, 0)):
         for j, w_ref in enumerate((own, other)):
             for z, v in enumerate(edge(planes, w_ref, p, dy)):
                 out[j, z] = v
 
 
-def first_kernel(me, planes, own, other, b_ref, out, ends, other_bias, hidden, sems):
+def first_kernel(planes, own, other, parcel, b_ref, out, ends, other_bias, hidden, sems):
     ny, nz, co, nx = planes.shape[-4:]
     n = out.shape[0]
-    slab = other[27]
+    slab = parcel[parcel.shape[0] - 1]
     biases = [column(b_ref, co), parcel_bias(slab, 0)]
     biases = [jnp.broadcast_to(b, (co, nx)) for b in biases]
     other_bias[...] = jnp.broadcast_to(parcel_bias(slab, 3), (co, nx))
@@ -118,7 +139,7 @@
                 hidden[j, y - 1, z] = gelu(v).astype(BF16)
 
     conv(planes, (own, other), take)
-    half = me[0] // n
+    half = half_index()
     copies = []
     for j, slot in enumerate((half, 1 - half)):
         for d in range(n):
@@ -129,9 +150,9 @@
         c.wait()
 
 
-def first_ends_kernel(me, ends, below, above, _, out, hidden, sems):
+def first_ends_kernel(ends, below, above, _, out, hidden, sems):
     n, _, ny = out.shape[:3]
-    half = me[0] // n
+    half = half_index()
     copies = []
     for side, other in enumerate((below, above)):
         for j, slot in enumerate((half, 1 - half)):
@@ -146,9 +167,9 @@
         c.wait()
 
 
-def second_edge_kernel(me, planes, own, other, outer_own, outer_other, inner_own, inner_other):
+def second_edge_kernel(planes, own, other, outer_own, outer_other, inner_own, inner_other):
     ny = planes.shape[-4]
-    half = me[0] // planes.shape[0]
+    half = half_index()
     outer, inner = ((ny - 1) * half, 2 - 2 * half), ((ny - 1) * (1 - half), 2 * half)
     for at, outs in ((outer, (outer_own, outer_other)), (inner, (inner_own, inner_other))):
         for w_ref, out in zip((own, other), outs):
@@ -160,84 +181,93 @@
     return jnp.stack(values, axis=1).astype(BF16)
 
 
-def two_parts(v):
-    high = v.astype(BF16)
-    return high, (v - high.astype(F32)).astype(BF16)
-
-
-def second_kernel(me, planes, own, other, b_ref, other_bias, v_ref, inner_other, out, ends, sent, mine, sem):
+def ends_role(y, ny):
+    return half_index() if y == 0 else 1 - half_index()
+
+
+def second_other_kernel(planes, w_ref, bias, v_ref, inner_edge, sent):
+    ny, nz = planes.shape[-4:-2]
+    n = planes.shape[0]
+    partner = lax.axis_index("ch") + n - 2 * n * half_index()
+
+    def take(_, y, values):
+        is_end = y == 0 or y == ny - 1
+        for z, v in enumerate(values):
+            v = v + bias[...]
+            if is_end:
+                sent[2 + ends_role(y, ny), z] = v.astype(BF16)
+            else:
+                sent[y - 1, z] = (v_ref[partner, y, z].astype(F32) + v).astype(BF16)
+
+    conv(planes, (w_ref,), take)
+    for z in range(nz):
+        sent[4, z] = inner_edge[z].astype(BF16)
+
+
+def second_own_kernel(planes, w_ref, b_ref, v_ref, out, ends, mine, sem):
     ny, nz, co, nx = planes.shape[-4:]
-    n = planes.shape[0]
-    half = me[0] // n
-    own_bias = jnp.broadcast_to(column(b_ref, co), (co, nx))
-    partner = me[0] + n - 2 * n * half
-
-    def send(at, z, v):
-        high, low = two_parts(v)
-        sent[at, z] = high
-        sent[at + 1, z] = low
-
-    def take(j, y, values):
-        side = y // (ny - 1)
-        is_end = y == 0 or y == ny - 1
-        role = half if side == 0 else 1 - half
-        if j == 0:
-            values = [v_ref[me[0], y, z].astype(F32) + (v + own_bias) for z, v in enumerate(values)]
-            if not is_end:
-                mine[:, y - 1] = channels_first(values)
-                return
+    bias = jnp.broadcast_to(column(b_ref, co), (co, nx))
+    me, half = lax.axis_index("ch"), half_index()
+
+    def take(_, y, values):
+        values = [v_ref[me, y, z].astype(F32) + (v + bias) for z, v in enumerate(values)]
+        if y == 0 or y == ny - 1:
             for z, v in enumerate(values):
-                ends[role, z] = v
-            return
-        values = [v_ref[partner, y, z].astype(F32) + (v + other_bias[...]) for z, v in enumerate(values)]
-        for z, v in enumerate(values):
-            if is_end:
-                send(2 + 2 * role, z, v)
-            else:
-                sent[y - 1, z] = v.astype(BF16)
-
-    conv(planes, (own, other), take)
-    for z in range(nz):
-        send(6, z, inner_other[z])
+                ends[ends_role(y, ny), z] = v
+        else:
+            mine[:, y - 1] = channels_first(values)
+
+    conv(planes, (w_ref,), take)
     copy = pltpu.make_async_copy(mine, out.at[:, pl.ds(half * ny + 1, ny - 2)], sem)
     copy.start()
     copy.wait()
 
 
-def last_kernel(me, ends, inner_own, straight, across, received, _, out, whole, rest, sems):
+def outer_end_kernel(ends, across, straight, _, out, plane, sem):
+    ny, half = out.shape[1] // 2, half_index()
+    plane[...] = channels_first([ends[0, z] + across[z] for z in range(ends.shape[1])])
+    copy = pltpu.make_async_copy(plane, out.at[:, half * ny + (ny - 1) * half], sem)
+    copy.start()
+    copy.wait()
+
+
+def last_kernel(ends, inner_own, straight, received, cells_first, _, out, whole, rest, sems):
     nz = ends.shape[1]
-    ny = out.shape[1] // 2
-    half = me[0] // 4
+    ny, half = out.shape[1] // 2, half_index()
     mine, theirs = half * ny, (1 - half) * ny
     outer, inner = (ny - 1) * half, (ny - 1) * (1 - half)
 
     def got(at, z):
-        return received[at, z].astype(F32) + received[at + 1, z].astype(F32)
+        return received[at, z].astype(F32)
+
+    def start(at, z):
+        return cells_first[at, z].astype(F32)
 
     ends_at = (
-        (mine + outer, lambda z: ends[0, z] + across[z]),
-        (mine + inner, lambda z: ends[1, z] + got(6, z)),
-        (theirs + inner, lambda z: got(2, z) + straight[z]),
-        (theirs + outer, lambda z: got(4, z) + inner_own[z]),
+        (mine + inner, lambda z: ends[1, z] + got(4, z)),
+        (theirs + inner, lambda z: start(theirs + inner, z) + (got(2, z) + straight[z])),
+        (theirs + outer, lambda z: start(theirs + outer, z) + (got(3, z) + inner_own[z])),
     )
     copies = []
+    for y in range(ny - 2):
+        whole[:, y] = channels_first([received[y, z].astype(F32) for z in range(nz)])
+    copies.append(pltpu.make_async_copy(whole, out.at[:, pl.ds(theirs + 1, ny - 2)], sems.at[3]))
+    copies[-1].start()
     for i, (at, value) in enumerate(ends_at):
         rest[i] = channels_first([value(z) for z in range(nz)])
         copies.append(pltpu.make_async_copy(rest.at[i], out.at[:, at], sems.at[i]))
         copies[-1].start()
-    for y in range(ny - 2):
-        whole[:, y] = channels_first([received[y, z].astype(F32) for z in range(nz)])
-    copies.append(pltpu.make_async_copy(whole, out.at[:, pl.ds(theirs + 1, ny - 2)], sems.at[4]))
-    copies[-1].start()
     for c in copies:
         c.wait()
 
 
 ANY = pl.BlockSpec(memory_space=pl.ANY)
 VMEM = pl.BlockSpec(memory_space=pltpu.VMEM)
-SMEM = pl.BlockSpec(memory_space=pltpu.SMEM)
 DMA = pltpu.SemaphoreType.DMA
 PARAMS = pltpu.CompilerParams(vmem_limit_bytes=48 << 20)
+
+
+LONG = pl.CostEstimate(flops=40_000_000_000, bytes_accessed=1_000_000, transcendentals=0)
 
 
 def call(kernel, out_shape, in_specs, out_specs, scratch, **extra):
@@ -294,63 +324,86 @@
         for x in range(g)
     ]
 
-    me = lax.axis_index("ch").astype(jnp.int32)[None]
+    core = lax.axis_index("gy") % 2
+    taps = 27
+    weight = first_weight.reshape(taps, co, -1)
+    part = (taps + 1) // 2
+    fetched = lax.ppermute(
+        lax.dynamic_slice_in_dim(weight, (taps - part) * core, part, axis=0), axes, weights_route
+    )
+    swapped = lax.ppermute(fetched, "gy", [(i, i ^ 1) for i in range(length)])
     columns = jnp.stack(three_parts(first_bias) + three_parts(second_bias), axis=1)
-    slab = jnp.pad(columns, ((0, 0), (0, first_weight.shape[4] - 6)))
-    parcel = jnp.concatenate([first_weight.reshape(27, co, -1), slab[None]], axis=0)
-    other_first = lax.ppermute(parcel, axes, weights_route)
-    other_second = lax.ppermute(second_weight, axes, weights_route)
+    slab = jnp.pad(columns, ((0, 0), (0, weight.shape[2] - 6)))
+    parcel = jnp.concatenate([second_weight.reshape(weight.shape), slab[None]], axis=0)
+    other_second = lax.ppermute(parcel, axes, weights_route)
 
     cells_first = jnp.transpose(volume, (1, 2, 0, 3))
-    sent = jnp.broadcast_to(cells_first.reshape(2, 1, ny, nz, co, nx), (2, g, ny, nz, co, nx))
-    main = lax.all_to_all(sent.reshape(n, ny, nz, co, nx), "ch", 0, 0, tiled=True)
-
-    below, above = call(first_edge_kernel, (f32(2), f32(2)), [VMEM] * 3, (VMEM, VMEM), [])(
-        main, first_weight, other_first
-    )
+    sent = call(spread_kernel, bf16(n, ny), [VMEM], ANY, [DMA((n,))])(cells_first)
+    main = lax.all_to_all(sent, "ch", 0, 0, tiled=True)
+
+    below, above, other_first = call(
+        first_edge_kernel,
+        (f32(2), f32(2), jax.ShapeDtypeStruct(weight.shape, BF16)),
+        [VMEM] * 4,
+        (VMEM,) * 3,
+        [],
+    )(main, first_weight, fetched, swapped)
     lower = lax.ppermute(above, axes, to_next)
     upper = lax.ppermute(below, axes, to_previous)
     hidden, ends, other_bias = call(
         first_kernel,
         (bf16(g, 2, ny), f32(2, 2), jax.ShapeDtypeStruct((co, nx), F32)),
-        [SMEM] + [VMEM] * 4,
+        [VMEM] * 5,
         (ANY, VMEM, VMEM),
         [pltpu.VMEM((2, ny - 2, nz, co, nx), BF16), DMA((2, g))],
-    )(me, main, first_weight, other_first, first_bias[None])
+    )(main, first_weight, other_first, other_second, first_bias[None])
     hidden = call(
         first_ends_kernel,
         bf16(g, 2, ny),
-        [SMEM] + [VMEM] * 3 + [ANY],
+        [VMEM] * 3 + [ANY],
         ANY,
         [pltpu.VMEM((2, 2, nz, co, nx), BF16), DMA((2, 2, g))],
-        input_output_aliases={4: 0},
-    )(me, ends, lower, upper, hidden)
+        input_output_aliases={3: 0},
+    )(ends, lower, upper, hidden)
 
     groups = [list(range(g)), list(range(g, n))]
     gathered = lax.all_to_all(hidden, "ch", 0, 0, tiled=True, axis_index_groups=groups)
 
     outer_own, outer_other, inner_own, inner_other = call(
-        second_edge_kernel, (f32(),) * 4, [SMEM] + [VMEM] * 3, (VMEM,) * 4, []
-    )(me, gathered, second_weight, other_second)
+        second_edge_kernel, (f32(),) * 4, [VMEM] * 3, (VMEM,) * 4, []
+    )(gathered, second_weight, other_second)
     straight = lax.ppermute(outer_own, axes, to_outer)
     across = lax.ppermute(outer_other, axes, to_across)
     out_type = jax.ShapeDtypeStruct(volume.shape, BF16)
-    out, ends, sent = call(
-        second_kernel,
-        (out_type, f32(2), bf16(8)),
-        [SMEM] + [VMEM] * 7,
-        (ANY, VMEM, VMEM),
+    sent = call(second_other_kernel, bf16(5), [VMEM] * 5, VMEM, [])(
+        gathered, other_second, other_bias, main, inner_other
+    )
+    received = lax.ppermute(sent, axes, to_partner)
+    out, ends = call(
+        second_own_kernel,
+        (out_type, f32(2)),
+        [VMEM] * 4,
+        (ANY, VMEM),
         [pltpu.VMEM((co, ny - 2, nz, nx), BF16), DMA],
-    )(me, gathered, second_weight, other_second, second_bias[None], other_bias, main, inner_other)
-    received = lax.ppermute(sent, axes, to_partner)
+        cost_estimate=LONG,
+    )(gathered, second_weight, second_bias[None], main)
+    out = call(
+        outer_end_kernel,
+        out_type,
+        [VMEM, VMEM, ANY, ANY],
+        ANY,
+        [pltpu.VMEM((co, nz, nx), BF16), DMA],
+        input_output_aliases={3: 0},
+        cost_estimate=LONG,
+    )(ends, across, straight, out)
     return call(
         last_kernel,
         out_type,
-        [SMEM] + [VMEM] * 5 + [ANY],
+        [VMEM] * 5 + [ANY],
         ANY,
-        [pltpu.VMEM((co, ny - 2, nz, nx), BF16), pltpu.VMEM((4, co, nz, nx), BF16), DMA((5,))],
-        input_output_aliases={6: 0},
-    )(me, ends, inner_own, straight, across, received, out)
+        [pltpu.VMEM((co, ny - 2, nz, nx), BF16), pltpu.VMEM((3, co, nz, nx), BF16), DMA((4,))],
+        input_output_aliases={5: 0},
+    )(ends, inner_own, straight, received, cells_first, out)
 
 
 def solution(mesh):

time: 79.2 us -> 73.3 us (0.926)
  the two profiles are of different devices: /device:TPU:123 before, /device:TPU:384 now
where the time goes in v3:
time: 73.3 us; the launch traced here: 72.9 us
  starting transfers between devices  34.9 us (48%)
  blocking collectives  16.4 us (22%)
  Pallas kernels  11.2 us (15%)
  waiting for transfers between devices  7.96 us (11%)
  local copies, waits for them, and re-layouts  1.24 us (2%)
  other arithmetic  0.87 us (1%)
    all_to_all x1, blocking collectives, per_device(): lax.all_to_all(hidden, 'ch', 0, 0, tiled=True, axis_index_groups=groups)  16.4 us
    ppermute x1, starting transfers between devices, per_device(): upper = lax.ppermute(below, axes, to_previous)  6.42 us
    ppermute x1, starting transfers between devices, per_device(): lax.ppermute(lax.dynamic_slice_in_dim(weight, (taps - part) * core, part,...  5.47 us
    all_to_all x1, starting transfers between devices, per_device(): main = lax.all_to_all(sent, 'ch', 0, 0, tiled=True)  5.46 us
    ppermute x1, starting transfers between devices, per_device(): across = lax.ppermute(outer_other, axes, to_across)  4.97 us
    ppermute x1, starting transfers between devices, per_device(): straight = lax.ppermute(outer_own, axes, to_outer)  4.37 us
    ppermute x1, waiting for transfers between devices, per_device(): lax.ppermute(lax.dynamic_slice_in_dim(weight, (taps - part) * core, part,...  2.99 us
    pallas_call x1, Pallas kernels, per_device(): call(first_kernel, (bf16(g, 2, ny), f32(2, 2), jax.ShapeDtypeStruct((co,...  2.85 us
  transfers between devices with their start and end apart: 9, of which 4 were waited for; matrix products, arithmetic and copies ran while one was open for 1% of the time, Pallas kernels for 10%

profile of v3, /device:TPU:384, one launch (start us, length us, event | category | flops | bytes accessed | tf_op | source)
XLA Modules:
  0.0 72.9 jit_solution(4267611135610461947)
XLA Ops:
  0.0 1.1 %copy.19 = bf16[32,8,4,128]{3,0,2,1:T(8,128)(2,1)S(1)} copy(bf16[32,8,4,128]{3,2,1,0:T(4,128)(2,1)} %param.5) | data formatting | bytes 524288 | tf_op args[0]
  1.1 1.1 %spread_kernel.1 = bf16[8,4,4,32,128]{4,3,2,1,0:T(8,128)(2,1)} custom-call(bf16[8,4,32,128]{3,2,1,0:T(8,128)(2,1)S(1)} %bitcast.22), custom_call_target="tpu_custom_call" | custom-call | tf_op jit(solution)/shard_map/spread_kernel/pallas_call | solution.py:341
  2.1 0.0 copy-start
  2.1 5.5 %all-to-all-start = ((bf16[8,4,4,32,128]{4,3,2,1,0:T(8,128)(2,1)}), bf16[8,4,4,32,128]{4,3,2,1,0:T(8,128)(2,1)S(1)}, u32[]{:S(2)}, u32[]{:S(2)}) async-start(bf16[8,4,4,32,128]{4,3,2,1,0:T(8,128)(2,1)} %spread_kernel.1), calls=%async_computation | async-start | bytes 2097152 | tf_op jit(solution)/shard_map/all_to_all | solution.py:342
  7.6 0.0 copy-start.2
  7.6 0.0 copy-start.3
  7.7 5.5 %collective-permute-start = (bf16[14,32,256]{2,1,0:T(8,128)(2,1)S(1)}, bf16[14,32,256]{2,1,0:T(8,128)(2,1)S(1)}, u32[]{:S(2)}, u32[]{:S(2)}) collective-permute-start(bf16[14,32,256]{2,1,0:T(8,128)(2,1)S(1)} %constant_dynamic-slice_fusion), channel_id=1, source_target_pairs={{20,0},{21,1},{22,2},{23,3},{16,4},{17,5},{18,6},{19,7},{28,8},{29... | collective-permute-start | bytes 688136 | tf_op jit(solution)/shard_map/ppermute | solution.py:331
  13.2 0.1 copy.17
  13.3 0.9 %pad_maximum_fusion = bf16[28,32,256]{2,1,0:T(8,128)(2,1)} fusion(bf16[1,32,256]{2,1,0:T(8,128)(2,1)S(1)} %pad_bitcast_fusion, bf16[27,32,256]{2,1,0:T(8,128)(2,1)S(1)} %bitcast.24), kind=kLoop, calls=%fused_computation | loop fusion | flops 229376 | bytes 917504 | tf_op jit(solution)/shard_map/concatenate | solution.py:337
  14.2 1.9 %collective-permute-start.2 = (bf16[28,32,256]{2,1,0:T(8,128)(2,1)}, bf16[28,32,256]{2,1,0:T(8,128)(2,1)S(1)}, u32[]{:S(2)}, u32[]{:S(2)}) collective-permute-start(bf16[28,32,256]{2,1,0:T(8,128)(2,1)} %pad_maximum_fusion), channel_id=1, source_target_pairs={{20,0},{21,1},{22,2},{23,3},{16,4},{17,5},{18,6},{19,7},{28,8},{29... | collective-permute-start | bytes 1376264 | tf_op jit(solution)/shard_map/ppermute | solution.py:338
  16.1 3.0 %collective-permute-done.fetched = bf16[14,32,256]{2,1,0:T(8,128)(2,1)S(1)} collective-permute-done((bf16[14,32,256]{2,1,0:T(8,128)(2,1)S(1)}, bf16[14,32,256]{2,1,0:T(8,128)(2,1)S(1)}, u32[]{:S(2)}, u32[]{:S(2)}) %collective-permute-start) | collective-permute-done | bytes 229408 | tf_op jit(solution)/shard_map/ppermute | solution.py:331
  19.1 1.9 %collective-permute-start.1 = (bf16[14,32,256]{2,1,0:T(8,128)(2,1)S(1)}, bf16[14,32,256]{2,1,0:T(8,128)(2,1)S(1)}, u32[]{:S(2)}, u32[]{:S(2)}) collective-permute-start(bf16[14,32,256]{2,1,0:T(8,128)(2,1)S(1)} %collective-permute-done.fetched), channel_id=1, source_target_pairs={{0,8},{8,0},{16,24},{24,16},{32,40},{40,32},{48,56},{56,48},{64,72... | collective-permute-start | bytes 688136 | tf_op jit(solution)/shard_map/ppermute | solution.py:334
  21.0 1.5 %collective-permute-done.1.swapped = bf16[14,32,256]{2,1,0:T(8,128)(2,1)S(1)} collective-permute-done((bf16[14,32,256]{2,1,0:T(8,128)(2,1)S(1)}, bf16[14,32,256]{2,1,0:T(8,128)(2,1)S(1)}, u32[]{:S(2)}, u32[]{:S(2)}) %collective-permute-start.1) | collective-permute-done | bytes 229408 | tf_op jit(solution)/shard_map/ppermute | solution.py:334
  22.5 0.8 %all-to-all-done.planes.v_ref = bf16[8,4,4,32,128]{4,3,2,1,0:T(8,128)(2,1)S(1)} async-done(((bf16[8,4,4,32,128]{4,3,2,1,0:T(8,128)(2,1)}), bf16[8,4,4,32,128]{4,3,2,1,0:T(8,128)(2,1)S(1)}, u32[]{:S(2)}, u32[]{:S(2)}) %all-to-all-start) | async-done | bytes 1048608 | tf_op jit(solution)/shard_map/all_to_all | solution.py:342
  23.3 0.9 %first_edge_kernel.1 = (f32[2,4,32,128]{3,2,1,0:T(8,128)S(1)}, f32[2,4,32,128]{3,2,1,0:T(8,128)S(1)}, bf16[27,32,256]{2,1,0:T(8,128)(2,1)S(1)}) custom-call(bf16[8,4,4,32,128]{4,3,2,1,0:T(8,128)(2,1)S(1)} %all-to-all-done.planes.v_ref, bf16[3,3,3,32,256]{4,3,2,1,0:T(8,128)(2,1)S(1)} %copy-done, bf16[14,32,256]{2,1,0:T(8,128)(2,1)S(1)} %collective-permute-done.fetched, ...), custom_call_target="tpu_custom_call" | custom-call | tf_op jit(solution)/shard_map/first_edge_kernel/pallas_call | solution.py:344
  24.2 2.5 %collective-permute-start.3 = (f32[2,4,32,128]{3,2,1,0:T(8,128)S(1)}, f32[2,4,32,128]{3,2,1,0:T(8,128)S(1)}, u32[]{:S(2)}, u32[]{:S(2)}) collective-permute-start(f32[2,4,32,128]{3,2,1,0:T(8,128)S(1)} %get-tuple-element.19), channel_id=1, source_target_pairs={{0,4},{1,5},{2,6},{3,7},{8,12},{9,13},{10,14},{11,15},{16,20},{17,... | collective-permute-start | bytes 393224 | tf_op jit(solution)/shard_map/ppermute | solution.py:351
  26.6 6.4 %collective-permute-start.4 = (f32[2,4,32,128]{3,2,1,0:T(8,128)S(1)}, f32[2,4,32,128]{3,2,1,0:T(8,128)S(1)}, u32[]{:S(2)}, u32[]{:S(2)}) collective-permute-start(f32[2,4,32,128]{3,2,1,0:T(8,128)S(1)} %get-tuple-element.20), channel_id=1, source_target_pairs={{4,0},{5,1},{6,2},{7,3},{12,8},{13,9},{14,10},{15,11},{20,16},{21,... | collective-permute-start | bytes 393224 | tf_op jit(solution)/shard_map/ppermute | solution.py:352
  33.1 0.0 collective-permute-done.2.parcel.other.w_ref
  33.1 2.9 %first_kernel.1 = (bf16[4,2,4,4,32,128]{5,4,3,2,1,0:T(8,128)(2,1)S(1)}, f32[2,2,4,32,128]{4,3,2,1,0:T(8,128)S(1)}, f32[32,128]{1,0:T(8,128)S(1)}) custom-call(bf16[8,4,4,32,128]{4,3,2,1,0:T(8,128)(2,1)S(1)} %all-to-all-done.planes.v_ref, bf16[3,3,3,32,256]{4,3,2,1,0:T(8,128)(2,1)S(1)} %copy-done, bf16[27,32,256]{2,1,0:T(8,128)(2,1)S(1)} %get-tuple-element.17.other, ...), custom_call_target="tpu_custom_call" | custom-call | tf_op jit(solution)/shard_map/first_kernel/pallas_call | solution.py:353
  35.9 0.0 collective-permute-done.4.above
  35.9 0.9 %first_ends_kernel.1 = bf16[4,2,4,4,32,128]{5,4,3,2,1,0:T(8,128)(2,1)S(1)} custom-call(f32[2,2,4,32,128]{4,3,2,1,0:T(8,128)S(1)} %get-tuple-element.18.ends, f32[2,4,32,128]{3,2,1,0:T(8,128)S(1)} %collective-permute-done.3.below, f32[2,4,32,128]{3,2,1,0:T(8,128)S(1)} %collective-permute-done.4.above, ...), custom_call_target="tpu_custom_call", output_to_operand_aliasing={{}: (3, {})} | custom-call | tf_op jit(solution)/shard_map/first_ends_kernel/pallas_call | solution.py:360
  36.9 16.4 %all_to_all.10.planes = bf16[4,2,4,4,32,128]{5,4,3,2,1,0:T(8,128)(2,1)S(1)} all-to-all(bf16[4,2,4,4,32,128]{5,4,3,2,1,0:T(8,128)(2,1)S(1)} %first_ends_kernel.1), channel_id=1, replica_groups={{0,1,2,3},{4,5,6,7},{8,9,10,11},{12,13,14,15},{16,17,18,19},{20,21,22,2..., dimensions={0} | all-to-all | bytes 2097152 | tf_op jit(solution)/shard_map/all_to_all | solution.py:370
  53.3 0.8 %second_edge_kernel.1 = (f32[4,32,128]{2,1,0:T(8,128)S(1)}, f32[4,32,128]{2,1,0:T(8,128)S(1)}, f32[4,32,128]{2,1,0:T(8,128)S(1)}, f32[4,32,128]{2,1,0:T(8,128)S(1)}) custom-call(bf16[4,2,4,4,32,128]{5,4,3,2,1,0:T(8,128)(2,1)S(1)} %all_to_all.10.planes, bf16[3,3,3,32,256]{4,3,2,1,0:T(8,128)(2,1)S(1)} %copy-done.1, ...), custom_call_target="tpu_custom_call" | custom-call | tf_op jit(solution)/shard_map/second_edge_kernel/pallas_call | solution.py:372
  54.2 4.4 %collective-permute-start.5 = (f32[4,32,128]{2,1,0:T(8,128)S(1)}, f32[4,32,128]{2,1,0:T(8,128)S(1)}, u32[]{:S(2)}, u32[]{:S(2)}) collective-permute-start(f32[4,32,128]{2,1,0:T(8,128)S(1)} %get-tuple-element.24), channel_id=1, source_target_pairs={{8,0},{9,1},{10,2},{11,3},{16,8},{17,9},{18,10},{19,11},{24,16},{2... | collective-permute-start | bytes 196616 | tf_op jit(solution)/shard_map/ppermute | solution.py:375
  58.6 5.0 %collective-permute-start.7 = (f32[4,32,128]{2,1,0:T(8,128)S(1)}, f32[4,32,128]{2,1,0:T(8,128)S(1)}, u32[]{:S(2)}, u32[]{:S(2)}) collective-permute-start(f32[4,32,128]{2,1,0:T(8,128)S(1)} %get-tuple-element.27), channel_id=1, source_target_pairs={{8,4},{9,5},{10,6},{11,7},{16,12},{17,13},{18,14},{19,15},{24,20},... | collective-permute-start | bytes 196616 | tf_op jit(solution)/shard_map/ppermute | solution.py:376
  63.5 1.2 %second_other_kernel.1 = bf16[5,4,32,128]{3,2,1,0:T(8,128)(2,1)S(1)} custom-call(bf16[4,2,4,4,32,128]{5,4,3,2,1,0:T(8,128)(2,1)S(1)} %all_to_all.10.planes, bf16[28,32,256]{2,1,0:T(8,128)(2,1)S(1)} %collective-permute-done.2.parcel.other.w_ref, f32[32,128]{1,0:T(8,128)S(1)} %get-tuple-element.25.bias, ...), custom_call_target="tpu_custom_call" | custom-call | tf_op jit(solution)/shard_map/second_other_kernel/pallas_call | solution.py:378
  64.7 1.9 %collective-permute-start.6 = (bf16[5,4,32,128]{3,2,1,0:T(8,128)(2,1)S(1)}, bf16[5,4,32,128]{3,2,1,0:T(8,128)(2,1)S(1)}, u32[]{:S(2)}, u32[]{:S(2)}) collective-permute-start(bf16[5,4,32,128]{3,2,1,0:T(8,128)(2,1)S(1)} %second_other_kernel.1), channel_id=1, source_target_pairs={{0,4},{1,5},{2,6},{3,7},{8,12},{9,13},{10,14},{11,15},{16,20},{17,... | collective-permute-start | bytes 491528 | tf_op jit(solution)/shard_map/ppermute | solution.py:381
  66.6 1.9 %second_own_kernel.1 = (bf16[32,8,4,128]{3,2,1,0:T(4,128)(2,1)}, f32[2,4,32,128]{3,2,1,0:T(8,128)S(1)}) custom-call(bf16[4,2,4,4,32,128]{5,4,3,2,1,0:T(8,128)(2,1)S(1)} %all_to_all.10.planes, bf16[3,3,3,32,256]{4,3,2,1,0:T(8,128)(2,1)S(1)} %copy-done.1, f32[1,32]{1,0:T(1,128)S(1)} %bitcast.26, bf16[8,4,4,32,128]{4,3,2,1,0:T(8,128)(2,1)S(1)} %all-to-all-done.planes.v_ref), custom_call_target="tpu_custom_call" | custom-call | flops 40000000000 | bytes 1000000 | tf_op jit(solution)/shard_map/second_own_kernel/pallas_call | solution.py:382
  68.5 0.0 collective-permute-done.5.straight
  68.5 0.7 outer_end_kernel.1._
  69.2 2.7 %collective-permute-done.6.received = bf16[5,4,32,128]{3,2,1,0:T(8,128)(2,1)S(1)} collective-permute-done((bf16[5,4,32,128]{3,2,1,0:T(8,128)(2,1)S(1)}, bf16[5,4,32,128]{3,2,1,0:T(8,128)(2,1)S(1)}, u32[]{:S(2)}, u32[]{:S(2)}) %collective-permute-start.6) | collective-permute-done | bytes 163872 | tf_op jit(solution)/shard_map/ppermute | solution.py:381
  71.9 1.0 %last_kernel.1 = bf16[32,8,4,128]{3,2,1,0:T(4,128)(2,1)} custom-call(f32[2,4,32,128]{3,2,1,0:T(8,128)S(1)} %get-tuple-element.22.ends, f32[4,32,128]{2,1,0:T(8,128)S(1)} %get-tuple-element.23.inner_own, f32[4,32,128]{2,1,0:T(8,128)S(1)} %collective-permute-done.5.straight, ...), custom_call_target="tpu_custom_call", output_to_operand_aliasing={{}: (5, {})} | custom-call | tf_op jit(solution)/shard_map/last_kernel/pallas_call | solution.py:399
  (11 shorter events, 0.1 us)
Async XLA Ops:
  2.1 5.5 %copy-start = (bf16[3,3,3,32,256]{4,3,2,1,0:T(8,128)(2,1)S(1)}, bf16[3,3,3,32,256]{4,3,2,1,0:T(8,128)(2,1)}, u32[]{:S(2)}) copy-start(bf16[3,3,3,32,256]{4,3,2,1,0:T(8,128)(2,1)} %own.4) | copy-start | bytes 1327108
  2.1 21.2 %all-to-all-start = ((bf16[8,4,4,32,128]{4,3,2,1,0:T(8,128)(2,1)}), bf16[8,4,4,32,128]{4,3,2,1,0:T(8,128)(2,1)S(1)}, u32[]{:S(2)}, u32[]{:S(2)}) async-start(bf16[8,4,4,32,128]{4,3,2,1,0:T(8,128)(2,1)} %spread_kernel.1), calls=%async_computation | async-start | bytes 2097152 | tf_op jit(solution)/shard_map/all_to_all | solution.py:342
  7.6 5.8 %copy-start.1 = (bf16[3,3,3,32,256]{4,3,2,1,0:T(8,128)(2,1)S(1)}, bf16[3,3,3,32,256]{4,3,2,1,0:T(8,128)(2,1)}, u32[]{:S(2)}) copy-start(bf16[3,3,3,32,256]{4,3,2,1,0:T(8,128)(2,1)} %own.5) | copy-start | bytes 1327108
  7.6 5.5 %copy-start.2 = (f32[32]{0:T(128)S(1)}, f32[32]{0:T(128)}, u32[]{:S(2)}) copy-start(f32[32]{0:T(128)} %param.7) | copy-start | bytes 388
  7.6 5.5 %copy-start.3 = (f32[32]{0:T(128)S(1)}, f32[32]{0:T(128)}, u32[]{:S(2)}) copy-start(f32[32]{0:T(128)} %param.9) | copy-start | bytes 388
  7.7 11.4 %collective-permute-start = (bf16[14,32,256]{2,1,0:T(8,128)(2,1)S(1)}, bf16[14,32,256]{2,1,0:T(8,128)(2,1)S(1)}, u32[]{:S(2)}, u32[]{:S(2)}) collective-permute-start(bf16[14,32,256]{2,1,0:T(8,128)(2,1)S(1)} %constant_dynamic-slice_fusion), channel_id=1, source_target_pairs={{20,0},{21,1},{22,2},{23,3},{16,4},{17,5},{18,6},{19,7},{28,8},{29... | collective-permute-start | bytes 688136 | tf_op jit(solution)/shard_map/ppermute | solution.py:331
  14.2 18.9 %collective-permute-start.2 = (bf16[28,32,256]{2,1,0:T(8,128)(2,1)}, bf16[28,32,256]{2,1,0:T(8,128)(2,1)S(1)}, u32[]{:S(2)}, u32[]{:S(2)}) collective-permute-start(bf16[28,32,256]{2,1,0:T(8,128)(2,1)} %pad_maximum_fusion), channel_id=1, source_target_pairs={{20,0},{21,1},{22,2},{23,3},{16,4},{17,5},{18,6},{19,7},{28,8},{29... | collective-permute-start | bytes 1376264 | tf_op jit(solution)/shard_map/ppermute | solution.py:338
  19.1 3.4 %collective-permute-start.1 = (bf16[14,32,256]{2,1,0:T(8,128)(2,1)S(1)}, bf16[14,32,256]{2,1,0:T(8,128)(2,1)S(1)}, u32[]{:S(2)}, u32[]{:S(2)}) collective-permute-start(bf16[14,32,256]{2,1,0:T(8,128)(2,1)S(1)} %collective-permute-done.fetched), channel_id=1, source_target_pairs={{0,8},{8,0},{16,24},{24,16},{32,40},{40,32},{48,56},{56,48},{64,72... | collective-permute-start | bytes 688136 | tf_op jit(solution)/shard_map/ppermute | solution.py:334
  24.2 11.8 %collective-permute-start.3 = (f32[2,4,32,128]{3,2,1,0:T(8,128)S(1)}, f32[2,4,32,128]{3,2,1,0:T(8,128)S(1)}, u32[]{:S(2)}, u32[]{:S(2)}) collective-permute-start(f32[2,4,32,128]{3,2,1,0:T(8,128)S(1)} %get-tuple-element.19), channel_id=1, source_target_pairs={{0,4},{1,5},{2,6},{3,7},{8,12},{9,13},{10,14},{11,15},{16,20},{17,... | collective-permute-start | bytes 393224 | tf_op jit(solution)/shard_map/ppermute | solution.py:351
  26.6 9.3 %collective-permute-start.4 = (f32[2,4,32,128]{3,2,1,0:T(8,128)S(1)}, f32[2,4,32,128]{3,2,1,0:T(8,128)S(1)}, u32[]{:S(2)}, u32[]{:S(2)}) collective-permute-start(f32[2,4,32,128]{3,2,1,0:T(8,128)S(1)} %get-tuple-element.20), channel_id=1, source_target_pairs={{4,0},{5,1},{6,2},{7,3},{12,8},{13,9},{14,10},{15,11},{20,16},{21,... | collective-permute-start | bytes 393224 | tf_op jit(solution)/shard_map/ppermute | solution.py:352
  54.2 14.3 %collective-permute-start.5 = (f32[4,32,128]{2,1,0:T(8,128)S(1)}, f32[4,32,128]{2,1,0:T(8,128)S(1)}, u32[]{:S(2)}, u32[]{:S(2)}) collective-permute-start(f32[4,32,128]{2,1,0:T(8,128)S(1)} %get-tuple-element.24), channel_id=1, source_target_pairs={{8,0},{9,1},{10,2},{11,3},{16,8},{17,9},{18,10},{19,11},{24,16},{2... | collective-permute-start | bytes 196616 | tf_op jit(solution)/shard_map/ppermute | solution.py:375
  58.6 10.0 %collective-permute-start.7 = (f32[4,32,128]{2,1,0:T(8,128)S(1)}, f32[4,32,128]{2,1,0:T(8,128)S(1)}, u32[]{:S(2)}, u32[]{:S(2)}) collective-permute-start(f32[4,32,128]{2,1,0:T(8,128)S(1)} %get-tuple-element.27), channel_id=1, source_target_pairs={{8,4},{9,5},{10,6},{11,7},{16,12},{17,13},{18,14},{19,15},{24,20},... | collective-permute-start | bytes 196616 | tf_op jit(solution)/shard_map/ppermute | solution.py:376
  64.7 7.2 %collective-permute-start.6 = (bf16[5,4,32,128]{3,2,1,0:T(8,128)(2,1)S(1)}, bf16[5,4,32,128]{3,2,1,0:T(8,128)(2,1)S(1)}, u32[]{:S(2)}, u32[]{:S(2)}) collective-permute-start(bf16[5,4,32,128]{3,2,1,0:T(8,128)(2,1)S(1)} %second_other_kernel.1), channel_id=1, source_target_pairs={{0,4},{1,5},{2,6},{3,7},{8,12},{9,13},{10,14},{11,15},{16,20},{17,... | collective-permute-start | bytes 491528 | tf_op jit(solution)/shard_map/ppermute | solution.py:381

commit v4 on v3

--- a/solution.py
+++ b/solution.py
@@ -1,3 +1,5 @@
+import math
+
 import jax
 import jax.numpy as jnp
 import numpy as np
@@ -63,18 +65,39 @@
     return [x_taps(s, co, nx) for s in z_taps(parts, co)]
 
 
-def conv(planes, weights, take):
-    ny, nz, co, nx = planes.shape[-4:]
+def half_cells(planes):
+    ny, nx = planes.shape[-4], planes.shape[-1]
+
+    def tile(p, z):
+        if 0 <= p < ny:
+            return cells(planes, p, z)
+        return jnp.zeros((math.prod(planes.shape[:-4]) * planes.shape[-2], nx), BF16)
+
+    return tile
+
+
+def wider_cells(planes):
+    ny, half = planes.shape[-4] - 1, half_index()
+
+    def tile(p, z):
+        if 0 <= p < ny:
+            return cells(planes, p + half, z)
+        v = cells(planes, max(p, 0), z)
+        return jnp.where(half == (1 if p < 0 else 0), v, jnp.zeros_like(v))
+
+    return tile
+
+
+def conv(tile, ny, planes, weights, take):
+    nz, co, nx = planes.shape[-3:]
     half = ny // 2
-    none = jnp.zeros((weights[0].shape[-1], nx), BF16)
     for q in range(half):
         parts = [[] for _ in weights]
         for zz in range(nz):
             tiles = []
             for dy in range(3):
                 pair = [q + dy - 1, q + dy - 1 + half]
-                pair = [cells(planes, p, zz) if 0 <= p < ny else none for p in pair]
-                tiles.append(jnp.concatenate(pair, axis=1))
+                tiles.append(jnp.concatenate([tile(p, zz) for p in pair], axis=1))
             for j, w_ref in enumerate(weights):
                 part = None
                 for dy in range(3):
@@ -99,8 +122,9 @@
 
 def spread_kernel(planes, out, sems):
     n, ny = out.shape[:2]
+    first = [0, planes.shape[0] - ny]
     copies = [
-        pltpu.make_async_copy(planes.at[pl.ds(d // (n // 2) * ny, ny)], out.at[d], sems.at[d])
+        pltpu.make_async_copy(planes.at[pl.ds(first[d // (n // 2)], ny)], out.at[d], sems.at[d])
         for d in range(n)
     ]
     for c in copies:
@@ -109,72 +133,73 @@
         c.wait()
 
 
-def first_edge_kernel(planes, own, fetched, swapped, below, above, other):
-    ny = planes.shape[-4]
+def first_edge_kernel(planes, own, fetched, swapped, outer, other):
     part = fetched.shape[0]
     second = other.shape[0] - part
     core = lax.axis_index("gy") % 2
     other[pl.ds(second * core, part)] = fetched[...]
     other[pl.ds(second * (1 - core), part)] = swapped[...]
-    for out, p, dy in ((below, 0, 2), (above, ny - 1, 0)):
-        for j, w_ref in enumerate((own, other)):
-            for z, v in enumerate(edge(planes, w_ref, p, dy)):
-                out[j, z] = v
+    half = half_index()
+    for j, w_ref in enumerate((own, other)):
+        for z, v in enumerate(edge(planes, w_ref, (planes.shape[-4] - 1) * half, 2 - 2 * half)):
+            outer[j, z] = v
 
 
 def first_kernel(planes, own, other, parcel, b_ref, out, ends, other_bias, hidden, sems):
-    ny, nz, co, nx = planes.shape[-4:]
-    n = out.shape[0]
+    n, _, ny, nz, co, nx = out.shape
     slab = parcel[parcel.shape[0] - 1]
     biases = [column(b_ref, co), parcel_bias(slab, 0)]
     biases = [jnp.broadcast_to(b, (co, nx)) for b in biases]
     other_bias[...] = jnp.broadcast_to(parcel_bias(slab, 3), (co, nx))
+
+    half = half_index()
+    copies = []
 
     def take(j, y, values):
         for z, v in enumerate(values):
             v = v + biases[j]
             if y == 0 or y == ny - 1:
                 ends[y // (ny - 1), j, z] = v
-            else:
-                hidden[j, y - 1, z] = gelu(v).astype(BF16)
-
-    conv(planes, (own, other), take)
-    half = half_index()
-    copies = []
+            hidden[j, y, z] = gelu(v).astype(BF16)
+
+    conv(wider_cells(planes), ny, planes, (own, other), take)
     for j, slot in enumerate((half, 1 - half)):
         for d in range(n):
-            c = pltpu.make_async_copy(hidden.at[j], out.at[d, slot, 1 : ny - 1], sems.at[j, d])
+            c = pltpu.make_async_copy(hidden.at[j], out.at[d, slot], sems.at[j, d])
             c.start()
             copies.append(c)
     for c in copies:
         c.wait()
 
 
-def first_ends_kernel(ends, below, above, _, out, hidden, sems):
+def first_ends_kernel(ends, outer, _, out, hidden, sems):
     n, _, ny = out.shape[:3]
     half = half_index()
     copies = []
-    for side, other in enumerate((below, above)):
-        for j, slot in enumerate((half, 1 - half)):
-            hidden[side, j] = gelu(ends[side, j] + other[1 - j]).astype(BF16)
-            for d in range(n):
-                c = pltpu.make_async_copy(
-                    hidden.at[side, j], out.at[d, slot, side * (ny - 1)], sems.at[side, j, d]
-                )
-                c.start()
-                copies.append(c)
+    for j, slot in enumerate((half, 1 - half)):
+        hidden[j] = gelu(ends[half, j] + outer[1 - j]).astype(BF16)
+        for d in range(n):
+            c = pltpu.make_async_copy(hidden.at[j], out.at[d, slot, (ny - 1) * half], sems.at[j, d])
+            c.start()
+            copies.append(c)
     for c in copies:
         c.wait()
 
 
-def second_edge_kernel(planes, own, other, outer_own, outer_other, inner_own, inner_other):
-    ny = planes.shape[-4]
-    half = half_index()
-    outer, inner = ((ny - 1) * half, 2 - 2 * half), ((ny - 1) * (1 - half), 2 * half)
-    for at, outs in ((outer, (outer_own, outer_other)), (inner, (inner_own, inner_other))):
-        for w_ref, out in zip((own, other), outs):
-            for z, v in enumerate(edge(planes, w_ref, *at)):
-                out[z] = v
+def outer_edge(planes):
+    half = half_index()
+    return (planes.shape[-4] - 1) * half, 2 - 2 * half
+
+
+def inner_edge(planes):
+    half = half_index()
+    return (planes.shape[-4] - 1) * (1 - half), 2 * half
+
+
+def second_edge_kernel(planes, own, other, outer):
+    for j, w_ref in enumerate((own, other)):
+        for z, v in enumerate(edge(planes, w_ref, *outer_edge(planes))):
+            outer[j, z] = v
 
 
 def channels_first(values):
@@ -185,53 +210,62 @@
     return half_index() if y == 0 else 1 - half_index()
 
 
-def second_other_kernel(planes, w_ref, bias, v_ref, inner_edge, sent):
-    ny, nz = planes.shape[-4:-2]
+def second_other_kernel(planes, w_ref, bias, v_ref, sent, ends):
+    ny = planes.shape[-4]
     n = planes.shape[0]
-    partner = lax.axis_index("ch") + n - 2 * n * half_index()
+    half = half_index()
+    partner = lax.axis_index("ch") + n - 2 * n * half
 
     def take(_, y, values):
-        is_end = y == 0 or y == ny - 1
         for z, v in enumerate(values):
             v = v + bias[...]
-            if is_end:
-                sent[2 + ends_role(y, ny), z] = v.astype(BF16)
+            whole = v_ref[partner, y + half, z].astype(F32) + v
+            if y == 0 or y == ny - 1:
+                role = ends_role(y, ny)
+                sent[2 + role, z] = v.astype(BF16)
+                ends[role, z] = whole
             else:
-                sent[y - 1, z] = (v_ref[partner, y, z].astype(F32) + v).astype(BF16)
-
-    conv(planes, (w_ref,), take)
-    for z in range(nz):
-        sent[4, z] = inner_edge[z].astype(BF16)
-
-
-def second_own_kernel(planes, w_ref, b_ref, v_ref, out, ends, mine, sem):
+                sent[y - 1, z] = whole.astype(BF16)
+
+    conv(half_cells(planes), ny, planes, (w_ref,), take)
+    for z, v in enumerate(edge(planes, w_ref, *inner_edge(planes))):
+        sent[4, z] = v.astype(BF16)
+
+
+def finish_kernel(ends, outer, _, sent):
+    sent[2] = (ends[0] + outer[0]).astype(BF16)
+
+
+def second_own_kernel(planes, w_ref, b_ref, v_ref, out, ends, inner_own, mine, sem):
     ny, nz, co, nx = planes.shape[-4:]
     bias = jnp.broadcast_to(column(b_ref, co), (co, nx))
     me, half = lax.axis_index("ch"), half_index()
 
     def take(_, y, values):
-        values = [v_ref[me, y, z].astype(F32) + (v + bias) for z, v in enumerate(values)]
+        values = [v_ref[me, y + half, z].astype(F32) + (v + bias) for z, v in enumerate(values)]
         if y == 0 or y == ny - 1:
             for z, v in enumerate(values):
                 ends[ends_role(y, ny), z] = v
         else:
             mine[:, y - 1] = channels_first(values)
 
-    conv(planes, (w_ref,), take)
+    conv(half_cells(planes), ny, planes, (w_ref,), take)
     copy = pltpu.make_async_copy(mine, out.at[:, pl.ds(half * ny + 1, ny - 2)], sem)
     copy.start()
+    for z, v in enumerate(edge(planes, w_ref, *inner_edge(planes))):
+        inner_own[z] = v
     copy.wait()
 
 
-def outer_end_kernel(ends, across, straight, _, out, plane, sem):
+def outer_end_kernel(ends, outer, _, out, plane, sem):
     ny, half = out.shape[1] // 2, half_index()
-    plane[...] = channels_first([ends[0, z] + across[z] for z in range(ends.shape[1])])
+    plane[...] = channels_first([ends[0, z] + outer[1, z] for z in range(ends.shape[1])])
     copy = pltpu.make_async_copy(plane, out.at[:, half * ny + (ny - 1) * half], sem)
     copy.start()
     copy.wait()
 
 
-def last_kernel(ends, inner_own, straight, received, cells_first, _, out, whole, rest, sems):
+def last_kernel(ends, inner_own, received, cells_first, _, out, whole, rest, sems):
     nz = ends.shape[1]
     ny, half = out.shape[1] // 2, half_index()
     mine, theirs = half * ny, (1 - half) * ny
@@ -245,7 +279,7 @@
 
     ends_at = (
         (mine + inner, lambda z: ends[1, z] + got(4, z)),
-        (theirs + inner, lambda z: start(theirs + inner, z) + (got(2, z) + straight[z])),
+        (theirs + inner, lambda z: got(2, z)),
         (theirs + outer, lambda z: start(theirs + outer, z) + (got(3, z) + inner_own[z])),
     )
     copies = []
@@ -312,9 +346,6 @@
             for x in range(g)
         ]
 
-    to_next = route((0, 0, 1), (1, 1, 0))
-    to_previous = route((1, 0, 0), (0, -1, 1))
-    to_outer = route((0, -1, 0), (1, 1, 1))
     to_across = route((0, -1, 1), (1, 1, 0))
     to_partner = route((0, 0, 1), (1, 0, 0))
     weights_route = [
@@ -338,72 +369,71 @@
     other_second = lax.ppermute(parcel, axes, weights_route)
 
     cells_first = jnp.transpose(volume, (1, 2, 0, 3))
-    sent = call(spread_kernel, bf16(n, ny), [VMEM], ANY, [DMA((n,))])(cells_first)
+    sent = call(spread_kernel, bf16(n, ny + 1), [VMEM], ANY, [DMA((n,))])(cells_first)
     main = lax.all_to_all(sent, "ch", 0, 0, tiled=True)
 
-    below, above, other_first = call(
+    outer, other_first = call(
         first_edge_kernel,
-        (f32(2), f32(2), jax.ShapeDtypeStruct(weight.shape, BF16)),
+        (f32(2), jax.ShapeDtypeStruct(weight.shape, BF16)),
         [VMEM] * 4,
-        (VMEM,) * 3,
+        (VMEM,) * 2,
         [],
     )(main, first_weight, fetched, swapped)
-    lower = lax.ppermute(above, axes, to_next)
-    upper = lax.ppermute(below, axes, to_previous)
+    outer = lax.ppermute(outer, axes, to_across)
     hidden, ends, other_bias = call(
         first_kernel,
         (bf16(g, 2, ny), f32(2, 2), jax.ShapeDtypeStruct((co, nx), F32)),
         [VMEM] * 5,
         (ANY, VMEM, VMEM),
-        [pltpu.VMEM((2, ny - 2, nz, co, nx), BF16), DMA((2, g))],
+        [pltpu.VMEM((2, ny, nz, co, nx), BF16), DMA((2, g))],
     )(main, first_weight, other_first, other_second, first_bias[None])
     hidden = call(
         first_ends_kernel,
         bf16(g, 2, ny),
-        [VMEM] * 3 + [ANY],
+        [VMEM] * 2 + [ANY],
         ANY,
-        [pltpu.VMEM((2, 2, nz, co, nx), BF16), DMA((2, 2, g))],
-        input_output_aliases={3: 0},
-    )(ends, lower, upper, hidden)
+        [pltpu.VMEM((2, nz, co, nx), BF16), DMA((2, g))],
+        input_output_aliases={2: 0},
+    )(ends, outer, hidden)
 
     groups = [list(range(g)), list(range(g, n))]
     gathered = lax.all_to_all(hidden, "ch", 0, 0, tiled=True, axis_index_groups=groups)
 
-    outer_own, outer_other, inner_own, inner_other = call(
-        second_edge_kernel, (f32(),) * 4, [VMEM] * 3, (VMEM,) * 4, []
-    )(gathered, second_weight, other_second)
-    straight = lax.ppermute(outer_own, axes, to_outer)
-    across = lax.ppermute(outer_other, axes, to_across)
+    outer = call(second_edge_kernel, f32(2), [VMEM] * 3, VMEM, [])(
+        gathered, second_weight, other_second
+    )
+    outer = lax.ppermute(outer, axes, to_across)
     out_type = jax.ShapeDtypeStruct(volume.shape, BF16)
-    sent = call(second_other_kernel, bf16(5), [VMEM] * 5, VMEM, [])(
-        gathered, other_second, other_bias, main, inner_other
+    sent, ends = call(second_other_kernel, (bf16(5), f32(2)), [VMEM] * 4, (VMEM, VMEM), [])(
+        gathered, other_second, other_bias, main
+    )
+    sent = call(finish_kernel, bf16(5), [VMEM] * 3, VMEM, [], input_output_aliases={2: 0})(
+        ends, outer, sent
     )
     received = lax.ppermute(sent, axes, to_partner)
-    out, ends = call(
+    out, ends, inner_own = call(
         second_own_kernel,
-        (out_type, f32(2)),
+        (out_type, f32(2), f32()),
         [VMEM] * 4,
-        (ANY, VMEM),
+        (ANY, VMEM, VMEM),
         [pltpu.VMEM((co, ny - 2, nz, nx), BF16), DMA],
-        cost_estimate=LONG,
     )(gathered, second_weight, second_bias[None], main)
     out = call(
         outer_end_kernel,
         out_type,
-        [VMEM, VMEM, ANY, ANY],
+        [VMEM, VMEM, ANY],
         ANY,
         [pltpu.VMEM((co, nz, nx), BF16), DMA],
-        input_output_aliases={3: 0},
-        cost_estimate=LONG,
-    )(ends, across, straight, out)
+        input_output_aliases={2: 0},
+    )(ends, outer, out)
     return call(
         last_kernel,
         out_type,
-        [VMEM] * 5 + [ANY],
+        [VMEM] * 4 + [ANY],
         ANY,
         [pltpu.VMEM((co, ny - 2, nz, nx), BF16), pltpu.VMEM((3, co, nz, nx), BF16), DMA((4,))],
-        input_output_aliases={5: 0},
-    )(ends, inner_own, straight, received, cells_first, out)
+        input_output_aliases={4: 0},
+    )(ends, inner_own, received, cells_first, out)
 
 
 def solution(mesh):

time: 73.3 us -> 70.2 us (0.958)
  starting transfers between devices: 34.9 us -> 28.5 us
  waiting for transfers between devices: 7.96 us -> 13.4 us
  blocking collectives: 16.4 us -> 14.5 us
    ppermute x4 -> x2, starting transfers between devices: 18.2 us -> 11.9 us  [per_device(): outer = lax.ppermute(outer, axes, to_across)]
    all_to_all x1, waiting for transfers between devices: 0.81 us -> 3.7 us  [per_device(): main = lax.all_to_all(sent, 'ch', 0, 0, tiled=True)]
    ppermute x4 -> x2, waiting for transfers between devices: 0.01 us -> 2.51 us  [per_device(): outer = lax.ppermute(outer, axes, to_across)]
    all_to_all x1, blocking collectives: 16.4 us -> 14.5 us  [per_device(): lax.all_to_all(hidden, 'ch', 0, 0, tiled=True, axis_index_groups=groups)]
    pallas_call x8 -> x9, Pallas kernels: 8.39 us -> 7.67 us  [the longest x1 1.99 us: per_device(): call(second_own_kernel, (out_type, f32(2), f32()), [VMEM] * 4, (ANY, VMEM...]
  transfers between devices with their start and end apart: 9 -> 7, of which waited for: 4 -> 6; matrix products, arithmetic and copies ran while one was open for 1% -> 1% of each run, Pallas kernels for 10% -> 12%
where the time goes in v4:
time: 70.2 us; the launch traced here: 69.9 us
  starting transfers between devices  28.5 us (41%)
  blocking collectives  14.5 us (21%)
  waiting for transfers between devices  13.4 us (19%)
  Pallas kernels  11.2 us (16%)
  local copies, waits for them, and re-layouts  1.25 us (2%)
  other arithmetic  0.82 us (1%)
    all_to_all x1, blocking collectives, per_device(): lax.all_to_all(hidden, 'ch', 0, 0, tiled=True, axis_index_groups=groups)  14.5 us
    ppermute x2, starting transfers between devices, per_device(): outer = lax.ppermute(outer, axes, to_across)  11.9 us
    all_to_all x1, starting transfers between devices, per_device(): main = lax.all_to_all(sent, 'ch', 0, 0, tiled=True)  5.46 us
    ppermute x1, starting transfers between devices, per_device(): lax.ppermute(lax.dynamic_slice_in_dim(weight, (taps - part) * core, part,...  5.36 us
    all_to_all x1, waiting for transfers between devices, per_device(): main = lax.all_to_all(sent, 'ch', 0, 0, tiled=True)  3.7 us
    pallas_call x1, Pallas kernels, per_device(): call(first_kernel, (bf16(g, 2, ny), f32(2, 2), jax.ShapeDtypeStruct((co,...  3.54 us
    ppermute x1, waiting for transfers between devices, per_device(): lax.ppermute(lax.dynamic_slice_in_dim(weight, (taps - part) * core, part,...  3.12 us
    ppermute x1, waiting for transfers between devices, per_device(): received = lax.ppermute(sent, axes, to_partner)  2.59 us
  transfers between devices with their start and end apart: 7, of which 6 were waited for; matrix products, arithmetic and copies ran while one was open for 1% of the time, Pallas kernels for 12%

profile of v4, /device:TPU:384, one launch (start us, length us, event | category | flops | bytes accessed | tf_op | source)
XLA Modules:
  0.0 69.9 jit_solution(12653617192872519078)
XLA Ops:
  0.0 1.1 %copy.20 = bf16[32,8,4,128]{3,0,2,1:T(8,128)(2,1)S(1)} copy(bf16[32,8,4,128]{3,2,1,0:T(4,128)(2,1)} %param.5) | data formatting | bytes 524288 | tf_op args[0]
  1.1 1.1 %spread_kernel.1 = bf16[8,5,4,32,128]{4,3,2,1,0:T(8,128)(2,1)} custom-call(bf16[8,4,32,128]{3,2,1,0:T(8,128)(2,1)S(1)} %bitcast.23), custom_call_target="tpu_custom_call" | custom-call | tf_op jit(solution)/shard_map/spread_kernel/pallas_call | solution.py:372
  2.2 0.0 copy-start.1
  2.2 0.0 copy-start.2
  2.2 0.0 copy-start.3
  2.2 0.0 copy-start
  2.3 5.5 %all-to-all-start = ((bf16[8,5,4,32,128]{4,3,2,1,0:T(8,128)(2,1)}), bf16[8,5,4,32,128]{4,3,2,1,0:T(8,128)(2,1)S(1)}, u32[]{:S(2)}, u32[]{:S(2)}) async-start(bf16[8,5,4,32,128]{4,3,2,1,0:T(8,128)(2,1)} %spread_kernel.1), calls=%async_computation | async-start | bytes 2621440 | tf_op jit(solution)/shard_map/all_to_all | solution.py:373
  7.7 5.4 %collective-permute-start = (bf16[14,32,256]{2,1,0:T(8,128)(2,1)S(1)}, bf16[14,32,256]{2,1,0:T(8,128)(2,1)S(1)}, u32[]{:S(2)}, u32[]{:S(2)}) collective-permute-start(bf16[14,32,256]{2,1,0:T(8,128)(2,1)S(1)} %constant_dynamic-slice_fusion), channel_id=1, source_target_pairs={{20,0},{21,1},{22,2},{23,3},{16,4},{17,5},{18,6},{19,7},{28,8},{29... | collective-permute-start | bytes 688136 | tf_op jit(solution)/shard_map/ppermute | solution.py:362
  13.1 0.0 copy-done.2
  13.2 0.1 copy.18
  13.3 0.8 %pad_maximum_fusion = bf16[28,32,256]{2,1,0:T(8,128)(2,1)} fusion(bf16[1,32,256]{2,1,0:T(8,128)(2,1)S(1)} %pad_bitcast_fusion, bf16[27,32,256]{2,1,0:T(8,128)(2,1)S(1)} %bitcast.21), kind=kLoop, calls=%fused_computation | loop fusion | flops 229376 | bytes 917504 | tf_op jit(solution)/shard_map/concatenate | solution.py:368
  14.1 1.9 %collective-permute-start.2 = (bf16[28,32,256]{2,1,0:T(8,128)(2,1)}, bf16[28,32,256]{2,1,0:T(8,128)(2,1)S(1)}, u32[]{:S(2)}, u32[]{:S(2)}) collective-permute-start(bf16[28,32,256]{2,1,0:T(8,128)(2,1)} %pad_maximum_fusion), channel_id=1, source_target_pairs={{20,0},{21,1},{22,2},{23,3},{16,4},{17,5},{18,6},{19,7},{28,8},{29... | collective-permute-start | bytes 1376264 | tf_op jit(solution)/shard_map/ppermute | solution.py:369
  16.0 3.1 %collective-permute-done.fetched = bf16[14,32,256]{2,1,0:T(8,128)(2,1)S(1)} collective-permute-done((bf16[14,32,256]{2,1,0:T(8,128)(2,1)S(1)}, bf16[14,32,256]{2,1,0:T(8,128)(2,1)S(1)}, u32[]{:S(2)}, u32[]{:S(2)}) %collective-permute-start) | collective-permute-done | bytes 229408 | tf_op jit(solution)/shard_map/ppermute | solution.py:362
  19.1 1.9 %collective-permute-start.1 = (bf16[14,32,256]{2,1,0:T(8,128)(2,1)S(1)}, bf16[14,32,256]{2,1,0:T(8,128)(2,1)S(1)}, u32[]{:S(2)}, u32[]{:S(2)}) collective-permute-start(bf16[14,32,256]{2,1,0:T(8,128)(2,1)S(1)} %collective-permute-done.fetched), channel_id=1, source_target_pairs={{0,8},{8,0},{16,24},{24,16},{32,40},{40,32},{48,56},{56,48},{64,72... | collective-permute-start | bytes 688136 | tf_op jit(solution)/shard_map/ppermute | solution.py:365
  21.1 1.5 %collective-permute-done.1.swapped = bf16[14,32,256]{2,1,0:T(8,128)(2,1)S(1)} collective-permute-done((bf16[14,32,256]{2,1,0:T(8,128)(2,1)S(1)}, bf16[14,32,256]{2,1,0:T(8,128)(2,1)S(1)}, u32[]{:S(2)}, u32[]{:S(2)}) %collective-permute-start.1) | collective-permute-done | bytes 229408 | tf_op jit(solution)/shard_map/ppermute | solution.py:365
  22.5 3.7 %all-to-all-done.planes.v_ref = bf16[8,5,4,32,128]{4,3,2,1,0:T(8,128)(2,1)S(1)} async-done(((bf16[8,5,4,32,128]{4,3,2,1,0:T(8,128)(2,1)}), bf16[8,5,4,32,128]{4,3,2,1,0:T(8,128)(2,1)S(1)}, u32[]{:S(2)}, u32[]{:S(2)}) %all-to-all-start) | async-done | bytes 1310752 | tf_op jit(solution)/shard_map/all_to_all | solution.py:373
  26.2 0.6 first_edge_kernel.1
  26.8 4.8 %collective-permute-start.3 = (f32[2,4,32,128]{3,2,1,0:T(8,128)S(1)}, f32[2,4,32,128]{3,2,1,0:T(8,128)S(1)}, u32[]{:S(2)}, u32[]{:S(2)}) collective-permute-start(f32[2,4,32,128]{3,2,1,0:T(8,128)S(1)} %get-tuple-element.17), channel_id=1, source_target_pairs={{8,4},{9,5},{10,6},{11,7},{16,12},{17,13},{18,14},{19,15},{24,20},... | collective-permute-start | bytes 393224 | tf_op jit(solution)/shard_map/ppermute | solution.py:382
  31.6 0.0 collective-permute-done.2.parcel.w_ref.other
  31.6 3.5 %first_kernel.1 = (bf16[4,2,4,4,32,128]{5,4,3,2,1,0:T(8,128)(2,1)S(1)}, f32[2,2,4,32,128]{4,3,2,1,0:T(8,128)S(1)}, f32[32,128]{1,0:T(8,128)S(1)}) custom-call(bf16[8,5,4,32,128]{4,3,2,1,0:T(8,128)(2,1)S(1)} %all-to-all-done.planes.v_ref, bf16[3,3,3,32,256]{4,3,2,1,0:T(8,128)(2,1)S(1)} %copy-done.1, bf16[27,32,256]{2,1,0:T(8,128)(2,1)S(1)} %get-tuple-element.15.other, ...), custom_call_target="tpu_custom_call" | custom-call | tf_op jit(solution)/shard_map/first_kernel/pallas_call | solution.py:383
  35.2 1.2 %collective-permute-done.3.outer = f32[2,4,32,128]{3,2,1,0:T(8,128)S(1)} collective-permute-done((f32[2,4,32,128]{3,2,1,0:T(8,128)S(1)}, f32[2,4,32,128]{3,2,1,0:T(8,128)S(1)}, u32[]{:S(2)}, u32[]{:S(2)}) %collective-permute-start.3) | collective-permute-done | bytes 131104 | tf_op jit(solution)/shard_map/ppermute | solution.py:382
  36.4 0.5 first_ends_kernel.1
  36.9 14.5 %all_to_all.10.planes = bf16[4,2,4,4,32,128]{5,4,3,2,1,0:T(8,128)(2,1)S(1)} all-to-all(bf16[4,2,4,4,32,128]{5,4,3,2,1,0:T(8,128)(2,1)S(1)} %first_ends_kernel.1), channel_id=1, replica_groups={{0,1,2,3},{4,5,6,7},{8,9,10,11},{12,13,14,15},{16,17,18,19},{20,21,22,2..., dimensions={0} | all-to-all | bytes 2097152 | tf_op jit(solution)/shard_map/all_to_all | solution.py:400
  51.4 0.5 second_edge_kernel.1
  52.0 7.1 %collective-permute-start.4 = (f32[2,4,32,128]{3,2,1,0:T(8,128)S(1)}, f32[2,4,32,128]{3,2,1,0:T(8,128)S(1)}, u32[]{:S(2)}, u32[]{:S(2)}) collective-permute-start(f32[2,4,32,128]{3,2,1,0:T(8,128)S(1)} %second_edge_kernel.1), channel_id=1, source_target_pairs={{8,4},{9,5},{10,6},{11,7},{16,12},{17,13},{18,14},{19,15},{24,20},... | collective-permute-start | bytes 393224 | tf_op jit(solution)/shard_map/ppermute | solution.py:405
  59.0 1.3 %second_other_kernel.1 = (bf16[5,4,32,128]{3,2,1,0:T(8,128)(2,1)S(1)}, f32[2,4,32,128]{3,2,1,0:T(8,128)S(1)}) custom-call(bf16[4,2,4,4,32,128]{5,4,3,2,1,0:T(8,128)(2,1)S(1)} %all_to_all.10.planes, bf16[28,32,256]{2,1,0:T(8,128)(2,1)S(1)} %collective-permute-done.2.parcel.w_ref.other, f32[32,128]{1,0:T(8,128)S(1)} %get-tuple-element.21.bias, ...), custom_call_target="tpu_custom_call" | custom-call | tf_op jit(solution)/shard_map/second_other_kernel/pallas_call | solution.py:407
  60.4 1.3 %collective-permute-done.4.outer = f32[2,4,32,128]{3,2,1,0:T(8,128)S(1)} collective-permute-done((f32[2,4,32,128]{3,2,1,0:T(8,128)S(1)}, f32[2,4,32,128]{3,2,1,0:T(8,128)S(1)}, u32[]{:S(2)}, u32[]{:S(2)}) %collective-permute-start.4) | collective-permute-done | bytes 131104 | tf_op jit(solution)/shard_map/ppermute | solution.py:405
  61.7 1.9 %collective-permute-start.5 = (bf16[5,4,32,128]{3,2,1,0:T(8,128)(2,1)S(1)}, bf16[5,4,32,128]{3,2,1,0:T(8,128)(2,1)S(1)}, u32[]{:S(2)}, u32[]{:S(2)}) collective-permute-start(bf16[5,4,32,128]{3,2,1,0:T(8,128)(2,1)S(1)} %finish_kernel.1), channel_id=1, source_target_pairs={{0,4},{1,5},{2,6},{3,7},{8,12},{9,13},{10,14},{11,15},{16,20},{17,... | collective-permute-start | bytes 491528 | tf_op jit(solution)/shard_map/ppermute | solution.py:413
  63.6 2.0 %second_own_kernel.1 = (bf16[32,8,4,128]{3,2,1,0:T(4,128)(2,1)}, f32[2,4,32,128]{3,2,1,0:T(8,128)S(1)}, f32[4,32,128]{2,1,0:T(8,128)S(1)}) custom-call(bf16[4,2,4,4,32,128]{5,4,3,2,1,0:T(8,128)(2,1)S(1)} %all_to_all.10.planes, bf16[3,3,3,32,256]{4,3,2,1,0:T(8,128)(2,1)S(1)} %copy-done, f32[1,32]{1,0:T(1,128)S(1)} %bitcast.26, ...), custom_call_target="tpu_custom_call" | custom-call | tf_op jit(solution)/shard_map/second_own_kernel/pallas_call | solution.py:414
  65.6 0.7 outer_end_kernel.1._
  66.3 2.6 %collective-permute-done.5.received = bf16[5,4,32,128]{3,2,1,0:T(8,128)(2,1)S(1)} collective-permute-done((bf16[5,4,32,128]{3,2,1,0:T(8,128)(2,1)S(1)}, bf16[5,4,32,128]{3,2,1,0:T(8,128)(2,1)S(1)}, u32[]{:S(2)}, u32[]{:S(2)}) %collective-permute-start.5) | collective-permute-done | bytes 163872 | tf_op jit(solution)/shard_map/ppermute | solution.py:413
  68.9 1.0 %last_kernel.1 = bf16[32,8,4,128]{3,2,1,0:T(4,128)(2,1)} custom-call(f32[2,4,32,128]{3,2,1,0:T(8,128)S(1)} %get-tuple-element.19.ends, f32[4,32,128]{2,1,0:T(8,128)S(1)} %get-tuple-element.20.inner_own, bf16[5,4,32,128]{3,2,1,0:T(8,128)(2,1)S(1)} %collective-permute-done.5.received, ...), custom_call_target="tpu_custom_call", output_to_operand_aliasing={{}: (4, {})} | custom-call | tf_op jit(solution)/shard_map/last_kernel/pallas_call | solution.py:429
  (8 shorter events, 0.1 us)
Async XLA Ops:
  2.2 5.5 %copy-start.1 = (bf16[3,3,3,32,256]{4,3,2,1,0:T(8,128)(2,1)S(1)}, bf16[3,3,3,32,256]{4,3,2,1,0:T(8,128)(2,1)}, u32[]{:S(2)}) copy-start(bf16[3,3,3,32,256]{4,3,2,1,0:T(8,128)(2,1)} %own.4) | copy-start | bytes 1327108
  2.2 10.9 %copy-start.2 = (f32[32]{0:T(128)S(1)}, f32[32]{0:T(128)}, u32[]{:S(2)}) copy-start(f32[32]{0:T(128)} %param.7) | copy-start | bytes 388
  2.2 10.9 %copy-start.3 = (f32[32]{0:T(128)S(1)}, f32[32]{0:T(128)}, u32[]{:S(2)}) copy-start(f32[32]{0:T(128)} %param.9) | copy-start | bytes 388
  2.2 11.1 %copy-start = (bf16[3,3,3,32,256]{4,3,2,1,0:T(8,128)(2,1)S(1)}, bf16[3,3,3,32,256]{4,3,2,1,0:T(8,128)(2,1)}, u32[]{:S(2)}) copy-start(bf16[3,3,3,32,256]{4,3,2,1,0:T(8,128)(2,1)} %own.5) | copy-start | bytes 1327108
  2.3 24.0 %all-to-all-start = ((bf16[8,5,4,32,128]{4,3,2,1,0:T(8,128)(2,1)}), bf16[8,5,4,32,128]{4,3,2,1,0:T(8,128)(2,1)S(1)}, u32[]{:S(2)}, u32[]{:S(2)}) async-start(bf16[8,5,4,32,128]{4,3,2,1,0:T(8,128)(2,1)} %spread_kernel.1), calls=%async_computation | async-start | bytes 2621440 | tf_op jit(solution)/shard_map/all_to_all | solution.py:373
  7.7 11.4 %collective-permute-start = (bf16[14,32,256]{2,1,0:T(8,128)(2,1)S(1)}, bf16[14,32,256]{2,1,0:T(8,128)(2,1)S(1)}, u32[]{:S(2)}, u32[]{:S(2)}) collective-permute-start(bf16[14,32,256]{2,1,0:T(8,128)(2,1)S(1)} %constant_dynamic-slice_fusion), channel_id=1, source_target_pairs={{20,0},{21,1},{22,2},{23,3},{16,4},{17,5},{18,6},{19,7},{28,8},{29... | collective-permute-start | bytes 688136 | tf_op jit(solution)/shard_map/ppermute | solution.py:362
  14.1 17.5 %collective-permute-start.2 = (bf16[28,32,256]{2,1,0:T(8,128)(2,1)}, bf16[28,32,256]{2,1,0:T(8,128)(2,1)S(1)}, u32[]{:S(2)}, u32[]{:S(2)}) collective-permute-start(bf16[28,32,256]{2,1,0:T(8,128)(2,1)} %pad_maximum_fusion), channel_id=1, source_target_pairs={{20,0},{21,1},{22,2},{23,3},{16,4},{17,5},{18,6},{19,7},{28,8},{29... | collective-permute-start | bytes 1376264 | tf_op jit(solution)/shard_map/ppermute | solution.py:369
  19.1 3.4 %collective-permute-start.1 = (bf16[14,32,256]{2,1,0:T(8,128)(2,1)S(1)}, bf16[14,32,256]{2,1,0:T(8,128)(2,1)S(1)}, u32[]{:S(2)}, u32[]{:S(2)}) collective-permute-start(bf16[14,32,256]{2,1,0:T(8,128)(2,1)S(1)} %collective-permute-done.fetched), channel_id=1, source_target_pairs={{0,8},{8,0},{16,24},{24,16},{32,40},{40,32},{48,56},{56,48},{64,72... | collective-permute-start | bytes 688136 | tf_op jit(solution)/shard_map/ppermute | solution.py:365
  26.8 9.6 %collective-permute-start.3 = (f32[2,4,32,128]{3,2,1,0:T(8,128)S(1)}, f32[2,4,32,128]{3,2,1,0:T(8,128)S(1)}, u32[]{:S(2)}, u32[]{:S(2)}) collective-permute-start(f32[2,4,32,128]{3,2,1,0:T(8,128)S(1)} %get-tuple-element.17), channel_id=1, source_target_pairs={{8,4},{9,5},{10,6},{11,7},{16,12},{17,13},{18,14},{19,15},{24,20},... | collective-permute-start | bytes 393224 | tf_op jit(solution)/shard_map/ppermute | solution.py:382
  52.0 9.7 %collective-permute-start.4 = (f32[2,4,32,128]{3,2,1,0:T(8,128)S(1)}, f32[2,4,32,128]{3,2,1,0:T(8,128)S(1)}, u32[]{:S(2)}, u32[]{:S(2)}) collective-permute-start(f32[2,4,32,128]{3,2,1,0:T(8,128)S(1)} %second_edge_kernel.1), channel_id=1, source_target_pairs={{8,4},{9,5},{10,6},{11,7},{16,12},{17,13},{18,14},{19,15},{24,20},... | collective-permute-start | bytes 393224 | tf_op jit(solution)/shard_map/ppermute | solution.py:405
  61.7 7.2 %collective-permute-start.5 = (bf16[5,4,32,128]{3,2,1,0:T(8,128)(2,1)S(1)}, bf16[5,4,32,128]{3,2,1,0:T(8,128)(2,1)S(1)}, u32[]{:S(2)}, u32[]{:S(2)}) collective-permute-start(bf16[5,4,32,128]{3,2,1,0:T(8,128)(2,1)S(1)} %finish_kernel.1), channel_id=1, source_target_pairs={{0,4},{1,5},{2,6},{3,7},{8,12},{9,13},{10,14},{11,15},{16,20},{17,... | collective-permute-start | bytes 491528 | tf_op jit(solution)/shard_map/ppermute | solution.py:413

commit v5 on v4

--- a/solution.py
+++ b/solution.py
@@ -142,7 +142,7 @@
     half = half_index()
     for j, w_ref in enumerate((own, other)):
         for z, v in enumerate(edge(planes, w_ref, (planes.shape[-4] - 1) * half, 2 - 2 * half)):
-            outer[j, z] = v
+            outer[j, z] = v.astype(BF16)
 
 
 def first_kernel(planes, own, other, parcel, b_ref, out, ends, other_bias, hidden, sems):
@@ -177,7 +177,7 @@
     half = half_index()
     copies = []
     for j, slot in enumerate((half, 1 - half)):
-        hidden[j] = gelu(ends[half, j] + outer[1 - j]).astype(BF16)
+        hidden[j] = gelu(ends[half, j] + outer[1 - j].astype(F32)).astype(BF16)
         for d in range(n):
             c = pltpu.make_async_copy(hidden.at[j], out.at[d, slot, (ny - 1) * half], sems.at[j, d])
             c.start()
@@ -199,7 +199,7 @@
 def second_edge_kernel(planes, own, other, outer):
     for j, w_ref in enumerate((own, other)):
         for z, v in enumerate(edge(planes, w_ref, *outer_edge(planes))):
-            outer[j, z] = v
+            outer[j, z] = v.astype(BF16)
 
 
 def channels_first(values):
@@ -233,7 +233,7 @@
 
 
 def finish_kernel(ends, outer, _, sent):
-    sent[2] = (ends[0] + outer[0]).astype(BF16)
+    sent[2] = (ends[0] + outer[0].astype(F32)).astype(BF16)
 
 
 def second_own_kernel(planes, w_ref, b_ref, v_ref, out, ends, inner_own, mine, sem):
@@ -259,7 +259,7 @@
 
 def outer_end_kernel(ends, outer, _, out, plane, sem):
     ny, half = out.shape[1] // 2, half_index()
-    plane[...] = channels_first([ends[0, z] + outer[1, z] for z in range(ends.shape[1])])
+    plane[...] = channels_first([ends[0, z] + outer[1, z].astype(F32) for z in range(ends.shape[1])])
     copy = pltpu.make_async_copy(plane, out.at[:, half * ny + (ny - 1) * half], sem)
     copy.start()
     copy.wait()
@@ -374,7 +374,7 @@
 
     outer, other_first = call(
         first_edge_kernel,
-        (f32(2), jax.ShapeDtypeStruct(weight.shape, BF16)),
+        (bf16(2), jax.ShapeDtypeStruct(weight.shape, BF16)),
         [VMEM] * 4,
         (VMEM,) * 2,
         [],
@@ -399,7 +399,7 @@
     groups = [list(range(g)), list(range(g, n))]
     gathered = lax.all_to_all(hidden, "ch", 0, 0, tiled=True, axis_index_groups=groups)
 
-    outer = call(second_edge_kernel, f32(2), [VMEM] * 3, VMEM, [])(
+    outer = call(second_edge_kernel, bf16(2), [VMEM] * 3, VMEM, [])(
         gathered, second_weight, other_second
     )
     outer = lax.ppermute(outer, axes, to_across)

time: 70.2 us -> 69.5 us (0.990)
  waiting for transfers between devices: 13.4 us -> 12 us
    ppermute x2, waiting for transfers between devices: 2.51 us -> 1.11 us  [per_device(): outer = lax.ppermute(outer, axes, to_across)]
    all_to_all x1, blocking collectives: 14.5 us -> 15.2 us  [per_device(): lax.all_to_all(hidden, 'ch', 0, 0, tiled=True, axis_index_groups=groups)]
where the time goes in v5:
time: 69.5 us; the launch traced here: 69.2 us
  starting transfers between devices  28.5 us (41%)
  blocking collectives  15.2 us (22%)
  waiting for transfers between devices  12 us (17%)
  Pallas kernels  11.2 us (16%)
  local copies, waits for them, and re-layouts  1.25 us (2%)
  other arithmetic  0.82 us (1%)
    all_to_all x1, blocking collectives, per_device(): lax.all_to_all(hidden, 'ch', 0, 0, tiled=True, axis_index_groups=groups)  15.2 us
    ppermute x2, starting transfers between devices, per_device(): outer = lax.ppermute(outer, axes, to_across)  11.9 us
    all_to_all x1, starting transfers between devices, per_device(): main = lax.all_to_all(sent, 'ch', 0, 0, tiled=True)  5.46 us
    ppermute x1, starting transfers between devices, per_device(): lax.ppermute(lax.dynamic_slice_in_dim(weight, (taps - part) * core, part,...  5.36 us
    all_to_all x1, waiting for transfers between devices, per_device(): main = lax.all_to_all(sent, 'ch', 0, 0, tiled=True)  3.7 us
    pallas_call x1, Pallas kernels, per_device(): call(first_kernel, (bf16(g, 2, ny), f32(2, 2), jax.ShapeDtypeStruct((co,...  3.54 us
    ppermute x1, waiting for transfers between devices, per_device(): lax.ppermute(lax.dynamic_slice_in_dim(weight, (taps - part) * core, part,...  3.12 us
    ppermute x1, waiting for transfers between devices, per_device(): received = lax.ppermute(sent, axes, to_partner)  2.59 us
  transfers between devices with their start and end apart: 7, of which 6 were waited for; matrix products, arithmetic and copies ran while one was open for 1% of the time, Pallas kernels for 12%

profile of v5, /device:TPU:384, one launch (start us, length us, event | category | flops | bytes accessed | tf_op | source)
XLA Modules:
  0.0 69.2 jit_solution(6335141506848202345)
XLA Ops:
  0.0 1.1 %copy.20 = bf16[32,8,4,128]{3,0,2,1:T(8,128)(2,1)S(1)} copy(bf16[32,8,4,128]{3,2,1,0:T(4,128)(2,1)} %param.5) | data formatting | bytes 524288 | tf_op args[0]
  1.1 1.1 %spread_kernel.1 = bf16[8,5,4,32,128]{4,3,2,1,0:T(8,128)(2,1)} custom-call(bf16[8,4,32,128]{3,2,1,0:T(8,128)(2,1)S(1)} %bitcast.23), custom_call_target="tpu_custom_call" | custom-call | tf_op jit(solution)/shard_map/spread_kernel/pallas_call | solution.py:372
  2.2 0.0 copy-start.1
  2.2 0.0 copy-start.2
  2.2 0.0 copy-start.3
  2.2 0.0 copy-start
  2.3 5.5 %all-to-all-start = ((bf16[8,5,4,32,128]{4,3,2,1,0:T(8,128)(2,1)}), bf16[8,5,4,32,128]{4,3,2,1,0:T(8,128)(2,1)S(1)}, u32[]{:S(2)}, u32[]{:S(2)}) async-start(bf16[8,5,4,32,128]{4,3,2,1,0:T(8,128)(2,1)} %spread_kernel.1), calls=%async_computation | async-start | bytes 2621440 | tf_op jit(solution)/shard_map/all_to_all | solution.py:373
  7.7 5.4 %collective-permute-start = (bf16[14,32,256]{2,1,0:T(8,128)(2,1)S(1)}, bf16[14,32,256]{2,1,0:T(8,128)(2,1)S(1)}, u32[]{:S(2)}, u32[]{:S(2)}) collective-permute-start(bf16[14,32,256]{2,1,0:T(8,128)(2,1)S(1)} %constant_dynamic-slice_fusion), channel_id=1, source_target_pairs={{20,0},{21,1},{22,2},{23,3},{16,4},{17,5},{18,6},{19,7},{28,8},{29... | collective-permute-start | bytes 688136 | tf_op jit(solution)/shard_map/ppermute | solution.py:362
  13.2 0.1 copy.18
  13.3 0.0 copy-done
  13.3 0.8 %pad_maximum_fusion = bf16[28,32,256]{2,1,0:T(8,128)(2,1)} fusion(bf16[1,32,256]{2,1,0:T(8,128)(2,1)S(1)} %pad_bitcast_fusion, bf16[27,32,256]{2,1,0:T(8,128)(2,1)S(1)} %bitcast.21), kind=kLoop, calls=%fused_computation | loop fusion | flops 229376 | bytes 917504 | tf_op jit(solution)/shard_map/concatenate | solution.py:368
  14.1 1.9 %collective-permute-start.2 = (bf16[28,32,256]{2,1,0:T(8,128)(2,1)}, bf16[28,32,256]{2,1,0:T(8,128)(2,1)S(1)}, u32[]{:S(2)}, u32[]{:S(2)}) collective-permute-start(bf16[28,32,256]{2,1,0:T(8,128)(2,1)} %pad_maximum_fusion), channel_id=1, source_target_pairs={{20,0},{21,1},{22,2},{23,3},{16,4},{17,5},{18,6},{19,7},{28,8},{29... | collective-permute-start | bytes 1376264 | tf_op jit(solution)/shard_map/ppermute | solution.py:369
  16.0 3.1 %collective-permute-done.fetched = bf16[14,32,256]{2,1,0:T(8,128)(2,1)S(1)} collective-permute-done((bf16[14,32,256]{2,1,0:T(8,128)(2,1)S(1)}, bf16[14,32,256]{2,1,0:T(8,128)(2,1)S(1)}, u32[]{:S(2)}, u32[]{:S(2)}) %collective-permute-start) | collective-permute-done | bytes 229408 | tf_op jit(solution)/shard_map/ppermute | solution.py:362
  19.1 1.9 %collective-permute-start.1 = (bf16[14,32,256]{2,1,0:T(8,128)(2,1)S(1)}, bf16[14,32,256]{2,1,0:T(8,128)(2,1)S(1)}, u32[]{:S(2)}, u32[]{:S(2)}) collective-permute-start(bf16[14,32,256]{2,1,0:T(8,128)(2,1)S(1)} %collective-permute-done.fetched), channel_id=1, source_target_pairs={{0,8},{8,0},{16,24},{24,16},{32,40},{40,32},{48,56},{56,48},{64,72... | collective-permute-start | bytes 688136 | tf_op jit(solution)/shard_map/ppermute | solution.py:365
  21.1 1.5 %collective-permute-done.1.swapped = bf16[14,32,256]{2,1,0:T(8,128)(2,1)S(1)} collective-permute-done((bf16[14,32,256]{2,1,0:T(8,128)(2,1)S(1)}, bf16[14,32,256]{2,1,0:T(8,128)(2,1)S(1)}, u32[]{:S(2)}, u32[]{:S(2)}) %collective-permute-start.1) | collective-permute-done | bytes 229408 | tf_op jit(solution)/shard_map/ppermute | solution.py:365
  22.5 3.7 %all-to-all-done.planes.v_ref = bf16[8,5,4,32,128]{4,3,2,1,0:T(8,128)(2,1)S(1)} async-done(((bf16[8,5,4,32,128]{4,3,2,1,0:T(8,128)(2,1)}), bf16[8,5,4,32,128]{4,3,2,1,0:T(8,128)(2,1)S(1)}, u32[]{:S(2)}, u32[]{:S(2)}) %all-to-all-start) | async-done | bytes 1310752 | tf_op jit(solution)/shard_map/all_to_all | solution.py:373
  26.2 0.6 first_edge_kernel.1
  26.8 4.8 %collective-permute-start.3 = (bf16[2,4,32,128]{3,2,1,0:T(8,128)(2,1)S(1)}, bf16[2,4,32,128]{3,2,1,0:T(8,128)(2,1)S(1)}, u32[]{:S(2)}, u32[]{:S(2)}) collective-permute-start(bf16[2,4,32,128]{3,2,1,0:T(8,128)(2,1)S(1)} %get-tuple-element.17), channel_id=1, source_target_pairs={{8,4},{9,5},{10,6},{11,7},{16,12},{17,13},{18,14},{19,15},{24,20},... | collective-permute-start | bytes 196616 | tf_op jit(solution)/shard_map/ppermute | solution.py:382
  31.6 0.0 collective-permute-done.2.parcel.w_ref.other
  31.6 3.5 %first_kernel.1 = (bf16[4,2,4,4,32,128]{5,4,3,2,1,0:T(8,128)(2,1)S(1)}, f32[2,2,4,32,128]{4,3,2,1,0:T(8,128)S(1)}, f32[32,128]{1,0:T(8,128)S(1)}) custom-call(bf16[8,5,4,32,128]{4,3,2,1,0:T(8,128)(2,1)S(1)} %all-to-all-done.planes.v_ref, bf16[3,3,3,32,256]{4,3,2,1,0:T(8,128)(2,1)S(1)} %copy-done.1, bf16[27,32,256]{2,1,0:T(8,128)(2,1)S(1)} %get-tuple-element.15.other, ...), custom_call_target="tpu_custom_call" | custom-call | tf_op jit(solution)/shard_map/first_kernel/pallas_call | solution.py:383
  35.2 0.5 collective-permute-done.3.outer
  35.7 0.5 first_ends_kernel.1
  36.2 15.2 %all_to_all.10.planes = bf16[4,2,4,4,32,128]{5,4,3,2,1,0:T(8,128)(2,1)S(1)} all-to-all(bf16[4,2,4,4,32,128]{5,4,3,2,1,0:T(8,128)(2,1)S(1)} %first_ends_kernel.1), channel_id=1, replica_groups={{0,1,2,3},{4,5,6,7},{8,9,10,11},{12,13,14,15},{16,17,18,19},{20,21,22,2..., dimensions={0} | all-to-all | bytes 2097152 | tf_op jit(solution)/shard_map/all_to_all | solution.py:400
  51.4 0.5 second_edge_kernel.1
  52.0 7.1 %collective-permute-start.4 = (bf16[2,4,32,128]{3,2,1,0:T(8,128)(2,1)S(1)}, bf16[2,4,32,128]{3,2,1,0:T(8,128)(2,1)S(1)}, u32[]{:S(2)}, u32[]{:S(2)}) collective-permute-start(bf16[2,4,32,128]{3,2,1,0:T(8,128)(2,1)S(1)} %second_edge_kernel.1), channel_id=1, source_target_pairs={{8,4},{9,5},{10,6},{11,7},{16,12},{17,13},{18,14},{19,15},{24,20},... | collective-permute-start | bytes 196616 | tf_op jit(solution)/shard_map/ppermute | solution.py:405
  59.0 1.3 %second_other_kernel.1 = (bf16[5,4,32,128]{3,2,1,0:T(8,128)(2,1)S(1)}, f32[2,4,32,128]{3,2,1,0:T(8,128)S(1)}) custom-call(bf16[4,2,4,4,32,128]{5,4,3,2,1,0:T(8,128)(2,1)S(1)} %all_to_all.10.planes, bf16[28,32,256]{2,1,0:T(8,128)(2,1)S(1)} %collective-permute-done.2.parcel.w_ref.other, f32[32,128]{1,0:T(8,128)S(1)} %get-tuple-element.21.bias, ...), custom_call_target="tpu_custom_call" | custom-call | tf_op jit(solution)/shard_map/second_other_kernel/pallas_call | solution.py:407
  60.4 0.6 collective-permute-done.4.outer
  61.0 1.9 %collective-permute-start.5 = (bf16[5,4,32,128]{3,2,1,0:T(8,128)(2,1)S(1)}, bf16[5,4,32,128]{3,2,1,0:T(8,128)(2,1)S(1)}, u32[]{:S(2)}, u32[]{:S(2)}) collective-permute-start(bf16[5,4,32,128]{3,2,1,0:T(8,128)(2,1)S(1)} %finish_kernel.1), channel_id=1, source_target_pairs={{0,4},{1,5},{2,6},{3,7},{8,12},{9,13},{10,14},{11,15},{16,20},{17,... | collective-permute-start | bytes 491528 | tf_op jit(solution)/shard_map/ppermute | solution.py:413
  62.9 2.0 %second_own_kernel.1 = (bf16[32,8,4,128]{3,2,1,0:T(4,128)(2,1)}, f32[2,4,32,128]{3,2,1,0:T(8,128)S(1)}, f32[4,32,128]{2,1,0:T(8,128)S(1)}) custom-call(bf16[4,2,4,4,32,128]{5,4,3,2,1,0:T(8,128)(2,1)S(1)} %all_to_all.10.planes, bf16[3,3,3,32,256]{4,3,2,1,0:T(8,128)(2,1)S(1)} %copy-done, f32[1,32]{1,0:T(1,128)S(1)} %bitcast.26, ...), custom_call_target="tpu_custom_call" | custom-call | tf_op jit(solution)/shard_map/second_own_kernel/pallas_call | solution.py:414
  64.9 0.7 %outer_end_kernel.1._ = bf16[32,8,4,128]{3,2,1,0:T(4,128)(2,1)} custom-call(f32[2,4,32,128]{3,2,1,0:T(8,128)S(1)} %get-tuple-element.19.ends, bf16[2,4,32,128]{3,2,1,0:T(8,128)(2,1)S(1)} %collective-permute-done.4.outer, bf16[32,8,4,128]{3,2,1,0:T(4,128)(2,1)} %get-tuple-element.24._), custom_call_target="tpu_custom_call", output_to_operand_aliasing={{}: (2, {})} | custom-call | tf_op jit(solution)/shard_map/outer_end_kernel/pallas_call | solution.py:421
  65.6 2.6 %collective-permute-done.5.received = bf16[5,4,32,128]{3,2,1,0:T(8,128)(2,1)S(1)} collective-permute-done((bf16[5,4,32,128]{3,2,1,0:T(8,128)(2,1)S(1)}, bf16[5,4,32,128]{3,2,1,0:T(8,128)(2,1)S(1)}, u32[]{:S(2)}, u32[]{:S(2)}) %collective-permute-start.5) | collective-permute-done | bytes 163872 | tf_op jit(solution)/shard_map/ppermute | solution.py:413
  68.2 1.0 %last_kernel.1 = bf16[32,8,4,128]{3,2,1,0:T(4,128)(2,1)} custom-call(f32[2,4,32,128]{3,2,1,0:T(8,128)S(1)} %get-tuple-element.19.ends, f32[4,32,128]{2,1,0:T(8,128)S(1)} %get-tuple-element.20.inner_own, bf16[5,4,32,128]{3,2,1,0:T(8,128)(2,1)S(1)} %collective-permute-done.5.received, ...), custom_call_target="tpu_custom_call", output_to_operand_aliasing={{}: (4, {})} | custom-call | tf_op jit(solution)/shard_map/last_kernel/pallas_call | solution.py:429
  (8 shorter events, 0.1 us)
Async XLA Ops:
  2.2 5.5 %copy-start.1 = (bf16[3,3,3,32,256]{4,3,2,1,0:T(8,128)(2,1)S(1)}, bf16[3,3,3,32,256]{4,3,2,1,0:T(8,128)(2,1)}, u32[]{:S(2)}) copy-start(bf16[3,3,3,32,256]{4,3,2,1,0:T(8,128)(2,1)} %own.4) | copy-start | bytes 1327108
  2.2 10.9 %copy-start.2 = (f32[32]{0:T(128)S(1)}, f32[32]{0:T(128)}, u32[]{:S(2)}) copy-start(f32[32]{0:T(128)} %param.7) | copy-start | bytes 388
  2.2 10.9 %copy-start.3 = (f32[32]{0:T(128)S(1)}, f32[32]{0:T(128)}, u32[]{:S(2)}) copy-start(f32[32]{0:T(128)} %param.9) | copy-start | bytes 388
  2.2 11.1 %copy-start = (bf16[3,3,3,32,256]{4,3,2,1,0:T(8,128)(2,1)S(1)}, bf16[3,3,3,32,256]{4,3,2,1,0:T(8,128)(2,1)}, u32[]{:S(2)}) copy-start(bf16[3,3,3,32,256]{4,3,2,1,0:T(8,128)(2,1)} %own.5) | copy-start | bytes 1327108
  2.3 24.0 %all-to-all-start = ((bf16[8,5,4,32,128]{4,3,2,1,0:T(8,128)(2,1)}), bf16[8,5,4,32,128]{4,3,2,1,0:T(8,128)(2,1)S(1)}, u32[]{:S(2)}, u32[]{:S(2)}) async-start(bf16[8,5,4,32,128]{4,3,2,1,0:T(8,128)(2,1)} %spread_kernel.1), calls=%async_computation | async-start | bytes 2621440 | tf_op jit(solution)/shard_map/all_to_all | solution.py:373
  7.7 11.4 %collective-permute-start = (bf16[14,32,256]{2,1,0:T(8,128)(2,1)S(1)}, bf16[14,32,256]{2,1,0:T(8,128)(2,1)S(1)}, u32[]{:S(2)}, u32[]{:S(2)}) collective-permute-start(bf16[14,32,256]{2,1,0:T(8,128)(2,1)S(1)} %constant_dynamic-slice_fusion), channel_id=1, source_target_pairs={{20,0},{21,1},{22,2},{23,3},{16,4},{17,5},{18,6},{19,7},{28,8},{29... | collective-permute-start | bytes 688136 | tf_op jit(solution)/shard_map/ppermute | solution.py:362
  14.1 17.5 %collective-permute-start.2 = (bf16[28,32,256]{2,1,0:T(8,128)(2,1)}, bf16[28,32,256]{2,1,0:T(8,128)(2,1)S(1)}, u32[]{:S(2)}, u32[]{:S(2)}) collective-permute-start(bf16[28,32,256]{2,1,0:T(8,128)(2,1)} %pad_maximum_fusion), channel_id=1, source_target_pairs={{20,0},{21,1},{22,2},{23,3},{16,4},{17,5},{18,6},{19,7},{28,8},{29... | collective-permute-start | bytes 1376264 | tf_op jit(solution)/shard_map/ppermute | solution.py:369
  19.1 3.4 %collective-permute-start.1 = (bf16[14,32,256]{2,1,0:T(8,128)(2,1)S(1)}, bf16[14,32,256]{2,1,0:T(8,128)(2,1)S(1)}, u32[]{:S(2)}, u32[]{:S(2)}) collective-permute-start(bf16[14,32,256]{2,1,0:T(8,128)(2,1)S(1)} %collective-permute-done.fetched), channel_id=1, source_target_pairs={{0,8},{8,0},{16,24},{24,16},{32,40},{40,32},{48,56},{56,48},{64,72... | collective-permute-start | bytes 688136 | tf_op jit(solution)/shard_map/ppermute | solution.py:365
  26.8 8.9 %collective-permute-start.3 = (bf16[2,4,32,128]{3,2,1,0:T(8,128)(2,1)S(1)}, bf16[2,4,32,128]{3,2,1,0:T(8,128)(2,1)S(1)}, u32[]{:S(2)}, u32[]{:S(2)}) collective-permute-start(bf16[2,4,32,128]{3,2,1,0:T(8,128)(2,1)S(1)} %get-tuple-element.17), channel_id=1, source_target_pairs={{8,4},{9,5},{10,6},{11,7},{16,12},{17,13},{18,14},{19,15},{24,20},... | collective-permute-start | bytes 196616 | tf_op jit(solution)/shard_map/ppermute | solution.py:382
  52.0 9.0 %collective-permute-start.4 = (bf16[2,4,32,128]{3,2,1,0:T(8,128)(2,1)S(1)}, bf16[2,4,32,128]{3,2,1,0:T(8,128)(2,1)S(1)}, u32[]{:S(2)}, u32[]{:S(2)}) collective-permute-start(bf16[2,4,32,128]{3,2,1,0:T(8,128)(2,1)S(1)} %second_edge_kernel.1), channel_id=1, source_target_pairs={{8,4},{9,5},{10,6},{11,7},{16,12},{17,13},{18,14},{19,15},{24,20},... | collective-permute-start | bytes 196616 | tf_op jit(solution)/shard_map/ppermute | solution.py:405
  61.0 7.2 %collective-permute-start.5 = (bf16[5,4,32,128]{3,2,1,0:T(8,128)(2,1)S(1)}, bf16[5,4,32,128]{3,2,1,0:T(8,128)(2,1)S(1)}, u32[]{:S(2)}, u32[]{:S(2)}) collective-permute-start(bf16[5,4,32,128]{3,2,1,0:T(8,128)(2,1)S(1)} %finish_kernel.1), channel_id=1, source_target_pairs={{0,4},{1,5},{2,6},{3,7},{8,12},{9,13},{10,14},{11,15},{16,20},{17,... | collective-permute-start | bytes 491528 | tf_op jit(solution)/shard_map/ppermute | solution.py:413

commit v6 on v4

--- a/solution.py
+++ b/solution.py
@@ -210,6 +210,11 @@
     return half_index() if y == 0 else 1 - half_index()
 
 
+def two_parts(v):
+    high = v.astype(BF16)
+    return high, (v - high.astype(F32)).astype(BF16)
+
+
 def second_other_kernel(planes, w_ref, bias, v_ref, sent, ends):
     ny = planes.shape[-4]
     n = planes.shape[0]
@@ -221,19 +226,18 @@
             v = v + bias[...]
             whole = v_ref[partner, y + half, z].astype(F32) + v
             if y == 0 or y == ny - 1:
-                role = ends_role(y, ny)
-                sent[2 + role, z] = v.astype(BF16)
-                ends[role, z] = whole
+                ends[ends_role(y, ny), z] = whole
             else:
                 sent[y - 1, z] = whole.astype(BF16)
 
     conv(half_cells(planes), ny, planes, (w_ref,), take)
     for z, v in enumerate(edge(planes, w_ref, *inner_edge(planes))):
-        sent[4, z] = v.astype(BF16)
+        sent[5, z], sent[6, z] = two_parts(v)
 
 
 def finish_kernel(ends, outer, _, sent):
     sent[2] = (ends[0] + outer[0]).astype(BF16)
+    sent[3], sent[4] = two_parts(ends[1])
 
 
 def second_own_kernel(planes, w_ref, b_ref, v_ref, out, ends, inner_own, mine, sem):
@@ -265,7 +269,7 @@
     copy.wait()
 
 
-def last_kernel(ends, inner_own, received, cells_first, _, out, whole, rest, sems):
+def last_kernel(ends, inner_own, received, _, out, whole, rest, sems):
     nz = ends.shape[1]
     ny, half = out.shape[1] // 2, half_index()
     mine, theirs = half * ny, (1 - half) * ny
@@ -274,13 +278,10 @@
     def got(at, z):
         return received[at, z].astype(F32)
 
-    def start(at, z):
-        return cells_first[at, z].astype(F32)
-
     ends_at = (
-        (mine + inner, lambda z: ends[1, z] + got(4, z)),
+        (mine + inner, lambda z: ends[1, z] + (got(5, z) + got(6, z))),
         (theirs + inner, lambda z: got(2, z)),
-        (theirs + outer, lambda z: start(theirs + outer, z) + (got(3, z) + inner_own[z])),
+        (theirs + outer, lambda z: (got(3, z) + got(4, z)) + inner_own[z]),
     )
     copies = []
     for y in range(ny - 2):
@@ -404,10 +405,10 @@
     )
     outer = lax.ppermute(outer, axes, to_across)
     out_type = jax.ShapeDtypeStruct(volume.shape, BF16)
-    sent, ends = call(second_other_kernel, (bf16(5), f32(2)), [VMEM] * 4, (VMEM, VMEM), [])(
+    sent, ends = call(second_other_kernel, (bf16(7), f32(2)), [VMEM] * 4, (VMEM, VMEM), [])(
         gathered, other_second, other_bias, main
     )
-    sent = call(finish_kernel, bf16(5), [VMEM] * 3, VMEM, [], input_output_aliases={2: 0})(
+    sent = call(finish_kernel, bf16(7), [VMEM] * 3, VMEM, [], input_output_aliases={2: 0})(
         ends, outer, sent
     )
     received = lax.ppermute(sent, axes, to_partner)
@@ -429,11 +430,11 @@
     return call(
         last_kernel,
         out_type,
-        [VMEM] * 4 + [ANY],
+        [VMEM] * 3 + [ANY],
         ANY,
         [pltpu.VMEM((co, ny - 2, nz, nx), BF16), pltpu.VMEM((3, co, nz, nx), BF16), DMA((4,))],
-        input_output_aliases={4: 0},
-    )(ends, inner_own, received, cells_first, out)
+        input_output_aliases={3: 0},
+    )(ends, inner_own, received, out)
 
 
 def solution(mesh):

time: 70.2 us -> 71 us (1.011)
  the two profiles are of different devices: /device:TPU:384 before, /device:TPU:217 now
where the time goes in v6:
time: 71 us; the launch traced here: 70.6 us
  starting transfers between devices  27 us (38%)
  blocking collectives  18 us (25%)
  waiting for transfers between devices  12 us (17%)
  Pallas kernels  11.2 us (16%)
  local copies, waits for them, and re-layouts  1.24 us (2%)
  other arithmetic  0.82 us (1%)
    all_to_all x1, blocking collectives, per_device(): lax.all_to_all(hidden, 'ch', 0, 0, tiled=True, axis_index_groups=groups)  18 us
    ppermute x2, starting transfers between devices, per_device(): outer = lax.ppermute(outer, axes, to_across)  7.48 us
    ppermute x1, starting transfers between devices, per_device(): swapped = lax.ppermute(fetched, 'gy', [(i, i ^ 1) for i in range(length)])  5.82 us
    all_to_all x1, starting transfers between devices, per_device(): main = lax.all_to_all(sent, 'ch', 0, 0, tiled=True)  5.34 us
    ppermute x1, starting transfers between devices, per_device(): other_second = lax.ppermute(parcel, axes, weights_route)  4.56 us
    ppermute x2, waiting for transfers between devices, per_device(): outer = lax.ppermute(outer, axes, to_across)  4.53 us
    pallas_call x1, Pallas kernels, per_device(): call(first_kernel, (bf16(g, 2, ny), f32(2, 2), jax.ShapeDtypeStruct((co,...  3.55 us
    ppermute x1, waiting for transfers between devices, per_device(): received = lax.ppermute(sent, axes, to_partner)  3.41 us
  transfers between devices with their start and end apart: 7, of which 5 were waited for; matrix products, arithmetic and copies ran while one was open for 1% of the time, Pallas kernels for 11%

profile of v6, /device:TPU:217, one launch (start us, length us, event | category | flops | bytes accessed | tf_op | source)
XLA Modules:
  0.0 70.6 jit_solution(10012620608743677133)
XLA Ops:
  0.0 1.1 %copy.20 = bf16[32,8,4,128]{3,0,2,1:T(8,128)(2,1)S(1)} copy(bf16[32,8,4,128]{3,2,1,0:T(4,128)(2,1)} %param.5) | data formatting | bytes 524288 | tf_op args[0]
  1.1 1.1 %spread_kernel.1 = bf16[8,5,4,32,128]{4,3,2,1,0:T(8,128)(2,1)} custom-call(bf16[8,4,32,128]{3,2,1,0:T(8,128)(2,1)S(1)} %bitcast.23), custom_call_target="tpu_custom_call" | custom-call | tf_op jit(solution)/shard_map/spread_kernel/pallas_call | solution.py:373
  2.2 0.0 copy-start.1
  2.2 0.0 copy-start.2
  2.2 0.0 copy-start.3
  2.2 0.0 copy-start
  2.3 5.3 %all-to-all-start = ((bf16[8,5,4,32,128]{4,3,2,1,0:T(8,128)(2,1)}), bf16[8,5,4,32,128]{4,3,2,1,0:T(8,128)(2,1)S(1)}, u32[]{:S(2)}, u32[]{:S(2)}) async-start(bf16[8,5,4,32,128]{4,3,2,1,0:T(8,128)(2,1)} %spread_kernel.1), calls=%async_computation | async-start | bytes 2621440 | tf_op jit(solution)/shard_map/all_to_all | solution.py:374
  7.6 0.0 copy-done.1
  7.6 1.9 %collective-permute-start = (bf16[14,32,256]{2,1,0:T(8,128)(2,1)S(1)}, bf16[14,32,256]{2,1,0:T(8,128)(2,1)S(1)}, u32[]{:S(2)}, u32[]{:S(2)}) collective-permute-start(bf16[14,32,256]{2,1,0:T(8,128)(2,1)S(1)} %constant_dynamic-slice_fusion), channel_id=1, source_target_pairs={{20,0},{21,1},{22,2},{23,3},{16,4},{17,5},{18,6},{19,7},{28,8},{29... | collective-permute-start | bytes 688136 | tf_op jit(solution)/shard_map/ppermute | solution.py:363
  9.6 0.1 copy.18
  9.7 0.8 %pad_maximum_fusion = bf16[28,32,256]{2,1,0:T(8,128)(2,1)} fusion(bf16[1,32,256]{2,1,0:T(8,128)(2,1)S(1)} %pad_bitcast_fusion, bf16[27,32,256]{2,1,0:T(8,128)(2,1)S(1)} %bitcast.21), kind=kLoop, calls=%fused_computation | loop fusion | flops 229376 | bytes 917504 | tf_op jit(solution)/shard_map/concatenate | solution.py:369
  10.5 4.6 %collective-permute-start.2 = (bf16[28,32,256]{2,1,0:T(8,128)(2,1)}, bf16[28,32,256]{2,1,0:T(8,128)(2,1)S(1)}, u32[]{:S(2)}, u32[]{:S(2)}) collective-permute-start(bf16[28,32,256]{2,1,0:T(8,128)(2,1)} %pad_maximum_fusion), channel_id=1, source_target_pairs={{20,0},{21,1},{22,2},{23,3},{16,4},{17,5},{18,6},{19,7},{28,8},{29... | collective-permute-start | bytes 1376264 | tf_op jit(solution)/shard_map/ppermute | solution.py:370
  15.1 1.5 %collective-permute-done.fetched = bf16[14,32,256]{2,1,0:T(8,128)(2,1)S(1)} collective-permute-done((bf16[14,32,256]{2,1,0:T(8,128)(2,1)S(1)}, bf16[14,32,256]{2,1,0:T(8,128)(2,1)S(1)}, u32[]{:S(2)}, u32[]{:S(2)}) %collective-permute-start) | collective-permute-done | bytes 229408 | tf_op jit(solution)/shard_map/ppermute | solution.py:363
  16.6 5.8 %collective-permute-start.1 = (bf16[14,32,256]{2,1,0:T(8,128)(2,1)S(1)}, bf16[14,32,256]{2,1,0:T(8,128)(2,1)S(1)}, u32[]{:S(2)}, u32[]{:S(2)}) collective-permute-start(bf16[14,32,256]{2,1,0:T(8,128)(2,1)S(1)} %collective-permute-done.fetched), channel_id=1, source_target_pairs={{0,8},{8,0},{16,24},{24,16},{32,40},{40,32},{48,56},{56,48},{64,72... | collective-permute-start | bytes 688136 | tf_op jit(solution)/shard_map/ppermute | solution.py:366
  22.4 1.1 %collective-permute-done.1.swapped = bf16[14,32,256]{2,1,0:T(8,128)(2,1)S(1)} collective-permute-done((bf16[14,32,256]{2,1,0:T(8,128)(2,1)S(1)}, bf16[14,32,256]{2,1,0:T(8,128)(2,1)S(1)}, u32[]{:S(2)}, u32[]{:S(2)}) %collective-permute-start.1) | collective-permute-done | bytes 229408 | tf_op jit(solution)/shard_map/ppermute | solution.py:366
  23.5 1.5 %all-to-all-done.planes.v_ref = bf16[8,5,4,32,128]{4,3,2,1,0:T(8,128)(2,1)S(1)} async-done(((bf16[8,5,4,32,128]{4,3,2,1,0:T(8,128)(2,1)}), bf16[8,5,4,32,128]{4,3,2,1,0:T(8,128)(2,1)S(1)}, u32[]{:S(2)}, u32[]{:S(2)}) %all-to-all-start) | async-done | bytes 1310752 | tf_op jit(solution)/shard_map/all_to_all | solution.py:374
  25.0 0.6 first_edge_kernel.1
  25.6 4.9 %collective-permute-start.3 = (f32[2,4,32,128]{3,2,1,0:T(8,128)S(1)}, f32[2,4,32,128]{3,2,1,0:T(8,128)S(1)}, u32[]{:S(2)}, u32[]{:S(2)}) collective-permute-start(f32[2,4,32,128]{3,2,1,0:T(8,128)S(1)} %get-tuple-element.17), channel_id=1, source_target_pairs={{8,4},{9,5},{10,6},{11,7},{16,12},{17,13},{18,14},{19,15},{24,20},... | collective-permute-start | bytes 393224 | tf_op jit(solution)/shard_map/ppermute | solution.py:383
  30.6 0.0 collective-permute-done.2.parcel.w_ref.other
  30.6 3.5 %first_kernel.1 = (bf16[4,2,4,4,32,128]{5,4,3,2,1,0:T(8,128)(2,1)S(1)}, f32[2,2,4,32,128]{4,3,2,1,0:T(8,128)S(1)}, f32[32,128]{1,0:T(8,128)S(1)}) custom-call(bf16[8,5,4,32,128]{4,3,2,1,0:T(8,128)(2,1)S(1)} %all-to-all-done.planes.v_ref, bf16[3,3,3,32,256]{4,3,2,1,0:T(8,128)(2,1)S(1)} %copy-done.1, bf16[27,32,256]{2,1,0:T(8,128)(2,1)S(1)} %get-tuple-element.15.other, ...), custom_call_target="tpu_custom_call" | custom-call | tf_op jit(solution)/shard_map/first_kernel/pallas_call | solution.py:384
  34.1 0.0 collective-permute-done.3.outer
  34.1 0.5 first_ends_kernel.1
  34.6 18.0 %all_to_all.10.planes = bf16[4,2,4,4,32,128]{5,4,3,2,1,0:T(8,128)(2,1)S(1)} all-to-all(bf16[4,2,4,4,32,128]{5,4,3,2,1,0:T(8,128)(2,1)S(1)} %first_ends_kernel.1), channel_id=1, replica_groups={{0,1,2,3},{4,5,6,7},{8,9,10,11},{12,13,14,15},{16,17,18,19},{20,21,22,2..., dimensions={0} | all-to-all | bytes 2097152 | tf_op jit(solution)/shard_map/all_to_all | solution.py:401
  52.6 0.5 second_edge_kernel.1
  53.2 2.5 %collective-permute-start.4 = (f32[2,4,32,128]{3,2,1,0:T(8,128)S(1)}, f32[2,4,32,128]{3,2,1,0:T(8,128)S(1)}, u32[]{:S(2)}, u32[]{:S(2)}) collective-permute-start(f32[2,4,32,128]{3,2,1,0:T(8,128)S(1)} %second_edge_kernel.1), channel_id=1, source_target_pairs={{8,4},{9,5},{10,6},{11,7},{16,12},{17,13},{18,14},{19,15},{24,20},... | collective-permute-start | bytes 393224 | tf_op jit(solution)/shard_map/ppermute | solution.py:406
  55.7 1.3 %second_other_kernel.1 = (bf16[7,4,32,128]{3,2,1,0:T(8,128)(2,1)S(1)}, f32[2,4,32,128]{3,2,1,0:T(8,128)S(1)}) custom-call(bf16[4,2,4,4,32,128]{5,4,3,2,1,0:T(8,128)(2,1)S(1)} %all_to_all.10.planes, bf16[28,32,256]{2,1,0:T(8,128)(2,1)S(1)} %collective-permute-done.2.parcel.w_ref.other, f32[32,128]{1,0:T(8,128)S(1)} %get-tuple-element.21.bias, ...), custom_call_target="tpu_custom_call" | custom-call | tf_op jit(solution)/shard_map/second_other_kernel/pallas_call | solution.py:408
  57.1 4.5 %collective-permute-done.4.outer = f32[2,4,32,128]{3,2,1,0:T(8,128)S(1)} collective-permute-done((f32[2,4,32,128]{3,2,1,0:T(8,128)S(1)}, f32[2,4,32,128]{3,2,1,0:T(8,128)S(1)}, u32[]{:S(2)}, u32[]{:S(2)}) %collective-permute-start.4) | collective-permute-done | bytes 131104 | tf_op jit(solution)/shard_map/ppermute | solution.py:406
  61.6 1.9 %collective-permute-start.5 = (bf16[7,4,32,128]{3,2,1,0:T(8,128)(2,1)S(1)}, bf16[7,4,32,128]{3,2,1,0:T(8,128)(2,1)S(1)}, u32[]{:S(2)}, u32[]{:S(2)}) collective-permute-start(bf16[7,4,32,128]{3,2,1,0:T(8,128)(2,1)S(1)} %finish_kernel.1), channel_id=1, source_target_pairs={{0,4},{1,5},{2,6},{3,7},{8,12},{9,13},{10,14},{11,15},{16,20},{17,... | collective-permute-start | bytes 688136 | tf_op jit(solution)/shard_map/ppermute | solution.py:414
  63.5 2.0 %second_own_kernel.1 = (bf16[32,8,4,128]{3,2,1,0:T(4,128)(2,1)}, f32[2,4,32,128]{3,2,1,0:T(8,128)S(1)}, f32[4,32,128]{2,1,0:T(8,128)S(1)}) custom-call(bf16[4,2,4,4,32,128]{5,4,3,2,1,0:T(8,128)(2,1)S(1)} %all_to_all.10.planes, bf16[3,3,3,32,256]{4,3,2,1,0:T(8,128)(2,1)S(1)} %copy-done, f32[1,32]{1,0:T(1,128)S(1)} %bitcast.25, ...), custom_call_target="tpu_custom_call" | custom-call | tf_op jit(solution)/shard_map/second_own_kernel/pallas_call | solution.py:415
  65.5 0.7 outer_end_kernel.1._
  66.2 3.4 %collective-permute-done.5.received = bf16[7,4,32,128]{3,2,1,0:T(8,128)(2,1)S(1)} collective-permute-done((bf16[7,4,32,128]{3,2,1,0:T(8,128)(2,1)S(1)}, bf16[7,4,32,128]{3,2,1,0:T(8,128)(2,1)S(1)}, u32[]{:S(2)}, u32[]{:S(2)}) %collective-permute-start.5) | collective-permute-done | bytes 229408 | tf_op jit(solution)/shard_map/ppermute | solution.py:414
  69.6 1.0 %last_kernel.1 = bf16[32,8,4,128]{3,2,1,0:T(4,128)(2,1)} custom-call(f32[2,4,32,128]{3,2,1,0:T(8,128)S(1)} %get-tuple-element.19.ends, f32[4,32,128]{2,1,0:T(8,128)S(1)} %get-tuple-element.20.inner_own, bf16[7,4,32,128]{3,2,1,0:T(8,128)(2,1)S(1)} %collective-permute-done.5.received, ...), custom_call_target="tpu_custom_call", output_to_operand_aliasing={{}: (3, {})} | custom-call | tf_op jit(solution)/shard_map/last_kernel/pallas_call | solution.py:430
  (8 shorter events, 0.1 us)
Async XLA Ops:
  2.2 5.4 %copy-start.1 = (bf16[3,3,3,32,256]{4,3,2,1,0:T(8,128)(2,1)S(1)}, bf16[3,3,3,32,256]{4,3,2,1,0:T(8,128)(2,1)}, u32[]{:S(2)}) copy-start(bf16[3,3,3,32,256]{4,3,2,1,0:T(8,128)(2,1)} %own.4) | copy-start | bytes 1327108
  2.2 7.3 %copy-start.2 = (f32[32]{0:T(128)S(1)}, f32[32]{0:T(128)}, u32[]{:S(2)}) copy-start(f32[32]{0:T(128)} %param.7) | copy-start | bytes 388
  2.2 7.3 %copy-start.3 = (f32[32]{0:T(128)S(1)}, f32[32]{0:T(128)}, u32[]{:S(2)}) copy-start(f32[32]{0:T(128)} %param.9) | copy-start | bytes 388
  2.2 7.5 %copy-start = (bf16[3,3,3,32,256]{4,3,2,1,0:T(8,128)(2,1)S(1)}, bf16[3,3,3,32,256]{4,3,2,1,0:T(8,128)(2,1)}, u32[]{:S(2)}) copy-start(bf16[3,3,3,32,256]{4,3,2,1,0:T(8,128)(2,1)} %own.5) | copy-start | bytes 1327108
  2.3 22.8 %all-to-all-start = ((bf16[8,5,4,32,128]{4,3,2,1,0:T(8,128)(2,1)}), bf16[8,5,4,32,128]{4,3,2,1,0:T(8,128)(2,1)S(1)}, u32[]{:S(2)}, u32[]{:S(2)}) async-start(bf16[8,5,4,32,128]{4,3,2,1,0:T(8,128)(2,1)} %spread_kernel.1), calls=%async_computation | async-start | bytes 2621440 | tf_op jit(solution)/shard_map/all_to_all | solution.py:374
  7.6 9.0 %collective-permute-start = (bf16[14,32,256]{2,1,0:T(8,128)(2,1)S(1)}, bf16[14,32,256]{2,1,0:T(8,128)(2,1)S(1)}, u32[]{:S(2)}, u32[]{:S(2)}) collective-permute-start(bf16[14,32,256]{2,1,0:T(8,128)(2,1)S(1)} %constant_dynamic-slice_fusion), channel_id=1, source_target_pairs={{20,0},{21,1},{22,2},{23,3},{16,4},{17,5},{18,6},{19,7},{28,8},{29... | collective-permute-start | bytes 688136 | tf_op jit(solution)/shard_map/ppermute | solution.py:363
  10.5 20.0 %collective-permute-start.2 = (bf16[28,32,256]{2,1,0:T(8,128)(2,1)}, bf16[28,32,256]{2,1,0:T(8,128)(2,1)S(1)}, u32[]{:S(2)}, u32[]{:S(2)}) collective-permute-start(bf16[28,32,256]{2,1,0:T(8,128)(2,1)} %pad_maximum_fusion), channel_id=1, source_target_pairs={{20,0},{21,1},{22,2},{23,3},{16,4},{17,5},{18,6},{19,7},{28,8},{29... | collective-permute-start | bytes 1376264 | tf_op jit(solution)/shard_map/ppermute | solution.py:370
  16.6 6.9 %collective-permute-start.1 = (bf16[14,32,256]{2,1,0:T(8,128)(2,1)S(1)}, bf16[14,32,256]{2,1,0:T(8,128)(2,1)S(1)}, u32[]{:S(2)}, u32[]{:S(2)}) collective-permute-start(bf16[14,32,256]{2,1,0:T(8,128)(2,1)S(1)} %collective-permute-done.fetched), channel_id=1, source_target_pairs={{0,8},{8,0},{16,24},{24,16},{32,40},{40,32},{48,56},{56,48},{64,72... | collective-permute-start | bytes 688136 | tf_op jit(solution)/shard_map/ppermute | solution.py:366
  25.6 8.5 %collective-permute-start.3 = (f32[2,4,32,128]{3,2,1,0:T(8,128)S(1)}, f32[2,4,32,128]{3,2,1,0:T(8,128)S(1)}, u32[]{:S(2)}, u32[]{:S(2)}) collective-permute-start(f32[2,4,32,128]{3,2,1,0:T(8,128)S(1)} %get-tuple-element.17), channel_id=1, source_target_pairs={{8,4},{9,5},{10,6},{11,7},{16,12},{17,13},{18,14},{19,15},{24,20},... | collective-permute-start | bytes 393224 | tf_op jit(solution)/shard_map/ppermute | solution.py:383
  53.2 8.4 %collective-permute-start.4 = (f32[2,4,32,128]{3,2,1,0:T(8,128)S(1)}, f32[2,4,32,128]{3,2,1,0:T(8,128)S(1)}, u32[]{:S(2)}, u32[]{:S(2)}) collective-permute-start(f32[2,4,32,128]{3,2,1,0:T(8,128)S(1)} %second_edge_kernel.1), channel_id=1, source_target_pairs={{8,4},{9,5},{10,6},{11,7},{16,12},{17,13},{18,14},{19,15},{24,20},... | collective-permute-start | bytes 393224 | tf_op jit(solution)/shard_map/ppermute | solution.py:406
  61.6 8.0 %collective-permute-start.5 = (bf16[7,4,32,128]{3,2,1,0:T(8,128)(2,1)S(1)}, bf16[7,4,32,128]{3,2,1,0:T(8,128)(2,1)S(1)}, u32[]{:S(2)}, u32[]{:S(2)}) collective-permute-start(bf16[7,4,32,128]{3,2,1,0:T(8,128)(2,1)S(1)} %finish_kernel.1), channel_id=1, source_target_pairs={{0,4},{1,5},{2,6},{3,7},{8,12},{9,13},{10,14},{11,15},{16,20},{17,... | collective-permute-start | bytes 688136 | tf_op jit(solution)/shard_map/ppermute | solution.py:414

commit v7 on v6

--- a/solution.py
+++ b/solution.py
@@ -215,7 +215,7 @@
     return high, (v - high.astype(F32)).astype(BF16)
 
 
-def second_other_kernel(planes, w_ref, bias, v_ref, sent, ends):
+def second_other_kernel(planes, w_ref, bias, v_ref, _, sent, ends):
     ny = planes.shape[-4]
     n = planes.shape[0]
     half = half_index()
@@ -231,13 +231,13 @@
                 sent[y - 1, z] = whole.astype(BF16)
 
     conv(half_cells(planes), ny, planes, (w_ref,), take)
+    sent[2], sent[3] = two_parts(ends[1])
     for z, v in enumerate(edge(planes, w_ref, *inner_edge(planes))):
-        sent[5, z], sent[6, z] = two_parts(v)
-
-
-def finish_kernel(ends, outer, _, sent):
-    sent[2] = (ends[0] + outer[0]).astype(BF16)
-    sent[3], sent[4] = two_parts(ends[1])
+        sent[4, z], sent[5, z] = two_parts(v)
+
+
+def finish_kernel(ends, outer, sent):
+    sent[...] = (ends[0] + outer[0]).astype(BF16)
 
 
 def second_own_kernel(planes, w_ref, b_ref, v_ref, out, ends, inner_own, mine, sem):
@@ -269,7 +269,7 @@
     copy.wait()
 
 
-def last_kernel(ends, inner_own, received, _, out, whole, rest, sems):
+def last_kernel(ends, inner_own, received, last_plane, _, out, whole, rest, sems):
     nz = ends.shape[1]
     ny, half = out.shape[1] // 2, half_index()
     mine, theirs = half * ny, (1 - half) * ny
@@ -279,9 +279,9 @@
         return received[at, z].astype(F32)
 
     ends_at = (
-        (mine + inner, lambda z: ends[1, z] + (got(5, z) + got(6, z))),
-        (theirs + inner, lambda z: got(2, z)),
-        (theirs + outer, lambda z: (got(3, z) + got(4, z)) + inner_own[z]),
+        (mine + inner, lambda z: ends[1, z] + (got(4, z) + got(5, z))),
+        (theirs + inner, lambda z: last_plane[z].astype(F32)),
+        (theirs + outer, lambda z: (got(2, z) + got(3, z)) + inner_own[z]),
     )
     copies = []
     for y in range(ny - 2):
@@ -400,18 +400,17 @@
     groups = [list(range(g)), list(range(g, n))]
     gathered = lax.all_to_all(hidden, "ch", 0, 0, tiled=True, axis_index_groups=groups)
 
-    outer = call(second_edge_kernel, f32(2), [VMEM] * 3, VMEM, [])(
+    edges = call(second_edge_kernel, f32(2), [VMEM] * 3, VMEM, [])(
         gathered, second_weight, other_second
     )
-    outer = lax.ppermute(outer, axes, to_across)
+    outer = lax.ppermute(edges, axes, to_across)
     out_type = jax.ShapeDtypeStruct(volume.shape, BF16)
-    sent, ends = call(second_other_kernel, (bf16(7), f32(2)), [VMEM] * 4, (VMEM, VMEM), [])(
-        gathered, other_second, other_bias, main
-    )
-    sent = call(finish_kernel, bf16(7), [VMEM] * 3, VMEM, [], input_output_aliases={2: 0})(
-        ends, outer, sent
+    sent, ends = call(second_other_kernel, (bf16(6), f32(2)), [VMEM] * 4 + [ANY], (VMEM, VMEM), [])(
+        gathered, other_second, other_bias, main, edges
     )
     received = lax.ppermute(sent, axes, to_partner)
+    last_plane = call(finish_kernel, bf16(), [VMEM] * 2, VMEM, [], cost_estimate=LONG)(ends, outer)
+    last_plane = lax.ppermute(last_plane, axes, to_partner)
     out, ends, inner_own = call(
         second_own_kernel,
         (out_type, f32(2), f32()),
@@ -430,11 +429,11 @@
     return call(
         last_kernel,
         out_type,
-        [VMEM] * 3 + [ANY],
+        [VMEM] * 4 + [ANY],
         ANY,
         [pltpu.VMEM((co, ny - 2, nz, nx), BF16), pltpu.VMEM((3, co, nz, nx), BF16), DMA((4,))],
-        input_output_aliases={3: 0},
-    )(ends, inner_own, received, out)
+        input_output_aliases={4: 0},
+    )(ends, inner_own, received, last_plane, out)
 
 
 def solution(mesh):

time: 71 us -> 70.3 us (level)
  the two profiles are of different devices: /device:TPU:217 before, /device:TPU:384 now
where the time goes in v7:
time: 70.3 us; the launch traced here: 70 us
  starting transfers between devices  32.4 us (46%)
  blocking collectives  14.5 us (21%)
  Pallas kernels  11.2 us (16%)
  waiting for transfers between devices  9.48 us (13%)
  local copies, waits for them, and re-layouts  1.25 us (2%)
  other arithmetic  0.84 us (1%)
    all_to_all x1, blocking collectives, per_device(): lax.all_to_all(hidden, 'ch', 0, 0, tiled=True, axis_index_groups=groups)  14.5 us
    ppermute x1, starting transfers between devices, per_device(): outer = lax.ppermute(edges, axes, to_across)  7.08 us
    all_to_all x1, starting transfers between devices, per_device(): main = lax.all_to_all(sent, 'ch', 0, 0, tiled=True)  5.46 us
    ppermute x1, starting transfers between devices, per_device(): lax.ppermute(lax.dynamic_slice_in_dim(weight, (taps - part) * core, part,...  5.36 us
    ppermute x1, starting transfers between devices, per_device(): outer = lax.ppermute(outer, axes, to_across)  4.83 us
    ppermute x1, starting transfers between devices, per_device(): last_plane = lax.ppermute(last_plane, axes, to_partner)  3.92 us
    all_to_all x1, waiting for transfers between devices, per_device(): main = lax.all_to_all(sent, 'ch', 0, 0, tiled=True)  3.7 us
    pallas_call x1, Pallas kernels, per_device(): call(first_kernel, (bf16(g, 2, ny), f32(2, 2), jax.ShapeDtypeStruct((co,...  3.54 us
  transfers between devices with their start and end apart: 8, of which 4 were waited for; matrix products, arithmetic and copies ran while one was open for 1% of the time, Pallas kernels for 12%

profile of v7, /device:TPU:384, one launch (start us, length us, event | category | flops | bytes accessed | tf_op | source)
XLA Modules:
  0.0 70.0 jit_solution(10391616147946153547)
XLA Ops:
  0.0 1.1 %copy.19 = bf16[32,8,4,128]{3,0,2,1:T(8,128)(2,1)S(1)} copy(bf16[32,8,4,128]{3,2,1,0:T(4,128)(2,1)} %param.5) | data formatting | bytes 524288 | tf_op args[0]
  1.1 1.2 %spread_kernel.1 = bf16[8,5,4,32,128]{4,3,2,1,0:T(8,128)(2,1)} custom-call(bf16[8,4,32,128]{3,2,1,0:T(8,128)(2,1)S(1)} %bitcast.23), custom_call_target="tpu_custom_call" | custom-call | tf_op jit(solution)/shard_map/spread_kernel/pallas_call | solution.py:373
  2.2 0.0 copy-start.1
  2.2 0.0 copy-start.2
  2.2 0.0 copy-start.3
  2.3 0.0 copy-start
  2.3 5.5 %all-to-all-start = ((bf16[8,5,4,32,128]{4,3,2,1,0:T(8,128)(2,1)}), bf16[8,5,4,32,128]{4,3,2,1,0:T(8,128)(2,1)S(1)}, u32[]{:S(2)}, u32[]{:S(2)}) async-start(bf16[8,5,4,32,128]{4,3,2,1,0:T(8,128)(2,1)} %spread_kernel.1), calls=%async_computation | async-start | bytes 2621440 | tf_op jit(solution)/shard_map/all_to_all | solution.py:374
  7.8 5.4 %collective-permute-start = (bf16[14,32,256]{2,1,0:T(8,128)(2,1)S(1)}, bf16[14,32,256]{2,1,0:T(8,128)(2,1)S(1)}, u32[]{:S(2)}, u32[]{:S(2)}) collective-permute-start(bf16[14,32,256]{2,1,0:T(8,128)(2,1)S(1)} %constant_dynamic-slice_fusion), channel_id=1, source_target_pairs={{20,0},{21,1},{22,2},{23,3},{16,4},{17,5},{18,6},{19,7},{28,8},{29... | collective-permute-start | bytes 688136 | tf_op jit(solution)/shard_map/ppermute | solution.py:363
  13.2 0.1 copy.17
  13.3 0.8 %pad_maximum_fusion = bf16[28,32,256]{2,1,0:T(8,128)(2,1)} fusion(bf16[1,32,256]{2,1,0:T(8,128)(2,1)S(1)} %pad_bitcast_fusion, bf16[27,32,256]{2,1,0:T(8,128)(2,1)S(1)} %bitcast.21), kind=kLoop, calls=%fused_computation | loop fusion | flops 229376 | bytes 917504 | tf_op jit(solution)/shard_map/concatenate | solution.py:369
  14.1 1.9 %collective-permute-start.2 = (bf16[28,32,256]{2,1,0:T(8,128)(2,1)}, bf16[28,32,256]{2,1,0:T(8,128)(2,1)S(1)}, u32[]{:S(2)}, u32[]{:S(2)}) collective-permute-start(bf16[28,32,256]{2,1,0:T(8,128)(2,1)} %pad_maximum_fusion), channel_id=1, source_target_pairs={{20,0},{21,1},{22,2},{23,3},{16,4},{17,5},{18,6},{19,7},{28,8},{29... | collective-permute-start | bytes 1376264 | tf_op jit(solution)/shard_map/ppermute | solution.py:370
  16.1 3.1 %collective-permute-done.fetched = bf16[14,32,256]{2,1,0:T(8,128)(2,1)S(1)} collective-permute-done((bf16[14,32,256]{2,1,0:T(8,128)(2,1)S(1)}, bf16[14,32,256]{2,1,0:T(8,128)(2,1)S(1)}, u32[]{:S(2)}, u32[]{:S(2)}) %collective-permute-start) | collective-permute-done | bytes 229408 | tf_op jit(solution)/shard_map/ppermute | solution.py:363
  19.2 1.9 %collective-permute-start.1 = (bf16[14,32,256]{2,1,0:T(8,128)(2,1)S(1)}, bf16[14,32,256]{2,1,0:T(8,128)(2,1)S(1)}, u32[]{:S(2)}, u32[]{:S(2)}) collective-permute-start(bf16[14,32,256]{2,1,0:T(8,128)(2,1)S(1)} %collective-permute-done.fetched), channel_id=1, source_target_pairs={{0,8},{8,0},{16,24},{24,16},{32,40},{40,32},{48,56},{56,48},{64,72... | collective-permute-start | bytes 688136 | tf_op jit(solution)/shard_map/ppermute | solution.py:366
  21.1 1.5 %collective-permute-done.1.swapped = bf16[14,32,256]{2,1,0:T(8,128)(2,1)S(1)} collective-permute-done((bf16[14,32,256]{2,1,0:T(8,128)(2,1)S(1)}, bf16[14,32,256]{2,1,0:T(8,128)(2,1)S(1)}, u32[]{:S(2)}, u32[]{:S(2)}) %collective-permute-start.1) | collective-permute-done | bytes 229408 | tf_op jit(solution)/shard_map/ppermute | solution.py:366
  22.5 3.7 %all-to-all-done.planes.v_ref = bf16[8,5,4,32,128]{4,3,2,1,0:T(8,128)(2,1)S(1)} async-done(((bf16[8,5,4,32,128]{4,3,2,1,0:T(8,128)(2,1)}), bf16[8,5,4,32,128]{4,3,2,1,0:T(8,128)(2,1)S(1)}, u32[]{:S(2)}, u32[]{:S(2)}) %all-to-all-start) | async-done | bytes 1310752 | tf_op jit(solution)/shard_map/all_to_all | solution.py:374
  26.2 0.6 first_edge_kernel.1
  26.8 4.8 %collective-permute-start.3 = (f32[2,4,32,128]{3,2,1,0:T(8,128)S(1)}, f32[2,4,32,128]{3,2,1,0:T(8,128)S(1)}, u32[]{:S(2)}, u32[]{:S(2)}) collective-permute-start(f32[2,4,32,128]{3,2,1,0:T(8,128)S(1)} %get-tuple-element.17), channel_id=1, source_target_pairs={{8,4},{9,5},{10,6},{11,7},{16,12},{17,13},{18,14},{19,15},{24,20},... | collective-permute-start | bytes 393224 | tf_op jit(solution)/shard_map/ppermute | solution.py:383
  31.6 0.0 collective-permute-done.2.parcel.other.w_ref
  31.7 3.5 %first_kernel.1 = (bf16[4,2,4,4,32,128]{5,4,3,2,1,0:T(8,128)(2,1)S(1)}, f32[2,2,4,32,128]{4,3,2,1,0:T(8,128)S(1)}, f32[32,128]{1,0:T(8,128)S(1)}) custom-call(bf16[8,5,4,32,128]{4,3,2,1,0:T(8,128)(2,1)S(1)} %all-to-all-done.planes.v_ref, bf16[3,3,3,32,256]{4,3,2,1,0:T(8,128)(2,1)S(1)} %copy-done.1, bf16[27,32,256]{2,1,0:T(8,128)(2,1)S(1)} %get-tuple-element.15.other, ...), custom_call_target="tpu_custom_call" | custom-call | tf_op jit(solution)/shard_map/first_kernel/pallas_call | solution.py:384
  35.2 1.2 %collective-permute-done.3.outer = f32[2,4,32,128]{3,2,1,0:T(8,128)S(1)} collective-permute-done((f32[2,4,32,128]{3,2,1,0:T(8,128)S(1)}, f32[2,4,32,128]{3,2,1,0:T(8,128)S(1)}, u32[]{:S(2)}, u32[]{:S(2)}) %collective-permute-start.3) | collective-permute-done | bytes 131104 | tf_op jit(solution)/shard_map/ppermute | solution.py:383
  36.4 0.5 first_ends_kernel.1
  36.9 14.5 %all_to_all.10.planes = bf16[4,2,4,4,32,128]{5,4,3,2,1,0:T(8,128)(2,1)S(1)} all-to-all(bf16[4,2,4,4,32,128]{5,4,3,2,1,0:T(8,128)(2,1)S(1)} %first_ends_kernel.1), channel_id=1, replica_groups={{0,1,2,3},{4,5,6,7},{8,9,10,11},{12,13,14,15},{16,17,18,19},{20,21,22,2..., dimensions={0} | all-to-all | bytes 2097152 | tf_op jit(solution)/shard_map/all_to_all | solution.py:401
  51.4 0.5 second_edge_kernel.1._
  52.0 7.1 %collective-permute-start.5 = (f32[2,4,32,128]{3,2,1,0:T(8,128)S(1)}, f32[2,4,32,128]{3,2,1,0:T(8,128)S(1)}, u32[]{:S(2)}, u32[]{:S(2)}) collective-permute-start(f32[2,4,32,128]{3,2,1,0:T(8,128)S(1)} %second_edge_kernel.1._), channel_id=1, source_target_pairs={{8,4},{9,5},{10,6},{11,7},{16,12},{17,13},{18,14},{19,15},{24,20},... | collective-permute-start | bytes 393224 | tf_op jit(solution)/shard_map/ppermute | solution.py:406
  59.1 1.3 %second_other_kernel.1 = (bf16[6,4,32,128]{3,2,1,0:T(8,128)(2,1)S(1)}, f32[2,4,32,128]{3,2,1,0:T(8,128)S(1)}) custom-call(bf16[4,2,4,4,32,128]{5,4,3,2,1,0:T(8,128)(2,1)S(1)} %all_to_all.10.planes, bf16[28,32,256]{2,1,0:T(8,128)(2,1)S(1)} %collective-permute-done.2.parcel.other.w_ref, f32[32,128]{1,0:T(8,128)S(1)} %get-tuple-element.21.bias, ...), custom_call_target="tpu_custom_call" | custom-call | tf_op jit(solution)/shard_map/second_other_kernel/pallas_call | solution.py:408
  60.4 1.9 %collective-permute-start.4 = (bf16[6,4,32,128]{3,2,1,0:T(8,128)(2,1)S(1)}, bf16[6,4,32,128]{3,2,1,0:T(8,128)(2,1)S(1)}, u32[]{:S(2)}, u32[]{:S(2)}) collective-permute-start(bf16[6,4,32,128]{3,2,1,0:T(8,128)(2,1)S(1)} %get-tuple-element.22), channel_id=1, source_target_pairs={{0,4},{1,5},{2,6},{3,7},{8,12},{9,13},{10,14},{11,15},{16,20},{17,... | collective-permute-start | bytes 589832 | tf_op jit(solution)/shard_map/ppermute | solution.py:411
  62.3 0.0 collective-permute-done.5.outer
  62.3 3.9 %collective-permute-start.6 = (bf16[4,32,128]{2,1,0:T(8,128)(2,1)S(1)}, bf16[4,32,128]{2,1,0:T(8,128)(2,1)S(1)}, u32[]{:S(2)}, u32[]{:S(2)}) collective-permute-start(bf16[4,32,128]{2,1,0:T(8,128)(2,1)S(1)} %finish_kernel.1), channel_id=1, source_target_pairs={{0,4},{1,5},{2,6},{3,7},{8,12},{9,13},{10,14},{11,15},{16,20},{17,... | collective-permute-start | bytes 98312 | tf_op jit(solution)/shard_map/ppermute | solution.py:413
  66.3 2.0 %second_own_kernel.1 = (bf16[32,8,4,128]{3,2,1,0:T(4,128)(2,1)}, f32[2,4,32,128]{3,2,1,0:T(8,128)S(1)}, f32[4,32,128]{2,1,0:T(8,128)S(1)}) custom-call(bf16[4,2,4,4,32,128]{5,4,3,2,1,0:T(8,128)(2,1)S(1)} %all_to_all.10.planes, bf16[3,3,3,32,256]{4,3,2,1,0:T(8,128)(2,1)S(1)} %copy-done, f32[1,32]{1,0:T(1,128)S(1)} %bitcast.25, ...), custom_call_target="tpu_custom_call" | custom-call | tf_op jit(solution)/shard_map/second_own_kernel/pallas_call | solution.py:414
  68.3 0.7 outer_end_kernel.1._
  69.0 0.0 collective-permute-done.6.last_plane
  69.0 1.0 %last_kernel.1 = bf16[32,8,4,128]{3,2,1,0:T(4,128)(2,1)} custom-call(f32[2,4,32,128]{3,2,1,0:T(8,128)S(1)} %get-tuple-element.19.ends, f32[4,32,128]{2,1,0:T(8,128)S(1)} %get-tuple-element.20.inner_own, bf16[6,4,32,128]{3,2,1,0:T(8,128)(2,1)S(1)} %collective-permute-done.4.received, ...), custom_call_target="tpu_custom_call", output_to_operand_aliasing={{}: (4, {})} | custom-call | tf_op jit(solution)/shard_map/last_kernel/pallas_call | solution.py:429
  (10 shorter events, 0.1 us)
Async XLA Ops:
  2.2 5.5 %copy-start.1 = (bf16[3,3,3,32,256]{4,3,2,1,0:T(8,128)(2,1)S(1)}, bf16[3,3,3,32,256]{4,3,2,1,0:T(8,128)(2,1)}, u32[]{:S(2)}) copy-start(bf16[3,3,3,32,256]{4,3,2,1,0:T(8,128)(2,1)} %own.4) | copy-start | bytes 1327108
  2.2 10.9 %copy-start.2 = (f32[32]{0:T(128)S(1)}, f32[32]{0:T(128)}, u32[]{:S(2)}) copy-start(f32[32]{0:T(128)} %param.7) | copy-start | bytes 388
  2.2 10.9 %copy-start.3 = (f32[32]{0:T(128)S(1)}, f32[32]{0:T(128)}, u32[]{:S(2)}) copy-start(f32[32]{0:T(128)} %param.9) | copy-start | bytes 388
  2.3 11.1 %copy-start = (bf16[3,3,3,32,256]{4,3,2,1,0:T(8,128)(2,1)S(1)}, bf16[3,3,3,32,256]{4,3,2,1,0:T(8,128)(2,1)}, u32[]{:S(2)}) copy-start(bf16[3,3,3,32,256]{4,3,2,1,0:T(8,128)(2,1)} %own.5) | copy-start | bytes 1327108
  2.3 24.0 %all-to-all-start = ((bf16[8,5,4,32,128]{4,3,2,1,0:T(8,128)(2,1)}), bf16[8,5,4,32,128]{4,3,2,1,0:T(8,128)(2,1)S(1)}, u32[]{:S(2)}, u32[]{:S(2)}) async-start(bf16[8,5,4,32,128]{4,3,2,1,0:T(8,128)(2,1)} %spread_kernel.1), calls=%async_computation | async-start | bytes 2621440 | tf_op jit(solution)/shard_map/all_to_all | solution.py:374
  7.8 11.4 %collective-permute-start = (bf16[14,32,256]{2,1,0:T(8,128)(2,1)S(1)}, bf16[14,32,256]{2,1,0:T(8,128)(2,1)S(1)}, u32[]{:S(2)}, u32[]{:S(2)}) collective-permute-start(bf16[14,32,256]{2,1,0:T(8,128)(2,1)S(1)} %constant_dynamic-slice_fusion), channel_id=1, source_target_pairs={{20,0},{21,1},{22,2},{23,3},{16,4},{17,5},{18,6},{19,7},{28,8},{29... | collective-permute-start | bytes 688136 | tf_op jit(solution)/shard_map/ppermute | solution.py:363
  14.1 17.5 %collective-permute-start.2 = (bf16[28,32,256]{2,1,0:T(8,128)(2,1)}, bf16[28,32,256]{2,1,0:T(8,128)(2,1)S(1)}, u32[]{:S(2)}, u32[]{:S(2)}) collective-permute-start(bf16[28,32,256]{2,1,0:T(8,128)(2,1)} %pad_maximum_fusion), channel_id=1, source_target_pairs={{20,0},{21,1},{22,2},{23,3},{16,4},{17,5},{18,6},{19,7},{28,8},{29... | collective-permute-start | bytes 1376264 | tf_op jit(solution)/shard_map/ppermute | solution.py:370
  19.2 3.4 %collective-permute-start.1 = (bf16[14,32,256]{2,1,0:T(8,128)(2,1)S(1)}, bf16[14,32,256]{2,1,0:T(8,128)(2,1)S(1)}, u32[]{:S(2)}, u32[]{:S(2)}) collective-permute-start(bf16[14,32,256]{2,1,0:T(8,128)(2,1)S(1)} %collective-permute-done.fetched), channel_id=1, source_target_pairs={{0,8},{8,0},{16,24},{24,16},{32,40},{40,32},{48,56},{56,48},{64,72... | collective-permute-start | bytes 688136 | tf_op jit(solution)/shard_map/ppermute | solution.py:366
  26.8 9.6 %collective-permute-start.3 = (f32[2,4,32,128]{3,2,1,0:T(8,128)S(1)}, f32[2,4,32,128]{3,2,1,0:T(8,128)S(1)}, u32[]{:S(2)}, u32[]{:S(2)}) collective-permute-start(f32[2,4,32,128]{3,2,1,0:T(8,128)S(1)} %get-tuple-element.17), channel_id=1, source_target_pairs={{8,4},{9,5},{10,6},{11,7},{16,12},{17,13},{18,14},{19,15},{24,20},... | collective-permute-start | bytes 393224 | tf_op jit(solution)/shard_map/ppermute | solution.py:383
  52.0 10.4 %collective-permute-start.5 = (f32[2,4,32,128]{3,2,1,0:T(8,128)S(1)}, f32[2,4,32,128]{3,2,1,0:T(8,128)S(1)}, u32[]{:S(2)}, u32[]{:S(2)}) collective-permute-start(f32[2,4,32,128]{3,2,1,0:T(8,128)S(1)} %second_edge_kernel.1._), channel_id=1, source_target_pairs={{8,4},{9,5},{10,6},{11,7},{16,12},{17,13},{18,14},{19,15},{24,20},... | collective-permute-start | bytes 393224 | tf_op jit(solution)/shard_map/ppermute | solution.py:406
  60.4 8.6 %collective-permute-start.4 = (bf16[6,4,32,128]{3,2,1,0:T(8,128)(2,1)S(1)}, bf16[6,4,32,128]{3,2,1,0:T(8,128)(2,1)S(1)}, u32[]{:S(2)}, u32[]{:S(2)}) collective-permute-start(bf16[6,4,32,128]{3,2,1,0:T(8,128)(2,1)S(1)} %get-tuple-element.22), channel_id=1, source_target_pairs={{0,4},{1,5},{2,6},{3,7},{8,12},{9,13},{10,14},{11,15},{16,20},{17,... | collective-permute-start | bytes 589832 | tf_op jit(solution)/shard_map/ppermute | solution.py:411
  62.3 6.6 %collective-permute-start.6 = (bf16[4,32,128]{2,1,0:T(8,128)(2,1)S(1)}, bf16[4,32,128]{2,1,0:T(8,128)(2,1)S(1)}, u32[]{:S(2)}, u32[]{:S(2)}) collective-permute-start(bf16[4,32,128]{2,1,0:T(8,128)(2,1)S(1)} %finish_kernel.1), channel_id=1, source_target_pairs={{0,4},{1,5},{2,6},{3,7},{8,12},{9,13},{10,14},{11,15},{16,20},{17,... | collective-permute-start | bytes 98312 | tf_op jit(solution)/shard_map/ppermute | solution.py:413

commit v8 on v7

--- a/solution.py
+++ b/solution.py
@@ -284,14 +284,14 @@
         (theirs + outer, lambda z: (got(2, z) + got(3, z)) + inner_own[z]),
     )
     copies = []
+    for i, (at, value) in enumerate(ends_at):
+        rest[i] = channels_first([value(z) for z in range(nz)])
+        copies.append(pltpu.make_async_copy(rest.at[i], out.at[:, at], sems.at[i]))
+        copies[-1].start()
     for y in range(ny - 2):
         whole[:, y] = channels_first([received[y, z].astype(F32) for z in range(nz)])
     copies.append(pltpu.make_async_copy(whole, out.at[:, pl.ds(theirs + 1, ny - 2)], sems.at[3]))
     copies[-1].start()
-    for i, (at, value) in enumerate(ends_at):
-        rest[i] = channels_first([value(z) for z in range(nz)])
-        copies.append(pltpu.make_async_copy(rest.at[i], out.at[:, at], sems.at[i]))
-        copies[-1].start()
     for c in copies:
         c.wait()
 

time: 70.3 us -> 70.4 us (level)
  no operation moved by 1% of the time
where the time goes in v8:
time: 70.4 us; the launch traced here: 70 us
  starting transfers between devices  32.4 us (46%)
  blocking collectives  14.5 us (21%)
  Pallas kernels  11.3 us (16%)
  waiting for transfers between devices  9.48 us (13%)
  local copies, waits for them, and re-layouts  1.25 us (2%)
  other arithmetic  0.84 us (1%)
    all_to_all x1, blocking collectives, per_device(): lax.all_to_all(hidden, 'ch', 0, 0, tiled=True, axis_index_groups=groups)  14.5 us
    ppermute x1, starting transfers between devices, per_device(): outer = lax.ppermute(edges, axes, to_across)  7.08 us
    all_to_all x1, starting transfers between devices, per_device(): main = lax.all_to_all(sent, 'ch', 0, 0, tiled=True)  5.46 us
    ppermute x1, starting transfers between devices, per_device(): lax.ppermute(lax.dynamic_slice_in_dim(weight, (taps - part) * core, part,...  5.36 us
    ppermute x1, starting transfers between devices, per_device(): outer = lax.ppermute(outer, axes, to_across)  4.83 us
    ppermute x1, starting transfers between devices, per_device(): last_plane = lax.ppermute(last_plane, axes, to_partner)  3.92 us
    all_to_all x1, waiting for transfers between devices, per_device(): main = lax.all_to_all(sent, 'ch', 0, 0, tiled=True)  3.7 us
    pallas_call x1, Pallas kernels, per_device(): call(first_kernel, (bf16(g, 2, ny), f32(2, 2), jax.ShapeDtypeStruct((co,...  3.54 us
  transfers between devices with their start and end apart: 8, of which 4 were waited for; matrix products, arithmetic and copies ran while one was open for 1% of the time, Pallas kernels for 12%

profile of v8, /device:TPU:384, one launch (start us, length us, event | category | flops | bytes accessed | tf_op | source)
XLA Modules:
  0.0 70.0 jit_solution(6893732525968323897)
XLA Ops:
  0.0 1.1 %copy.19 = bf16[32,8,4,128]{3,0,2,1:T(8,128)(2,1)S(1)} copy(bf16[32,8,4,128]{3,2,1,0:T(4,128)(2,1)} %param.5) | data formatting | bytes 524288 | tf_op args[0]
  1.1 1.2 %spread_kernel.1 = bf16[8,5,4,32,128]{4,3,2,1,0:T(8,128)(2,1)} custom-call(bf16[8,4,32,128]{3,2,1,0:T(8,128)(2,1)S(1)} %bitcast.23), custom_call_target="tpu_custom_call" | custom-call | tf_op jit(solution)/shard_map/spread_kernel/pallas_call | solution.py:373
  2.2 0.0 copy-start.1
  2.2 0.0 copy-start.2
  2.2 0.0 copy-start.3
  2.3 0.0 copy-start
  2.3 5.5 %all-to-all-start = ((bf16[8,5,4,32,128]{4,3,2,1,0:T(8,128)(2,1)}), bf16[8,5,4,32,128]{4,3,2,1,0:T(8,128)(2,1)S(1)}, u32[]{:S(2)}, u32[]{:S(2)}) async-start(bf16[8,5,4,32,128]{4,3,2,1,0:T(8,128)(2,1)} %spread_kernel.1), calls=%async_computation | async-start | bytes 2621440 | tf_op jit(solution)/shard_map/all_to_all | solution.py:374
  7.8 5.4 %collective-permute-start = (bf16[14,32,256]{2,1,0:T(8,128)(2,1)S(1)}, bf16[14,32,256]{2,1,0:T(8,128)(2,1)S(1)}, u32[]{:S(2)}, u32[]{:S(2)}) collective-permute-start(bf16[14,32,256]{2,1,0:T(8,128)(2,1)S(1)} %constant_dynamic-slice_fusion), channel_id=1, source_target_pairs={{20,0},{21,1},{22,2},{23,3},{16,4},{17,5},{18,6},{19,7},{28,8},{29... | collective-permute-start | bytes 688136 | tf_op jit(solution)/shard_map/ppermute | solution.py:363
  13.2 0.1 copy.17
  13.3 0.8 %pad_maximum_fusion = bf16[28,32,256]{2,1,0:T(8,128)(2,1)} fusion(bf16[1,32,256]{2,1,0:T(8,128)(2,1)S(1)} %pad_bitcast_fusion, bf16[27,32,256]{2,1,0:T(8,128)(2,1)S(1)} %bitcast.21), kind=kLoop, calls=%fused_computation | loop fusion | flops 229376 | bytes 917504 | tf_op jit(solution)/shard_map/concatenate | solution.py:369
  14.1 1.9 %collective-permute-start.2 = (bf16[28,32,256]{2,1,0:T(8,128)(2,1)}, bf16[28,32,256]{2,1,0:T(8,128)(2,1)S(1)}, u32[]{:S(2)}, u32[]{:S(2)}) collective-permute-start(bf16[28,32,256]{2,1,0:T(8,128)(2,1)} %pad_maximum_fusion), channel_id=1, source_target_pairs={{20,0},{21,1},{22,2},{23,3},{16,4},{17,5},{18,6},{19,7},{28,8},{29... | collective-permute-start | bytes 1376264 | tf_op jit(solution)/shard_map/ppermute | solution.py:370
  16.1 3.1 %collective-permute-done.fetched = bf16[14,32,256]{2,1,0:T(8,128)(2,1)S(1)} collective-permute-done((bf16[14,32,256]{2,1,0:T(8,128)(2,1)S(1)}, bf16[14,32,256]{2,1,0:T(8,128)(2,1)S(1)}, u32[]{:S(2)}, u32[]{:S(2)}) %collective-permute-start) | collective-permute-done | bytes 229408 | tf_op jit(solution)/shard_map/ppermute | solution.py:363
  19.2 1.9 %collective-permute-start.1 = (bf16[14,32,256]{2,1,0:T(8,128)(2,1)S(1)}, bf16[14,32,256]{2,1,0:T(8,128)(2,1)S(1)}, u32[]{:S(2)}, u32[]{:S(2)}) collective-permute-start(bf16[14,32,256]{2,1,0:T(8,128)(2,1)S(1)} %collective-permute-done.fetched), channel_id=1, source_target_pairs={{0,8},{8,0},{16,24},{24,16},{32,40},{40,32},{48,56},{56,48},{64,72... | collective-permute-start | bytes 688136 | tf_op jit(solution)/shard_map/ppermute | solution.py:366
  21.1 1.5 %collective-permute-done.1.swapped = bf16[14,32,256]{2,1,0:T(8,128)(2,1)S(1)} collective-permute-done((bf16[14,32,256]{2,1,0:T(8,128)(2,1)S(1)}, bf16[14,32,256]{2,1,0:T(8,128)(2,1)S(1)}, u32[]{:S(2)}, u32[]{:S(2)}) %collective-permute-start.1) | collective-permute-done | bytes 229408 | tf_op jit(solution)/shard_map/ppermute | solution.py:366
  22.5 3.7 %all-to-all-done.planes.v_ref = bf16[8,5,4,32,128]{4,3,2,1,0:T(8,128)(2,1)S(1)} async-done(((bf16[8,5,4,32,128]{4,3,2,1,0:T(8,128)(2,1)}), bf16[8,5,4,32,128]{4,3,2,1,0:T(8,128)(2,1)S(1)}, u32[]{:S(2)}, u32[]{:S(2)}) %all-to-all-start) | async-done | bytes 1310752 | tf_op jit(solution)/shard_map/all_to_all | solution.py:374
  26.2 0.6 first_edge_kernel.1
  26.8 4.8 %collective-permute-start.3 = (f32[2,4,32,128]{3,2,1,0:T(8,128)S(1)}, f32[2,4,32,128]{3,2,1,0:T(8,128)S(1)}, u32[]{:S(2)}, u32[]{:S(2)}) collective-permute-start(f32[2,4,32,128]{3,2,1,0:T(8,128)S(1)} %get-tuple-element.17), channel_id=1, source_target_pairs={{8,4},{9,5},{10,6},{11,7},{16,12},{17,13},{18,14},{19,15},{24,20},... | collective-permute-start | bytes 393224 | tf_op jit(solution)/shard_map/ppermute | solution.py:383
  31.6 0.0 collective-permute-done.2.parcel.other.w_ref
  31.7 3.5 %first_kernel.1 = (bf16[4,2,4,4,32,128]{5,4,3,2,1,0:T(8,128)(2,1)S(1)}, f32[2,2,4,32,128]{4,3,2,1,0:T(8,128)S(1)}, f32[32,128]{1,0:T(8,128)S(1)}) custom-call(bf16[8,5,4,32,128]{4,3,2,1,0:T(8,128)(2,1)S(1)} %all-to-all-done.planes.v_ref, bf16[3,3,3,32,256]{4,3,2,1,0:T(8,128)(2,1)S(1)} %copy-done.1, bf16[27,32,256]{2,1,0:T(8,128)(2,1)S(1)} %get-tuple-element.15.other, ...), custom_call_target="tpu_custom_call" | custom-call | tf_op jit(solution)/shard_map/first_kernel/pallas_call | solution.py:384
  35.2 1.2 %collective-permute-done.3.outer = f32[2,4,32,128]{3,2,1,0:T(8,128)S(1)} collective-permute-done((f32[2,4,32,128]{3,2,1,0:T(8,128)S(1)}, f32[2,4,32,128]{3,2,1,0:T(8,128)S(1)}, u32[]{:S(2)}, u32[]{:S(2)}) %collective-permute-start.3) | collective-permute-done | bytes 131104 | tf_op jit(solution)/shard_map/ppermute | solution.py:383
  36.4 0.5 first_ends_kernel.1
  36.9 14.5 %all_to_all.10.planes = bf16[4,2,4,4,32,128]{5,4,3,2,1,0:T(8,128)(2,1)S(1)} all-to-all(bf16[4,2,4,4,32,128]{5,4,3,2,1,0:T(8,128)(2,1)S(1)} %first_ends_kernel.1), channel_id=1, replica_groups={{0,1,2,3},{4,5,6,7},{8,9,10,11},{12,13,14,15},{16,17,18,19},{20,21,22,2..., dimensions={0} | all-to-all | bytes 2097152 | tf_op jit(solution)/shard_map/all_to_all | solution.py:401
  51.4 0.5 second_edge_kernel.1._
  52.0 7.1 %collective-permute-start.5 = (f32[2,4,32,128]{3,2,1,0:T(8,128)S(1)}, f32[2,4,32,128]{3,2,1,0:T(8,128)S(1)}, u32[]{:S(2)}, u32[]{:S(2)}) collective-permute-start(f32[2,4,32,128]{3,2,1,0:T(8,128)S(1)} %second_edge_kernel.1._), channel_id=1, source_target_pairs={{8,4},{9,5},{10,6},{11,7},{16,12},{17,13},{18,14},{19,15},{24,20},... | collective-permute-start | bytes 393224 | tf_op jit(solution)/shard_map/ppermute | solution.py:406
  59.1 1.3 %second_other_kernel.1 = (bf16[6,4,32,128]{3,2,1,0:T(8,128)(2,1)S(1)}, f32[2,4,32,128]{3,2,1,0:T(8,128)S(1)}) custom-call(bf16[4,2,4,4,32,128]{5,4,3,2,1,0:T(8,128)(2,1)S(1)} %all_to_all.10.planes, bf16[28,32,256]{2,1,0:T(8,128)(2,1)S(1)} %collective-permute-done.2.parcel.other.w_ref, f32[32,128]{1,0:T(8,128)S(1)} %get-tuple-element.21.bias, ...), custom_call_target="tpu_custom_call" | custom-call | tf_op jit(solution)/shard_map/second_other_kernel/pallas_call | solution.py:408
  60.4 1.9 %collective-permute-start.4 = (bf16[6,4,32,128]{3,2,1,0:T(8,128)(2,1)S(1)}, bf16[6,4,32,128]{3,2,1,0:T(8,128)(2,1)S(1)}, u32[]{:S(2)}, u32[]{:S(2)}) collective-permute-start(bf16[6,4,32,128]{3,2,1,0:T(8,128)(2,1)S(1)} %get-tuple-element.22), channel_id=1, source_target_pairs={{0,4},{1,5},{2,6},{3,7},{8,12},{9,13},{10,14},{11,15},{16,20},{17,... | collective-permute-start | bytes 589832 | tf_op jit(solution)/shard_map/ppermute | solution.py:411
  62.3 0.0 collective-permute-done.5.outer
  62.3 3.9 %collective-permute-start.6 = (bf16[4,32,128]{2,1,0:T(8,128)(2,1)S(1)}, bf16[4,32,128]{2,1,0:T(8,128)(2,1)S(1)}, u32[]{:S(2)}, u32[]{:S(2)}) collective-permute-start(bf16[4,32,128]{2,1,0:T(8,128)(2,1)S(1)} %finish_kernel.1), channel_id=1, source_target_pairs={{0,4},{1,5},{2,6},{3,7},{8,12},{9,13},{10,14},{11,15},{16,20},{17,... | collective-permute-start | bytes 98312 | tf_op jit(solution)/shard_map/ppermute | solution.py:413
  66.3 2.0 %second_own_kernel.1 = (bf16[32,8,4,128]{3,2,1,0:T(4,128)(2,1)}, f32[2,4,32,128]{3,2,1,0:T(8,128)S(1)}, f32[4,32,128]{2,1,0:T(8,128)S(1)}) custom-call(bf16[4,2,4,4,32,128]{5,4,3,2,1,0:T(8,128)(2,1)S(1)} %all_to_all.10.planes, bf16[3,3,3,32,256]{4,3,2,1,0:T(8,128)(2,1)S(1)} %copy-done, f32[1,32]{1,0:T(1,128)S(1)} %bitcast.25, ...), custom_call_target="tpu_custom_call" | custom-call | tf_op jit(solution)/shard_map/second_own_kernel/pallas_call | solution.py:414
  68.3 0.7 outer_end_kernel.1._
  69.0 0.0 collective-permute-done.6.last_plane
  69.0 1.0 %last_kernel.1 = bf16[32,8,4,128]{3,2,1,0:T(4,128)(2,1)} custom-call(f32[2,4,32,128]{3,2,1,0:T(8,128)S(1)} %get-tuple-element.19.ends, f32[4,32,128]{2,1,0:T(8,128)S(1)} %get-tuple-element.20.inner_own, bf16[6,4,32,128]{3,2,1,0:T(8,128)(2,1)S(1)} %collective-permute-done.4.received, ...), custom_call_target="tpu_custom_call", output_to_operand_aliasing={{}: (4, {})} | custom-call | tf_op jit(solution)/shard_map/last_kernel/pallas_call | solution.py:429
  (10 shorter events, 0.1 us)
Async XLA Ops:
  2.2 5.5 %copy-start.1 = (bf16[3,3,3,32,256]{4,3,2,1,0:T(8,128)(2,1)S(1)}, bf16[3,3,3,32,256]{4,3,2,1,0:T(8,128)(2,1)}, u32[]{:S(2)}) copy-start(bf16[3,3,3,32,256]{4,3,2,1,0:T(8,128)(2,1)} %own.4) | copy-start | bytes 1327108
  2.2 10.9 %copy-start.2 = (f32[32]{0:T(128)S(1)}, f32[32]{0:T(128)}, u32[]{:S(2)}) copy-start(f32[32]{0:T(128)} %param.7) | copy-start | bytes 388
  2.2 10.9 %copy-start.3 = (f32[32]{0:T(128)S(1)}, f32[32]{0:T(128)}, u32[]{:S(2)}) copy-start(f32[32]{0:T(128)} %param.9) | copy-start | bytes 388
  2.3 11.1 %copy-start = (bf16[3,3,3,32,256]{4,3,2,1,0:T(8,128)(2,1)S(1)}, bf16[3,3,3,32,256]{4,3,2,1,0:T(8,128)(2,1)}, u32[]{:S(2)}) copy-start(bf16[3,3,3,32,256]{4,3,2,1,0:T(8,128)(2,1)} %own.5) | copy-start | bytes 1327108
  2.3 24.0 %all-to-all-start = ((bf16[8,5,4,32,128]{4,3,2,1,0:T(8,128)(2,1)}), bf16[8,5,4,32,128]{4,3,2,1,0:T(8,128)(2,1)S(1)}, u32[]{:S(2)}, u32[]{:S(2)}) async-start(bf16[8,5,4,32,128]{4,3,2,1,0:T(8,128)(2,1)} %spread_kernel.1), calls=%async_computation | async-start | bytes 2621440 | tf_op jit(solution)/shard_map/all_to_all | solution.py:374
  7.8 11.4 %collective-permute-start = (bf16[14,32,256]{2,1,0:T(8,128)(2,1)S(1)}, bf16[14,32,256]{2,1,0:T(8,128)(2,1)S(1)}, u32[]{:S(2)}, u32[]{:S(2)}) collective-permute-start(bf16[14,32,256]{2,1,0:T(8,128)(2,1)S(1)} %constant_dynamic-slice_fusion), channel_id=1, source_target_pairs={{20,0},{21,1},{22,2},{23,3},{16,4},{17,5},{18,6},{19,7},{28,8},{29... | collective-permute-start | bytes 688136 | tf_op jit(solution)/shard_map/ppermute | solution.py:363
  14.1 17.5 %collective-permute-start.2 = (bf16[28,32,256]{2,1,0:T(8,128)(2,1)}, bf16[28,32,256]{2,1,0:T(8,128)(2,1)S(1)}, u32[]{:S(2)}, u32[]{:S(2)}) collective-permute-start(bf16[28,32,256]{2,1,0:T(8,128)(2,1)} %pad_maximum_fusion), channel_id=1, source_target_pairs={{20,0},{21,1},{22,2},{23,3},{16,4},{17,5},{18,6},{19,7},{28,8},{29... | collective-permute-start | bytes 1376264 | tf_op jit(solution)/shard_map/ppermute | solution.py:370
  19.2 3.4 %collective-permute-start.1 = (bf16[14,32,256]{2,1,0:T(8,128)(2,1)S(1)}, bf16[14,32,256]{2,1,0:T(8,128)(2,1)S(1)}, u32[]{:S(2)}, u32[]{:S(2)}) collective-permute-start(bf16[14,32,256]{2,1,0:T(8,128)(2,1)S(1)} %collective-permute-done.fetched), channel_id=1, source_target_pairs={{0,8},{8,0},{16,24},{24,16},{32,40},{40,32},{48,56},{56,48},{64,72... | collective-permute-start | bytes 688136 | tf_op jit(solution)/shard_map/ppermute | solution.py:366
  26.8 9.6 %collective-permute-start.3 = (f32[2,4,32,128]{3,2,1,0:T(8,128)S(1)}, f32[2,4,32,128]{3,2,1,0:T(8,128)S(1)}, u32[]{:S(2)}, u32[]{:S(2)}) collective-permute-start(f32[2,4,32,128]{3,2,1,0:T(8,128)S(1)} %get-tuple-element.17), channel_id=1, source_target_pairs={{8,4},{9,5},{10,6},{11,7},{16,12},{17,13},{18,14},{19,15},{24,20},... | collective-permute-start | bytes 393224 | tf_op jit(solution)/shard_map/ppermute | solution.py:383
  52.0 10.4 %collective-permute-start.5 = (f32[2,4,32,128]{3,2,1,0:T(8,128)S(1)}, f32[2,4,32,128]{3,2,1,0:T(8,128)S(1)}, u32[]{:S(2)}, u32[]{:S(2)}) collective-permute-start(f32[2,4,32,128]{3,2,1,0:T(8,128)S(1)} %second_edge_kernel.1._), channel_id=1, source_target_pairs={{8,4},{9,5},{10,6},{11,7},{16,12},{17,13},{18,14},{19,15},{24,20},... | collective-permute-start | bytes 393224 | tf_op jit(solution)/shard_map/ppermute | solution.py:406
  60.4 8.6 %collective-permute-start.4 = (bf16[6,4,32,128]{3,2,1,0:T(8,128)(2,1)S(1)}, bf16[6,4,32,128]{3,2,1,0:T(8,128)(2,1)S(1)}, u32[]{:S(2)}, u32[]{:S(2)}) collective-permute-start(bf16[6,4,32,128]{3,2,1,0:T(8,128)(2,1)S(1)} %get-tuple-element.22), channel_id=1, source_target_pairs={{0,4},{1,5},{2,6},{3,7},{8,12},{9,13},{10,14},{11,15},{16,20},{17,... | collective-permute-start | bytes 589832 | tf_op jit(solution)/shard_map/ppermute | solution.py:411
  62.3 6.6 %collective-permute-start.6 = (bf16[4,32,128]{2,1,0:T(8,128)(2,1)S(1)}, bf16[4,32,128]{2,1,0:T(8,128)(2,1)S(1)}, u32[]{:S(2)}, u32[]{:S(2)}) collective-permute-start(bf16[4,32,128]{2,1,0:T(8,128)(2,1)S(1)} %finish_kernel.1), channel_id=1, source_target_pairs={{0,4},{1,5},{2,6},{3,7},{8,12},{9,13},{10,14},{11,15},{16,20},{17,... | collective-permute-start | bytes 98312 | tf_op jit(solution)/shard_map/ppermute | solution.py:413
